TPU v7x, 32 devices: a whole 2x2x4 slice. The times are simulated.
32 devices in a mesh: dp: 8 (over z, y), tensor: 4 (over x, core).
Axes of the slice: x: 2, y: 2, z: 4, core: 2. Of those that a mesh axis runs over, the one named last changes fastest.
Arguments:
- hidden_in: bfloat16 [8192, 1024], P(('dp', 'tensor')), may hold values from -6 to 6
- attn_gain: float32 [1024], replicated, may hold values from 0.1 to 1.9
- qkv_weight: bfloat16 [3, 1024, 1024], P(None, 'dp', 'tensor'), may hold values from -0.1875 to 0.1875
- out_weight: bfloat16 [1024, 1024], P('tensor', 'dp'), may hold values from -2 to 2
- mlp_gain: float32 [1024], replicated, may hold values from 0.1 to 1.9
- in_weight: bfloat16 [2, 1024, 2624], P(None, 'dp', 'tensor'), may hold values from -0.1875 to 0.1875
- down_weight: bfloat16 [2624, 1024], P('tensor', 'dp'), may hold values from -0.125 to 0.125
- cotangent: bfloat16 [8192, 1024], P(('dp', 'tensor')), may hold values from -6 to 6
Outputs:
- layer_out: bfloat16 [8192, 1024], P(('dp', 'tensor'))
- input_grad: float32 [8192, 1024], P(('dp', 'tensor'))
- attn_gain_grad: float32 [1024], replicated
- qkv_weight_grad: float32 [3, 1024, 1024], P(None, 'dp', 'tensor')
- out_weight_grad: float32 [1024, 1024], P('tensor', 'dp')
- mlp_gain_grad: float32 [1024], replicated
- in_weight_grad: float32 [2, 1024, 2624], P(None, 'dp', 'tensor')
- down_weight_grad: float32 [2624, 1024], P('tensor', 'dp')
All inputs are finite; a program needn't handle non-finite values.
Results may differ from a plain program's by a relative error of at most 0.015.
Values may be sent and summed in bfloat16 or wider, within the bound.
No kernel may reach another device: no remote copies, remote signals or barrier semaphores. Data moves between devices by JAX's collectives and lax.ppermute only.
A program may use at most 128 MiB of HBM per device.

v0:
```python
import functools
import math

import jax
import jax.numpy as jnp
import numpy as np
from jax import lax
from jax.experimental import pallas as pl
from jax.experimental.pallas import tpu as pltpu
from jax.sharding import PartitionSpec as P

HD = 64
NORM_EPS = 1e-05
ROPE_BASE = 160000.0
BF = jnp.bfloat16
F32 = jnp.float32
LOG2E = math.log2(math.e)
COST = 1000
VMEM_MIB = 56

NN = (((1,), (0,)), ((), ()))
NT = (((1,), (1,)), ((), ()))
TN = (((0,), (0,)), ((), ()))


def mm(a, b, dims=NN):
    return lax.dot_general(a, b, dims, preferred_element_type=F32)


def vmem():
    return pl.BlockSpec(memory_space=pltpu.VMEM)


def smem():
    return pl.BlockSpec(memory_space=pltpu.SMEM)


def hbm():
    return pl.BlockSpec(memory_space=pltpu.HBM)


def call(body, ins, outs, scratch=(), name=None):
    return pl.pallas_call(
        body,
        out_shape=[jax.ShapeDtypeStruct(o[0], o[1]) for o in outs],
        in_specs=[i[1] for i in ins],
        out_specs=[o[2] for o in outs],
        scratch_shapes=list(scratch),
        compiler_params=pltpu.CompilerParams(vmem_limit_bytes=VMEM_MIB * 1024 * 1024),
        cost_estimate=pl.CostEstimate(flops=COST, transcendentals=0, bytes_accessed=COST),
        name=name,
    )(*[i[0] for i in ins])


def swap(value, axis, size, distance, label):
    with jax.named_scope(label):
        return lax.ppermute(value, axis, [(i, i ^ distance) for i in range(size)])


def gate(values, others):
    return list(lax.optimization_barrier((tuple(values), tuple(others)))[0])


def start(source, target, sem):
    copy = pltpu.make_async_copy(source, target, sem)
    copy.start()
    return copy


def start_pieces(pieces, offs, size, target, sem, axis):
    copies = []
    for i, piece in enumerate(pieces):
        where = pl.ds(pl.multiple_of(offs[i] * size, size), size)
        copies.append(start(piece, target.at[(slice(None),) * axis + (where,)], sem.at[i]))
    return copies


def wait(copies):
    for c in copies:
        c.wait()


def angles_at(table, block, rows):
    both = table[pl.ds(pl.multiple_of(block * rows, rows), rows), :]
    other = pltpu.roll(both, 64, 1)
    lane = lax.broadcasted_iota(jnp.int32, both.shape, 1)
    cos = jnp.where(lane < 64, both, other)
    sin = jnp.where(lane < 64, other, both)
    return cos, jnp.where((lane & 63) < 32, -sin, sin)


def turn(u, cos, sin):
    lane = lax.broadcasted_iota(jnp.int32, u.shape, 1)
    low = (lane & 63) < 32
    turned = jnp.where(low, pltpu.roll(u, 96, 1), pltpu.roll(u, 32, 1))
    return u * cos + turned * sin


def head_mask(shape, head):
    lane = lax.broadcasted_iota(jnp.int32, shape, 1)
    return (lane >> 6) == head


def attend_forward(n_pieces, piece_rows, scale, refs):
    offs, mine = refs[:2]
    norms, table = refs[2:6], refs[6]
    pieces = refs[7 : 7 + n_pieces]
    refs = refs[7 + n_pieces :]
    parts, (mixed_out, q_out, k_out, v_out, lse_ref) = refs[0:4], refs[4:9]
    n, tab, w, q, k, v, mixed, sem_w, sem = refs[9:]
    rows, width = n.shape[1], w.shape[2]
    loads = start_pieces(pieces, offs, piece_rows, w, sem_w, 1)
    norm_loads = [start(norms[i], n.at[i], sem.at[i]) for i in range(4)]
    table_load = start(table, tab, sem.at[4])
    wait(loads)
    table_load.wait()
    for i in range(4):
        at = pl.ds(i * rows, rows)
        cos, sin = angles_at(tab, mine[0] ^ i, rows)
        norm_loads[i].wait()
        for j, ref in ((0, q), (1, k)):
            u = mm(n[i], w[j])
            for g in range(width // 128):
                col = slice(g * 128, g * 128 + 128)
                ref[at, col] = turn(u[:, col], cos, sin).astype(BF)
        v[at, :] = mm(n[i], w[2]).astype(BF)
    stores = [start(x, y, sem.at[5 + i]) for i, (x, y) in enumerate(((q, q_out), (k, k_out), (v, v_out)))]
    factor = scale * LOG2E
    heads = width // HD
    group = 2 * rows
    for half in range(2):
        at = pl.ds(half * group, group)
        masks = [head_mask((group, width), h) for h in range(heads)]

        def scores(h):
            return mm(jnp.where(masks[h], q[at, :], jnp.zeros((), BF)), k[...], NT)

        acc = jnp.zeros((group, width), F32)
        s = scores(0)
        for h in range(heads):
            ahead = scores(h + 1) if h + 1 < heads else None
            top = jnp.max(s, axis=1, keepdims=True)
            e = jnp.exp2((s - top) * factor)
            total = jnp.sum(e, axis=1, keepdims=True)
            o = mm(e.astype(BF), v[...]) * (1.0 / total)
            lse2 = top * factor + jnp.log2(total)
            row = jnp.transpose(jnp.broadcast_to(lse2, (group, 128)))
            lse_ref[pl.ds(h, 1), at] = row[0:1, :]
            acc = jnp.where(masks[h], o, acc)
            s = ahead
        low = acc.astype(BF)
        mixed[at, :] = low
        part = mm(low, w[3], NT).astype(BF)
        parts[2 * half][...] = part[:rows]
        parts[2 * half + 1][...] = part[rows:]
    stores.append(start(mixed, mixed_out, sem.at[8]))
    wait(stores)


def norm_stats(v):
    mean = jnp.mean(v, axis=-1, keepdims=True)
    centred = v - mean
    spread = jnp.mean(centred * centred, axis=-1, keepdims=True)
    r = lax.rsqrt(spread + NORM_EPS)
    return centred * r, r


def norm_body(h_ref, gain_ref, o_ref):
    xhat, _ = norm_stats(h_ref[...].astype(F32))
    o_ref[...] = (xhat * gain_ref[...]).astype(BF)


def pack_body(qkv, out, inner, down, first, second):
    first[0:3] = qkv[...]
    first[3] = out[...].T
    second[0:2] = inner[...]
    second[2] = down[...]


def middle_rows(h_ref, gain, a, b, c, mid_ref, norm_ref):
    total = h_ref[...].astype(F32) + (a[...].astype(F32) + b[...].astype(F32) + c[...].astype(F32))
    mid_ref[...] = total
    xhat, _ = norm_stats(total)
    norm_ref[...] = (xhat * gain[...]).astype(BF)


INV_SQRT2 = 1.0 / math.sqrt(2.0)
INV_SQRT2PI = 1.0 / math.sqrt(2.0 * math.pi)


def feed_rows(n, c, w, grads, outs, hid, gug):
    rows = n.shape[1]
    products = [(mm(n[i], w[0], NT), mm(n[i], w[1], NT), mm(c[i], w[2], NT)) for i in range(2)]
    for i, (gate, up, back) in enumerate(products):
        at = pl.ds(i * rows, rows)
        cdf = 0.5 * (1.0 + lax.erf(gate * INV_SQRT2))
        pdf = jnp.exp(-0.5 * gate * gate) * INV_SQRT2PI
        act = gate * cdf
        hidden = (act * up).astype(BF)
        g0 = (back * up * (cdf + gate * pdf)).astype(BF)
        g1 = (back * act).astype(BF)
        grads[i][...] = (mm(g0, w[0]) + mm(g1, w[1])).astype(BF)
        outs[i][...] = mm(hidden, w[2]).astype(BF)
        hid[:, at] = hidden.T
        gug[0, :, at] = g0.T
        gug[1, :, at] = g1.T


def load_mlp(pieces, offs, size, w, sem):
    return [
        start_pieces([x.at[j] for x in pieces], offs, size, w.at[j], sem.at[j], 1) for j in range(3)
    ]


def feed_far(n_pieces, size, refs):
    offs, n_in, c_in, pieces = refs[0], refs[1:3], refs[3:5], refs[5 : 5 + n_pieces]
    grads, outs, (hid, gug), (n, c, w, sem_w, sem) = (
        refs[5 + n_pieces : 7 + n_pieces],
        refs[7 + n_pieces : 9 + n_pieces],
        refs[9 + n_pieces : 11 + n_pieces],
        refs[11 + n_pieces :],
    )
    loads = [start(n_in[i], n.at[i], sem.at[i]) for i in range(2)]
    loads += [start(c_in[i], c.at[i], sem.at[2 + i]) for i in range(2)]
    for group in load_mlp(pieces, offs, size, w, sem_w):
        wait(group)
    wait(loads)
    feed_rows(n, c, w, grads, outs, hid, gug)


def pick_columns(ref, first, second, size):
    a = ref[:, pl.ds(pl.multiple_of(first * size, size), size)]
    b = ref[:, pl.ds(pl.multiple_of(second * size, size), size)]
    return jnp.concatenate([a, b], axis=1)


def mlp_grads(cols, blocks, n, c, hidden, grads, outs):
    group = hidden[0].shape[1]
    for k, block in enumerate(blocks):
        first, second = cols[2 * block], cols[2 * block + 1]
        rights = [pick_columns(x, first, second, 128) for x in (n, c)]
        for j in range(3):
            left = hidden if j == 2 else [x.at[j] for x in grads]
            right = rights[1] if j == 2 else rights[0]
            total = mm(left[0][...], right[:group]) + mm(left[1][...], right[group:])
            outs[2 * k][j] = total[:, :128].astype(BF)
            outs[2 * k + 1][j] = total[:, 128:].astype(BF)


def start_rows(sources, target, sem, at):
    rows = sources[0].shape[0]
    return [start(x, target.at[pl.ds(i * rows, rows)], sem.at[at + i]) for i, x in enumerate(sources)]


class Halves:
    def __init__(self, ref, rows):
        self.ref, self.shape = ref, (2, rows, ref.shape[1])

    def __getitem__(self, i):
        return self.ref[pl.ds(i * self.shape[1], self.shape[1]), :]


def feed_near(n_pieces, size, refs):
    offs, cols, n_in, c_in, hid_far, gug_far = refs[0], refs[1], refs[2:6], refs[6:10], refs[10], refs[11]
    pieces = refs[12 : 12 + n_pieces]
    refs = refs[12 + n_pieces :]
    grads, outs, (hid, gug), blocks = refs[0:2], refs[2:4], refs[4:6], refs[6:10]
    n, c, hf, gf, w, sem_w, sem = refs[10:]
    loads = start_rows(n_in, n, sem, 0)[:2]
    groups = load_mlp(pieces, offs, size, w, sem_w)
    rows = n_in[0].shape[0]
    more = start_rows(c_in, c, sem, 4)
    late = [start(hid_far, hf, sem.at[8]), start(gug_far, gf, sem.at[9])]
    for group in groups:
        wait(group)
    wait(loads)
    wait(more)
    feed_rows(Halves(n, rows), Halves(c, rows), w, grads, outs, hid, gug)
    for i in (2, 3):
        pltpu.make_async_copy(n_in[i], n.at[pl.ds(i * rows, rows)], sem.at[i]).wait()
    wait(late)
    mlp_grads(cols, (0, 1), n, c, (hid, hf), (gug, gf), blocks)


def feed_late(refs):
    cols, n_in, c_in = refs[0], refs[1:5], refs[5:9]
    sources, blocks = refs[9:13], refs[13:17]
    n, c, hn, hf, gn, gf, sem = refs[17:]
    loads = start_rows(n_in, n, sem, 0)
    loads += [start(x, y, sem.at[8 + i]) for i, (x, y) in enumerate(zip(sources, (hn, hf, gn, gf)))]
    loads += start_rows(c_in, c, sem, 4)
    wait(loads)
    mlp_grads(cols, (2, 3), n, c, (hn, hf), (gn, gf), blocks)


def norm_back(v, g):
    xhat, r = norm_stats(v)
    mean_g = jnp.mean(g, axis=-1, keepdims=True)
    mean_gx = jnp.mean(g * xhat, axis=-1, keepdims=True)
    return r * (g - mean_g - xhat * mean_gx), xhat


def middle_back(mid, cot, gain, sa, sb, sc, mg_ref, low_ref, gain_ref):
    got = sa[...].astype(F32) + sb[...].astype(F32) + sc[...].astype(F32)
    back, xhat = norm_back(mid[...], gain[...] * got)
    sums = jnp.sum(got * xhat, axis=0, keepdims=True)
    for i in range(8):
        gain_ref[pl.ds(i, 1), :] = sums[:, 128 * i : 128 * i + 128]
    mg = cot[...].astype(F32) + back
    mg_ref[...] = mg
    low_ref[...] = mg.astype(BF)


def attend_backward(n_pieces, piece_rows, scale, refs):
    cols, mine, offs, gain, gain_two = refs[:5]
    refs = refs[5:]
    grads_in, mixed_in, q_in, k_in, v_in, lse_in, table, norms = (
        refs[0:4], refs[4], refs[5], refs[6], refs[7], refs[8], refs[9], refs[10:14]
    )
    pieces = refs[14 : 14 + n_pieces]
    refs = refs[14 + n_pieces :]
    outs, parts, gain_ref = refs[0:8], refs[8:12], refs[12]
    pg, do, o, q, k, v, lse, tab, n, a, dot_rows, dq, w, sem_w, sem = refs[13:]
    rows = grads_in[0].shape[0]
    length, width = q.shape
    heads = width // HD
    weights = start_pieces(pieces, offs, piece_rows, w, sem_w, 1)
    grads = start_rows(grads_in, a, sem, 0)
    pairs = ((mixed_in, o), (q_in, q), (k_in, k), (v_in, v), (lse_in, lse))
    near = [start(x, y, sem.at[4 + i]) for i, (x, y) in enumerate(pairs)]
    late = [start(table, tab, sem.at[12])]
    late += start_rows(norms, n, sem, 13)
    wait(weights)
    for i in range(4):
        grads[i].wait()
        at = pl.ds(i * rows, rows)
        do[at, :] = mm(a[at, :], w[3]).astype(BF)
    wait(near)
    lane = lax.broadcasted_iota(jnp.int32, (8, width), 1) >> 6
    head = lax.broadcasted_iota(jnp.int32, (8, width), 0)
    ones = jnp.where(lane == head, 1.0, 0.0).astype(BF)
    for i in range(4):
        at = pl.ds(i * rows, rows)
        t = do[at, :].astype(F32) * o[at, :].astype(F32)
        hi = t.astype(BF)
        lo = (t - hi.astype(F32)).astype(BF)
        dot_rows[:, at] = mm(ones, hi, NT) + mm(ones, lo, NT)
    dq[...] = jnp.zeros_like(dq)
    factor = scale * LOG2E
    nil = jnp.zeros((), BF)

    def one_block(i, carry):
        at = pl.ds(pl.multiple_of(i * rows, rows), rows)
        dk_acc = jnp.zeros((rows, width), F32)
        dv_acc = jnp.zeros((rows, width), F32)
        dq_acc = None
        for h in range(heads):
            mask = head_mask((length, width), h)
            qm = jnp.where(mask, q[...], nil)
            dom = jnp.where(mask, do[...], nil)
            km = jnp.where(head_mask((rows, width), h), k[at, :], nil)
            s = mm(k[at, :], qm, NT)
            dp = mm(v[at, :], dom, NT)
            p = jnp.exp2(s * factor - lse[pl.ds(h, 1), :])
            ds = (p * (dp - dot_rows[pl.ds(h, 1), :])).astype(BF)
            dv_acc = dv_acc + mm(p.astype(BF), dom)
            dk_acc = dk_acc + mm(ds, qm)
            part = mm(ds, km, TN)
            dq_acc = part if dq_acc is None else dq_acc + part
        dq[...] += dq_acc
        cos, sin = angles_at(tab, mine[0] ^ i, rows)
        for g in range(width // 128):
            col = slice(g * 128, g * 128 + 128)
            to = slice(width + g * 128, width + g * 128 + 128)
            pg[at, to] = turn(dk_acc[:, col] * scale, cos, -sin).astype(BF)
        pg[at, 2 * width :] = dv_acc.astype(BF)
        return carry

    wait(late[:1])
    lax.fori_loop(0, 4, one_block, 0)
    for i in range(4):
        at = pl.ds(i * rows, rows)
        cos, sin = angles_at(tab, mine[0] ^ i, rows)
        for g in range(width // 128):
            col = slice(g * 128, g * 128 + 128)
            pg[at, col] = turn(dq[at, col] * scale, cos, -sin).astype(BF)
    wait(late[1:])
    for block in range(4):
        first, second = cols[2 * block], cols[2 * block + 1]
        total = mm(pick_columns(n, first, second, 128), pg[...], TN)
        for j in range(3):
            part = total[:, j * width : (j + 1) * width].astype(BF)
            outs[2 * block][j] = part[:128]
            outs[2 * block + 1][j] = part[128:]
        part = mm(pick_columns(a, first, second, 128), o[...], TN).astype(BF)
        outs[2 * block][3] = part[:128]
        outs[2 * block + 1][3] = part[128:]
    sums = None
    for i in range(4):
        at = pl.ds(i * rows, rows)
        total = sum(mm(pg[at, j * width : (j + 1) * width], w[j], NT) for j in range(3))
        parts[i][pl.ds(0, rows), :] = total.astype(BF)
        part = jnp.sum(total * n[at, :].astype(F32), axis=0, keepdims=True)
        sums = part if sums is None else sums + part
    sums = sums / gain[...]
    both = [sums[:, 128 * i : 128 * i + 128] for i in range(8)] + [gain_two[...]]
    gain_ref[...] = write_gains(parts[3], rows, jnp.concatenate(both, axis=0))


def write_gains(ref, rows, gains):
    high = gains.astype(BF)
    low = (gains - high.astype(F32)).astype(BF)
    tail = pl.ds(rows, 16)
    ref[tail, :] = jnp.zeros((16, ref.shape[1]), BF)
    ref[tail, 0:128] = high
    ref[tail, 128:256] = low
    return high.astype(F32) + low.astype(F32)


def read_gains(ref, rows):
    tail = pl.ds(rows, 16)
    return ref[tail, 0:128].astype(F32) + ref[tail, 128:256].astype(F32)


def add_far(part, got, gains, o_ref, gains_ref):
    rows = part.shape[0]
    o_ref[pl.ds(0, rows), :] = (part[...].astype(F32) + got[pl.ds(0, rows), :].astype(F32)).astype(BF)
    gains_ref[...] = write_gains(o_ref, rows, gains[...] + read_gains(got, rows))


def input_back(h, mg, gain, sa, sb, sc, gains, o_ref, gains_ref):
    rows = sa.shape[0]
    gains_ref[...] = gains[...] + read_gains(sc, rows)
    got = sa[...].astype(F32) + sb[...].astype(F32) + sc[pl.ds(0, rows), :].astype(F32)
    back, _ = norm_back(h[...].astype(F32), gain[...] * got)
    o_ref[...] = mg[...] + back


def body(function, *static):
    return lambda *refs: function(*static, refs)


def angle_table(length):
    exponents = np.arange(0, HD, 2).astype(np.float32) / np.float32(HD)
    inverse = np.float32(ROPE_BASE) ** (-exponents)
    angles = np.arange(length).astype(np.float32)[:, None] * inverse[None, :]
    cos, sin = np.cos(angles), np.sin(angles)
    return np.concatenate([cos, cos, sin, sin], axis=1).astype(np.float32)


def shards(sizes, *args):
    hidden_in, attn_gain, qkv_weight, out_weight, mlp_gain, in_weight, down_weight, cotangent = args
    dp, tp = sizes
    rows, model = hidden_in.shape
    length = rows * tp
    piece_rows = qkv_weight.shape[1]
    width = qkv_weight.shape[2]
    units = in_weight.shape[2]
    scale = HD ** (-0.5)
    direct = dp == 8
    mine_one = lax.axis_index("tensor").astype(jnp.int32).reshape(1)
    place = lax.axis_index("dp")
    gain_one, gain_two = attn_gain.reshape(1, model), mlp_gain.reshape(1, model)

    def tensor(value, k, label):
        return swap(value, "tensor", tp, k, f"{label}_t{k}")

    def depth(value, k, label):
        return swap(value, "dp", dp, k, f"{label}_d{k}")

    def gather(shard, axis, label):
        if direct:
            far = depth(shard, 4, label)
            along = [shard, depth(shard, 2, label), far, depth(far, 2, label + "far")]
            across = [depth(v, 1, f"{label}{i}") for i, v in enumerate(along)]
            return [v for pair in zip(along, across) for v in pair]
        return [lax.all_gather(shard, "dp", axis=axis, tiled=True)]

    def only_direct(values):
        return values if direct else []

    if direct:
        offs = place ^ jnp.arange(8, dtype=jnp.int32)
        n_pieces, piece = 8, piece_rows
        z, y = place // 2, place % 2
        order = [1, 3, 2, 0]
        cols = jnp.stack([c for b in order for c in ((z ^ b) * 2 + (1 - y), (z ^ b) * 2 + y)])
    else:
        offs = jnp.zeros((1,), jnp.int32)
        n_pieces, piece = 1, model
        cols = jnp.arange(8, dtype=jnp.int32)
    cols = cols.astype(jnp.int32)
    sems = lambda *s: pltpu.SemaphoreType.DMA(s)
    add = lambda a, b: (a.astype(F32) + b.astype(F32)).astype(BF)

    def spread(own, label):
        far = tensor(own, 2, label)
        return [own, tensor(own, 1, label), far, tensor(far, 1, label + "far")]

    def exchange(blocks, label):
        return [blocks[0]] + [tensor(blocks[k], k, label) for k in (1, 2, 3)]

    def reduce(blocks, axis, label):
        whole = jnp.concatenate(blocks, axis=axis)
        return lax.psum_scatter(whole, "dp", scatter_dimension=axis, tiled=True).astype(F32)

    def sum_of(*values):
        return sum(v.astype(F32) for v in values)

    near = lambda *xs: [(x, vmem()) for x in xs]
    away = lambda xs: [(x, hbm()) for x in xs]
    scalar = lambda *xs: [(x, smem()) for x in xs]
    vm = lambda shape, dtype=BF: (shape, dtype, vmem())
    hb = lambda shape, dtype=BF: (shape, dtype, hbm())
    buf = lambda *shape, dtype=BF: pltpu.VMEM(shape, dtype)

    shard, mlp_shard = call(
        pack_body,
        near(qkv_weight, out_weight, in_weight.transpose(0, 2, 1), down_weight),
        [vm((4, piece_rows, width)), vm((3, units, piece_rows))],
        name="pack",
    )
    qkvo = gather(shard, 1, "qkvo")
    (normed,) = call(norm_body, near(hidden_in, gain_one), [vm((rows, model))], name="norm")
    if direct:
        (normed,) = gate([normed], [qkvo[1], qkvo[2], qkvo[4]])
    normed_attn = spread(normed, "norm")
    table = jnp.asarray(angle_table(length))
    if direct:
        (mlp_along,) = gate([mlp_shard], [qkvo[6]])
        (mlp_across,) = gate([mlp_shard], [qkvo[7]])
        z2, z1 = [depth(mlp_along, 2 * k, "mlp") for k in (2, 1)]
        (cotangent_there,) = gate([cotangent], [normed_attn[2]])
    else:
        cotangent_there = cotangent
    cot = spread(cotangent_there, "cot")
    if direct:
        before = []
    else:
        mlp, before = gather(mlp_shard, 2, "mlp"), []
    *parts, mixed, q, k, v, lse = call(
        body(attend_forward, n_pieces, piece, scale),
        scalar(offs, mine_one)
        + away(normed_attn)
        + away([table] + qkvo),
        [vm((rows, model))] * 4 + [hb((length, width))] * 4 + [vm((8, length), F32)],
        [buf(4, rows, model), buf(length, 128, dtype=F32), buf(4, model, width)]
        + [buf(length, width)] * 4
        + [sems(n_pieces), sems(9)],
        name="attend_forward",
    )
    if direct:
        y0 = depth(mlp_across, 1, "mlp0")
        *parts, lse = gate(parts + [lse], [z1, z2, y0])
    attn_far = add(parts[2], tensor(parts[3], 1, "afar"))
    attn_near = tensor(parts[1], 1, "anear")
    attn_got = tensor(attn_far, 2, "afar")
    if direct:
        z3 = depth(gate([z2], [lse])[0], 2, "mlpfar")
        y1, y2, y3 = [depth(gate([x], [lse])[0], 1, f"mlp{i}") for i, x in ((1, z1), (2, z2), (3, z3))]
        before = [y1, z3]
        mlp = [mlp_shard, y0, z1, y1, z2, y2, z3, y3]
    middle, normed_two = call(
        middle_rows,
        near(hidden_in, gain_two, *gate([parts[0]], before), attn_near, attn_got),
        [vm((rows, model), F32), vm((rows, model))],
        name="middle_rows",
    )

    normed_far = tensor(normed_two, 2, "norm2")
    (normed_relay,) = gate([normed_far], only_direct(mlp[5:]))
    normed_mlp = [normed_two, tensor(normed_two, 1, "norm2"), normed_far, tensor(normed_relay, 1, "norm2far")]
    far_back, far_send, far_out, far_out_send, far_hidden, far_grad = call(
        body(feed_far, n_pieces, piece),
        scalar(offs) + away(normed_mlp[2:] + cot[2:] + mlp),
        [vm((rows, model))] * 4 + [vm((units, 2 * rows)), vm((2, units, 2 * rows))],
        [buf(2, rows, model)] * 2 + [buf(3, units, model), sems(3, n_pieces), sems(4)],
        name="feed_far",
    )
    far_sum = add(far_back, tensor(far_send, 1, "far"))
    from_far = tensor(far_sum, 2, "far")
    near_back, near_send, near_out, near_out_send, near_hidden, near_grad, *grads = call(
        body(feed_near, n_pieces, piece),
        scalar(offs, cols)
        + away(gate(normed_mlp, [far_sum]) + cot + [far_hidden, far_grad] + mlp),
        [vm((rows, model))] * 4
        + [vm((units, 2 * rows)), vm((2, units, 2 * rows))]
        + [vm((3, units, 128))] * 4,
        [buf(length, model)] * 2
        + [buf(units, 2 * rows), buf(2, units, 2 * rows)]
        + [buf(3, units, model), sems(3, n_pieces), sems(10)],
        name="feed_near",
    )
    near_got = tensor(near_send, 1, "near")
    out_sum = add(far_out, tensor(far_out_send, 1, "lofar"))
    out_near = tensor(near_out_send, 1, "lonear")

    middle_grad, low_grad, gain_two_part = call(
        middle_back,
        near(middle, cotangent, gain_two, near_back, near_got, from_far),
        [vm((rows, model), F32), vm((rows, model)), vm((8, 128), F32)],
        name="middle_back",
    )
    attn_out_grad = spread(low_grad, "aog")
    grads += call(
        body(feed_late),
        scalar(cols)
        + away(gate(normed_mlp, [low_grad, out_sum, out_near]) + cot + [near_hidden, far_hidden, near_grad, far_grad]),
        [vm((3, units, 128))] * 4,
        [buf(length, model)] * 2
        + [buf(units, 2 * rows)] * 2
        + [buf(2, units, 2 * rows)] * 2
        + [sems(12)],
        name="feed_late",
    )
    early = [grads[7]]
    if direct:
        grads[0], grads[2] = gate([grads[0], grads[2]], [from_far])
        grads[4], grads[6] = gate([grads[4], grads[6]], [attn_out_grad[2]])
        got = [depth(grads[2 * i], 1, f"gmlp{i}") for i in range(4)]
        sums = [add(grads[2 * i + 1], got[i]) for i in range(2)]
        early.append(sums[0])
        back = [depth(sums[i], 2, f"gmlpz{i}") for i in range(2)]

    *attn, b0, b1, b2, b3, gains = call(
        body(attend_backward, n_pieces, piece, scale),
        scalar(cols, mine_one, offs)
        + near(gain_one, gain_two_part)
        + away(gate(attn_out_grad, early) + [mixed, q, k, v, lse, table] + normed_attn + qkvo),
        [vm((4, 128, width))] * 8
        + [vm((rows, model))] * 3
        + [vm((rows + 16, model)), vm((16, 128), F32)],
        [buf(length, 3 * width)]
        + [buf(length, width)] * 5
        + [buf(8, length, dtype=F32), buf(length, 128, dtype=F32), buf(length, model), buf(length, model)]
        + [buf(8, length, dtype=F32), buf(length, width, dtype=F32)]
        + [buf(4, model, width), sems(n_pieces), sems(17)],
        name="attend_backward",
    )
    if direct:
        late = sum_of(gate([grads[5]], [b0])[0], got[2], back[1]).astype(BF)
        last = depth(late, 4, "gmlp")
        *attn, b3 = gate(attn + [b3], [late, back[0], got[3]])
        gqkv = [depth(attn[2 * i], 1, f"gqkv{i}") for i in range(3)]
        qkv_sums = [add(attn[2 * i + 1], gqkv[i]) for i in range(2)]
        qkv_back = [depth(qkv_sums[i], 2, f"gqkvz{i}") for i in range(2)]
    sent_far, gains = call(
        add_far,
        near(b2, tensor(b3, 1, "nfar"), gains),
        [vm((rows + 16, model)), vm((16, 128), F32)],
        name="add_far",
    )
    got_far = tensor(sent_far, 2, "nfar")
    (b1,) = gate([b1], [sent_far])
    near_sum = tensor(b1, 1, "nnear")
    if direct:
        (b0,) = gate([b0], [last])
    input_grad, gains = call(
        input_back,
        near(hidden_in, middle_grad, gain_one, b0, near_sum, got_far, gains),
        [vm((rows, model), F32), vm((16, 128), F32)],
        name="input_back",
    )
    out_far = tensor(gate([out_sum], [got_far])[0], 2, "lofar")
    out_near = near_out.astype(F32) + out_near.astype(F32)
    layer_out = (middle + (out_near + out_far.astype(F32))).astype(BF)

    if direct:
        (attn[6],) = gate(attn[6:7], [input_grad])
        gains = gains + depth(gains, 1, "gain")
        gains = gains + depth(gains, 2, "gain")
        gains = gains + depth(gains, 4, "gain")
        gqkv.append(depth(attn[6], 1, "gqkv3"))
        qkv_late = sum_of(attn[5], gqkv[2], qkv_back[1]).astype(BF)
        qkv_last = depth(qkv_late, 4, "gqkv")
        attn_total = sum_of(attn[7], gqkv[3], qkv_back[0], gate([qkv_last], [out_far, gains])[0])
    else:
        gains = lax.psum(gains, "dp")
        attn_total = reduce(attn, 1, "gqkv")
    qkv_shard, out_shard = attn_total[0:3], attn_total[3].T
    gains = gains.reshape(2, model)

    if direct:
        mlp_total = sum_of(grads[7], got[3], back[0], gate([last], [input_grad])[0])
    else:
        mlp_total = reduce(grads, 2, "gmlp")
    in_shard, down_shard = mlp_total[0:2].transpose(0, 2, 1), mlp_total[2]

    return (layer_out, input_grad, gains[0], qkv_shard, out_shard, gains[1], in_shard, down_shard)


def solution(mesh):
    sizes = (mesh.shape["dp"], mesh.shape["tensor"])
    return jax.shard_map(
        functools.partial(shards, sizes),
        mesh=mesh,
        in_specs=(
            P(("dp", "tensor"), None),
            P(),
            P(None, "dp", "tensor"),
            P("tensor", "dp"),
            P(),
            P(None, "dp", "tensor"),
            P("tensor", "dp"),
            P(("dp", "tensor"), None),
        ),
        out_specs=(
            P(("dp", "tensor"), None),
            P(("dp", "tensor"), None),
            P(),
            P(None, "dp", "tensor"),
            P("tensor", "dp"),
            P(),
            P(None, "dp", "tensor"),
            P("tensor", "dp"),
        ),
        check_vma=False,
    )
```

profile of v0, /device:TPU:0, one launch (start us, length us, event | category | flops | bytes accessed | tf_op | source)
XLA Modules:
  0.0 270.3 jit_solution(242056736426470544)
XLA Ops:
  0.6 2.1 pack.1
  2.7 4.0 %collective-permute-start.2 = (bf16[4,128,256]{2,1,0:T(8,128)(2,1)}, bf16[4,128,256]{2,1,0:T(8,128)(2,1)S(1)}, u32[]{:S(2)}, u32[]{:S(2)}) collective-permute-start(bf16[4,128,256]{2,1,0:T(8,128)(2,1)} %get-tuple-element.107.refs_7_.refs_19_), channel_id=1, source_target_pairs={{0,16},{4,20},{8,24},{12,28},{16,0},{20,4},{24,8},{28,12},{1,17},{... | collective-permute-start | bytes 786440 | tf_op jit(solution)/shard_map/qkvo_d4/ppermute | solution.py:57
  9.8 2.2 norm.1.refs_2_.refs_15_
  12.0 6.9 %collective-permute-done.2.refs_11_.refs_23_ = bf16[4,128,256]{2,1,0:T(8,128)(2,1)S(1)} collective-permute-done((bf16[4,128,256]{2,1,0:T(8,128)(2,1)}, bf16[4,128,256]{2,1,0:T(8,128)(2,1)S(1)}, u32[]{:S(2)}, u32[]{:S(2)}) %collective-permute-start.2) | collective-permute-done | bytes 262176 | tf_op jit(solution)/shard_map/qkvo_d4/ppermute | solution.py:57
  22.2 5.3 %collective-permute-done.8.refs_13_.refs_25_ = bf16[4,128,256]{2,1,0:T(8,128)(2,1)S(1)} collective-permute-done((bf16[4,128,256]{2,1,0:T(8,128)(2,1)S(1)}, bf16[4,128,256]{2,1,0:T(8,128)(2,1)S(1)}, u32[]{:S(2)}, u32[]{:S(2)}) %collective-permute-start.8) | collective-permute-done | bytes 262176 | tf_op jit(solution)/shard_map/qkvofar_d2/ppermute | solution.py:57
  32.3 4.4 %collective-permute-done.9.refs_14_.refs_26_ = bf16[4,128,256]{2,1,0:T(8,128)(2,1)S(1)} collective-permute-done((bf16[4,128,256]{2,1,0:T(8,128)(2,1)S(1)}, bf16[4,128,256]{2,1,0:T(8,128)(2,1)S(1)}, u32[]{:S(2)}, u32[]{:S(2)}) %collective-permute-start.9) | collective-permute-done | bytes 262176 | tf_op jit(solution)/shard_map/qkvo3_d1/ppermute | solution.py:57
  36.7 3.3 %collective-permute-start.11 = (bf16[3,656,128]{2,1,0:T(8,128)(2,1)}, bf16[3,656,128]{2,1,0:T(8,128)(2,1)S(1)}, u32[]{:S(2)}, u32[]{:S(2)}) collective-permute-start(bf16[3,656,128]{2,1,0:T(8,128)(2,1)} %get-tuple-element.116.refs_5_.refs_12_), channel_id=1, source_target_pairs={{0,16},{4,20},{8,24},{12,28},{16,0},{20,4},{24,8},{28,12},{1,17},{... | collective-permute-start | bytes 1511432 | tf_op jit(solution)/shard_map/mlp_d4/ppermute | solution.py:57
  41.7 2.1 collective-permute-start.10
  48.0 14.2 %attend_forward.1 = (bf16[256,1024]{1,0:T(8,128)(2,1)}, bf16[256,1024]{1,0:T(8,128)(2,1)}, bf16[256,1024]{1,0:T(8,128)(2,1)}, bf16[256,1024]{1,0:T(8,128)(2,1)},...) custom-call(s32[8]{0:T(128)} %iota_xor_fusion.refs_0_.refs_2_, ...), custom_call_target="tpu_custom_call" | custom-call | flops 1000 | bytes 1000 | tf_op jit(solution)/shard_map/attend_forward/pallas_call | solution.py:43
  70.3 9.3 %collective-permute-done.13.refs_8_.refs_15_ = bf16[3,656,128]{2,1,0:T(8,128)(2,1)S(1)} collective-permute-done((bf16[3,656,128]{2,1,0:T(8,128)(2,1)S(1)}, bf16[3,656,128]{2,1,0:T(8,128)(2,1)S(1)}, u32[]{:S(2)}, u32[]{:S(2)}) %collective-permute-start.13) | collective-permute-done | bytes 503840 | tf_op jit(solution)/shard_map/mlp1_d1/ppermute | solution.py:57
  81.4 3.1 %middle_rows.1 = (f32[256,1024]{1,0:T(8,128)}, bf16[256,1024]{1,0:T(8,128)(2,1)}) custom-call(bf16[256,1024]{1,0:T(8,128)(2,1)} %h.1, f32[1,1024]{1,0:T(1,128)} %bitcast.28, bf16[256,1024]{1,0:T(8,128)(2,1)} %get-tuple-element.121.a, bf16[256,1024]{1,0:T(8,128)(2,1)} %copy-done.35, bf16[256,1024]{1,0:T(8,128)(2,1)} %copy-done.36), custom_call_target="tpu_custom_call" | custom-call | flops 1000 | bytes 1000 | tf_op jit(solution)/shard_map/middle_rows/pallas_call | solution.py:43
  87.7 4.1 %collective-permute-done.23.refs_3_.refs_8_.refs_7_ = bf16[256,1024]{1,0:T(8,128)(2,1)S(1)} collective-permute-done((bf16[256,1024]{1,0:T(8,128)(2,1)S(1)}, bf16[256,1024]{1,0:T(8,128)(2,1)S(1)}, u32[]{:S(2)}, u32[]{:S(2)}) %collective-permute-start.23) | collective-permute-done | bytes 524320 | tf_op jit(solution)/shard_map/cot_t2/ppermute | solution.py:57
  91.8 8.3 %collective-permute-done.20.refs_10_.refs_17_ = bf16[3,656,128]{2,1,0:T(8,128)(2,1)S(1)} collective-permute-done((bf16[3,656,128]{2,1,0:T(8,128)(2,1)S(1)}, bf16[3,656,128]{2,1,0:T(8,128)(2,1)S(1)}, u32[]{:S(2)}, u32[]{:S(2)}) %collective-permute-start.20) | collective-permute-done | bytes 503840 | tf_op jit(solution)/shard_map/mlp2_d1/ppermute | solution.py:57
  100.1 8.2 %collective-permute-done.21.refs_12_.refs_19_ = bf16[3,656,128]{2,1,0:T(8,128)(2,1)S(1)} collective-permute-done((bf16[3,656,128]{2,1,0:T(8,128)(2,1)S(1)}, bf16[3,656,128]{2,1,0:T(8,128)(2,1)S(1)}, u32[]{:S(2)}, u32[]{:S(2)}) %collective-permute-start.21) | collective-permute-done | bytes 503840 | tf_op jit(solution)/shard_map/mlp3_d1/ppermute | solution.py:57
  108.4 1.9 collective-permute-done.22.refs_2_.refs_5_.refs_4_
  111.2 10.5 %feed_far.1 = (bf16[256,1024]{1,0:T(8,128)(2,1)}, bf16[256,1024]{1,0:T(8,128)(2,1)}, bf16[256,1024]{1,0:T(8,128)(2,1)}, bf16[256,1024]{1,0:T(8,128)(2,1)}, bf16[...) custom-call(s32[8]{0:T(128)} %iota_xor_fusion.refs_0_.refs_2_, bf16[256,1024]{1,0:T(8,128)(2,1)} %copy-done.1, ...), custom_call_target="tpu_custom_call" | custom-call | flops 1000 | bytes 1000 | tf_op jit(solution)/shard_map/feed_far/pallas_call | solution.py:43
  126.8 13.4 %feed_near.1 = (bf16[256,1024]{1,0:T(8,128)(2,1)}, bf16[256,1024]{1,0:T(8,128)(2,1)}, bf16[256,1024]{1,0:T(8,128)(2,1)}, bf16[256,1024]{1,0:T(8,128)(2,1)}, bf16...) custom-call(s32[8]{0:T(128)} %iota_xor_fusion.refs_0_.refs_2_, ...), custom_call_target="tpu_custom_call" | custom-call | flops 1000 | bytes 1000 | tf_op jit(solution)/shard_map/feed_near/pallas_call | solution.py:43
  140.4 11.9 %collective-permute-start.28 = (bf16[256,1024]{1,0:T(8,128)(2,1)S(1)}, bf16[256,1024]{1,0:T(8,128)(2,1)S(1)}, u32[]{:S(2)}, u32[]{:S(2)}) collective-permute-start(bf16[256,1024]{1,0:T(8,128)(2,1)S(1)} %copy-done.48), channel_id=1, source_target_pairs={{0,1},{1,0},{2,3},{3,2},{4,5},{5,4},{6,7},{7,6},{8,9},{9,8},{10,11... | collective-permute-start | bytes 1572872 | tf_op jit(solution)/shard_map/lofar_t1/ppermute | solution.py:57
  153.6 4.0 %middle_back.1 = (f32[256,1024]{1,0:T(8,128)}, bf16[256,1024]{1,0:T(8,128)(2,1)}, f32[8,128]{1,0:T(8,128)}) custom-call(f32[256,1024]{1,0:T(8,128)} %get-tuple-element.125.mid, bf16[256,1024]{1,0:T(8,128)(2,1)} %refs_5_, f32[1,1024]{1,0:T(1,128)} %bitcast.29, bf16[256,1024]{1,0:T(8,128)(2,1)} %get-tuple-element.142.sa, bf16[256,1024]{1,0:T(8,128)(2,1)} %copy-done.37, ...), custom_call_target="tpu_custom_call" | custom-call | flops 1000 | bytes 1000 | tf_op jit(solution)/shard_map/middle_back/pallas_call | solution.py:43
  161.3 7.5 %feed_late.1 = (bf16[3,656,128]{2,1,0:T(8,128)(2,1)}, bf16[3,656,128]{2,1,0:T(8,128)(2,1)}, bf16[3,656,128]{2,1,0:T(8,128)(2,1)}, bf16[3,656,128]{2,1,0:T(8,128)(2,1)}) custom-call(s32[8]{0:T(128)} %stack.35.refs_1_.refs_0_, bf16[256,1024]{1,0:T(8,128)(2,1)} %get-tuple-element.146.refs_2_.refs_1_, bf16[256,1024]{1,0:T(8,128)(2,1)} %copy-done.10, ...), custom_call_target="tpu_custom_call" | custom-call | flops 1000 | bytes 1000 | tf_op jit(solution)/shard_map/feed_late/pallas_call | solution.py:43
  168.8 3.0 %collective-permute-done.32.refs_7_ = bf16[256,1024]{1,0:T(8,128)(2,1)S(1)} collective-permute-done((bf16[256,1024]{1,0:T(8,128)(2,1)}, bf16[256,1024]{1,0:T(8,128)(2,1)S(1)}, u32[]{:S(2)}, u32[]{:S(2)}) %collective-permute-start.32) | collective-permute-done | bytes 524320 | tf_op jit(solution)/shard_map/aog_t2/ppermute | solution.py:57
  173.5 1.8 collective-permute-start.37
  176.5 7.6 %collective-permute-done.34 = bf16[3,656,128]{2,1,0:T(8,128)(2,1)S(1)} collective-permute-done((bf16[3,656,128]{2,1,0:T(8,128)(2,1)S(1)}, bf16[3,656,128]{2,1,0:T(8,128)(2,1)S(1)}, u32[]{:S(2)}, u32[]{:S(2)}) %collective-permute-start.34) | collective-permute-done | bytes 503840 | tf_op jit(solution)/shard_map/gmlp0_d1/ppermute | solution.py:57
  188.2 24.9 %attend_backward.1 = (bf16[4,128,256]{2,1,0:T(8,128)(2,1)}, bf16[4,128,256]{2,1,0:T(8,128)(2,1)}, bf16[4,128,256]{2,1,0:T(8,128)(2,1)}, bf16[4,128,256]{2,1,0:T(...) custom-call(s32[8]{0:T(128)} %stack.35.refs_1_.refs_0_, ...), custom_call_target="tpu_custom_call" | custom-call | flops 1000 | bytes 1000 | tf_op jit(solution)/shard_map/attend_backward/pallas_call | solution.py:43
  216.3 4.1 %collective-permute-start.43 = (bf16[3,656,128]{2,1,0:T(8,128)(2,1)S(1)}, bf16[3,656,128]{2,1,0:T(8,128)(2,1)S(1)}, u32[]{:S(2)}, u32[]{:S(2)}) collective-permute-start(bf16[3,656,128]{2,1,0:T(8,128)(2,1)S(1)} %add_convert_fusion.4), channel_id=1, source_target_pairs={{0,16},{4,20},{8,24},{12,28},{16,0},{20,4},{24,8},{28,12},{1,17},{... | collective-permute-start | bytes 1511432 | tf_op jit(solution)/shard_map/gmlp_d4/ppermute | solution.py:57
  221.9 2.1 add_far.1
  224.8 4.1 %collective-permute-done.49 = bf16[4,128,256]{2,1,0:T(8,128)(2,1)S(1)} collective-permute-done((bf16[4,128,256]{2,1,0:T(8,128)(2,1)}, bf16[4,128,256]{2,1,0:T(8,128)(2,1)S(1)}, u32[]{:S(2)}, u32[]{:S(2)}) %collective-permute-start.49) | collective-permute-done | bytes 262176 | tf_op jit(solution)/shard_map/gqkv0_d1/ppermute | solution.py:57
  229.3 13.4 %collective-permute-done.43 = bf16[3,656,128]{2,1,0:T(8,128)(2,1)S(1)} collective-permute-done((bf16[3,656,128]{2,1,0:T(8,128)(2,1)S(1)}, bf16[3,656,128]{2,1,0:T(8,128)(2,1)S(1)}, u32[]{:S(2)}, u32[]{:S(2)}) %collective-permute-start.43) | collective-permute-done | bytes 503840 | tf_op jit(solution)/shard_map/gmlp_d4/ppermute | solution.py:57
  242.8 5.7 %collective-permute-done.53 = bf16[4,128,256]{2,1,0:T(8,128)(2,1)S(1)} collective-permute-done((bf16[4,128,256]{2,1,0:T(8,128)(2,1)S(1)}, bf16[4,128,256]{2,1,0:T(8,128)(2,1)S(1)}, u32[]{:S(2)}, u32[]{:S(2)}) %collective-permute-start.53) | collective-permute-done | bytes 262176 | tf_op jit(solution)/shard_map/gqkvz1_d2/ppermute | solution.py:57
  250.4 3.7 %input_back.1 = (f32[256,1024]{1,0:T(8,128)}, f32[16,128]{1,0:T(8,128)}) custom-call(bf16[256,1024]{1,0:T(8,128)(2,1)} %h.1, f32[256,1024]{1,0:T(8,128)} %get-tuple-element.188.mg, f32[1,1024]{1,0:T(1,128)} %bitcast.27, bf16[256,1024]{1,0:T(8,128)(2,1)} %get-tuple-element.189.sa, bf16[256,1024]{1,0:T(8,128)(2,1)} %copy-done.32, ...), custom_call_target="tpu_custom_call" | custom-call | flops 1000 | bytes 1000 | tf_op jit(solution)/shard_map/input_back/pallas_call | solution.py:43
  258.0 2.5 collective-permute-start.46
  264.5 2.2 collective-permute-done.47
  (224 shorter events, 67.1 us)
Async XLA Ops:
  2.7 16.3 %collective-permute-start.2 = (bf16[4,128,256]{2,1,0:T(8,128)(2,1)}, bf16[4,128,256]{2,1,0:T(8,128)(2,1)S(1)}, u32[]{:S(2)}, u32[]{:S(2)}) collective-permute-start(bf16[4,128,256]{2,1,0:T(8,128)(2,1)} %get-tuple-element.107.refs_7_.refs_19_), channel_id=1, source_target_pairs={{0,16},{4,20},{8,24},{12,28},{16,0},{20,4},{24,8},{28,12},{1,17},{... | collective-permute-start | bytes 786440 | tf_op jit(solution)/shard_map/qkvo_d4/ppermute | solution.py:57
  29.5 15.5 %collective-permute-start.6 = (bf16[4,128,256]{2,1,0:T(8,128)(2,1)S(1)}, bf16[4,128,256]{2,1,0:T(8,128)(2,1)S(1)}, u32[]{:S(2)}, u32[]{:S(2)}) collective-permute-start(bf16[4,128,256]{2,1,0:T(8,128)(2,1)S(1)} %collective-permute-done.1.refs_9_.refs_21_), channel_id=1, source_target_pairs={{0,4},{4,0},{8,12},{12,8},{16,20},{20,16},{24,28},{28,24},{1,5},{5... | collective-permute-start | bytes 786440 | tf_op jit(solution)/shard_map/qkvo1_d1/ppermute | solution.py:57
  31.0 16.0 %collective-permute-start.3 = (bf16[256,1024]{1,0:T(8,128)(2,1)}, bf16[256,1024]{1,0:T(8,128)(2,1)S(1)}, u32[]{:S(2)}, u32[]{:S(2)}) collective-permute-start(bf16[256,1024]{1,0:T(8,128)(2,1)} %norm.1.refs_2_.refs_15_), channel_id=1, source_target_pairs={{0,1},{1,0},{2,3},{3,2},{4,5},{5,4},{6,7},{7,6},{8,9},{9,8},{10,11... | collective-permute-start | bytes 1572872 | tf_op jit(solution)/shard_map/norm_t1/ppermute | solution.py:57
  32.3 14.7 %collective-permute-start.5 = (bf16[256,1024]{1,0:T(8,128)(2,1)S(1)}, bf16[256,1024]{1,0:T(8,128)(2,1)S(1)}, u32[]{:S(2)}, u32[]{:S(2)}) collective-permute-start(bf16[256,1024]{1,0:T(8,128)(2,1)S(1)} %collective-permute-done.4.refs_4_.refs_17_), channel_id=1, source_target_pairs={{0,1},{1,0},{2,3},{3,2},{4,5},{5,4},{6,7},{7,6},{8,9},{9,8},{10,11... | collective-permute-start | bytes 1572872 | tf_op jit(solution)/shard_map/normfar_t1/ppermute | solution.py:57
  36.7 25.5 %collective-permute-start.11 = (bf16[3,656,128]{2,1,0:T(8,128)(2,1)}, bf16[3,656,128]{2,1,0:T(8,128)(2,1)S(1)}, u32[]{:S(2)}, u32[]{:S(2)}) collective-permute-start(bf16[3,656,128]{2,1,0:T(8,128)(2,1)} %get-tuple-element.116.refs_5_.refs_12_), channel_id=1, source_target_pairs={{0,16},{4,20},{8,24},{12,28},{16,0},{20,4},{24,8},{28,12},{1,17},{... | collective-permute-start | bytes 1511432 | tf_op jit(solution)/shard_map/mlp_d4/ppermute | solution.py:57
  41.7 20.6 %collective-permute-start.10 = (bf16[3,656,128]{2,1,0:T(8,128)(2,1)}, bf16[3,656,128]{2,1,0:T(8,128)(2,1)S(1)}, u32[]{:S(2)}, u32[]{:S(2)}) collective-permute-start(bf16[3,656,128]{2,1,0:T(8,128)(2,1)} %get-tuple-element.116.refs_5_.refs_12_), channel_id=1, source_target_pairs={{0,8},{4,12},{8,0},{12,4},{16,24},{20,28},{24,16},{28,20},{1,9},{5... | collective-permute-start | bytes 1511432 | tf_op jit(solution)/shard_map/mlp_d2/ppermute | solution.py:57
  45.0 17.3 %collective-permute-start.12 = (bf16[3,656,128]{2,1,0:T(8,128)(2,1)}, bf16[3,656,128]{2,1,0:T(8,128)(2,1)}, u32[]{:S(2)}, u32[]{:S(2)}) collective-permute-start(bf16[3,656,128]{2,1,0:T(8,128)(2,1)} %get-tuple-element.116.refs_5_.refs_12_), channel_id=1, source_target_pairs={{0,4},{4,0},{8,12},{12,8},{16,20},{20,16},{24,28},{28,24},{1,5},{5... | collective-permute-start | bytes 1511432 | tf_op jit(solution)/shard_map/mlp0_d1/ppermute | solution.py:57
  62.4 17.7 %collective-permute-start.15 = (bf16[256,1024]{1,0:T(8,128)(2,1)}, bf16[256,1024]{1,0:T(8,128)(2,1)S(1)}, u32[]{:S(2)}, u32[]{:S(2)}) collective-permute-start(bf16[256,1024]{1,0:T(8,128)(2,1)} %get-tuple-element.122), channel_id=1, source_target_pairs={{0,1},{1,0},{2,3},{3,2},{4,5},{5,4},{6,7},{7,6},{8,9},{9,8},{10,11... | collective-permute-start | bytes 1572872 | tf_op jit(solution)/shard_map/anear_t1/ppermute | solution.py:57
  65.7 14.8 %collective-permute-start.17 = (bf16[256,1024]{1,0:T(8,128)(2,1)S(1)}, bf16[256,1024]{1,0:T(8,128)(2,1)S(1)}, u32[]{:S(2)}, u32[]{:S(2)}) collective-permute-start(bf16[256,1024]{1,0:T(8,128)(2,1)S(1)} %add_convert_fusion.3), channel_id=1, source_target_pairs={{0,2},{1,3},{2,0},{3,1},{4,6},{5,7},{6,4},{7,5},{8,10},{9,11},{10,... | collective-permute-start | bytes 1572872 | tf_op jit(solution)/shard_map/afar_t2/ppermute | solution.py:57
  68.8 23.0 %collective-permute-start.23 = (bf16[256,1024]{1,0:T(8,128)(2,1)S(1)}, bf16[256,1024]{1,0:T(8,128)(2,1)S(1)}, u32[]{:S(2)}, u32[]{:S(2)}) collective-permute-start(bf16[256,1024]{1,0:T(8,128)(2,1)S(1)} %copy-done.4), channel_id=1, source_target_pairs={{0,2},{1,3},{2,0},{3,1},{4,6},{5,7},{6,4},{7,5},{8,10},{9,11},{10,... | collective-permute-start | bytes 1572872 | tf_op jit(solution)/shard_map/cot_t2/ppermute | solution.py:57
  84.5 23.8 %collective-permute-start.19 = (bf16[256,1024]{1,0:T(8,128)(2,1)}, bf16[256,1024]{1,0:T(8,128)(2,1)S(1)}, u32[]{:S(2)}, u32[]{:S(2)}) collective-permute-start(bf16[256,1024]{1,0:T(8,128)(2,1)} %get-tuple-element.146.refs_2_.refs_1_), channel_id=1, source_target_pairs={{0,2},{1,3},{2,0},{3,1},{4,6},{5,7},{6,4},{7,5},{8,10},{9,11},{10,... | collective-permute-start | bytes 1572872 | tf_op jit(solution)/shard_map/norm2_t2/ppermute | solution.py:57
  85.7 14.4 %collective-permute-start.20 = (bf16[3,656,128]{2,1,0:T(8,128)(2,1)S(1)}, bf16[3,656,128]{2,1,0:T(8,128)(2,1)S(1)}, u32[]{:S(2)}, u32[]{:S(2)}) collective-permute-start(bf16[3,656,128]{2,1,0:T(8,128)(2,1)S(1)} %collective-permute-done.11.refs_9_.refs_16_), channel_id=1, source_target_pairs={{0,4},{4,0},{8,12},{12,8},{16,20},{20,16},{24,28},{28,24},{1,5},{5... | collective-permute-start | bytes 1511432 | tf_op jit(solution)/shard_map/mlp2_d1/ppermute | solution.py:57
  87.0 21.3 %collective-permute-start.21 = (bf16[3,656,128]{2,1,0:T(8,128)(2,1)S(1)}, bf16[3,656,128]{2,1,0:T(8,128)(2,1)S(1)}, u32[]{:S(2)}, u32[]{:S(2)}) collective-permute-start(bf16[3,656,128]{2,1,0:T(8,128)(2,1)S(1)} %collective-permute-done.14.refs_11_.refs_18_), channel_id=1, source_target_pairs={{0,4},{4,0},{8,12},{12,8},{16,20},{20,16},{24,28},{28,24},{1,5},{5... | collective-permute-start | bytes 1511432 | tf_op jit(solution)/shard_map/mlp3_d1/ppermute | solution.py:57
  91.8 16.6 %collective-permute-start.24 = (bf16[256,1024]{1,0:T(8,128)(2,1)S(1)}, bf16[256,1024]{1,0:T(8,128)(2,1)S(1)}, u32[]{:S(2)}, u32[]{:S(2)}) collective-permute-start(bf16[256,1024]{1,0:T(8,128)(2,1)S(1)} %collective-permute-done.23.refs_3_.refs_8_.refs_7_), channel_id=1, source_target_pairs={{0,1},{1,0},{2,3},{3,2},{4,5},{5,4},{6,7},{7,6},{8,9},{9,8},{10,11... | collective-permute-start | bytes 1572872 | tf_op jit(solution)/shard_map/cotfar_t1/ppermute | solution.py:57
  125.1 27.5 %collective-permute-start.30 = (bf16[256,1024]{1,0:T(8,128)(2,1)S(1)}, bf16[256,1024]{1,0:T(8,128)(2,1)S(1)}, u32[]{:S(2)}, u32[]{:S(2)}) collective-permute-start(bf16[256,1024]{1,0:T(8,128)(2,1)S(1)} %add_convert_fusion.2), channel_id=1, source_target_pairs={{0,2},{1,3},{2,0},{3,1},{4,6},{5,7},{6,4},{7,5},{8,10},{9,11},{10,... | collective-permute-start | bytes 1572872 | tf_op jit(solution)/shard_map/far_t2/ppermute | solution.py:57
  140.4 20.6 %collective-permute-start.28 = (bf16[256,1024]{1,0:T(8,128)(2,1)S(1)}, bf16[256,1024]{1,0:T(8,128)(2,1)S(1)}, u32[]{:S(2)}, u32[]{:S(2)}) collective-permute-start(bf16[256,1024]{1,0:T(8,128)(2,1)S(1)} %copy-done.48), channel_id=1, source_target_pairs={{0,1},{1,0},{2,3},{3,2},{4,5},{5,4},{6,7},{7,6},{8,9},{9,8},{10,11... | collective-permute-start | bytes 1572872 | tf_op jit(solution)/shard_map/lofar_t1/ppermute | solution.py:57
  157.6 14.2 %collective-permute-start.32 = (bf16[256,1024]{1,0:T(8,128)(2,1)}, bf16[256,1024]{1,0:T(8,128)(2,1)S(1)}, u32[]{:S(2)}, u32[]{:S(2)}) collective-permute-start(bf16[256,1024]{1,0:T(8,128)(2,1)} %get-tuple-element.157.refs_5_), channel_id=1, source_target_pairs={{0,2},{1,3},{2,0},{3,1},{4,6},{5,7},{6,4},{7,5},{8,10},{9,11},{10,... | collective-permute-start | bytes 1572872 | tf_op jit(solution)/shard_map/aog_t2/ppermute | solution.py:57
  158.9 14.4 %collective-permute-start.36 = (bf16[3,656,128]{2,1,0:T(8,128)(2,1)S(1)}, bf16[3,656,128]{2,1,0:T(8,128)(2,1)S(1)}, u32[]{:S(2)}, u32[]{:S(2)}) collective-permute-start(bf16[3,656,128]{2,1,0:T(8,128)(2,1)S(1)} %copy-done.52), channel_id=1, source_target_pairs={{0,4},{4,0},{8,12},{12,8},{16,20},{20,16},{24,28},{28,24},{1,5},{5... | collective-permute-start | bytes 1511432 | tf_op jit(solution)/shard_map/gmlp1_d1/ppermute | solution.py:57
  160.2 23.9 %collective-permute-start.34 = (bf16[3,656,128]{2,1,0:T(8,128)(2,1)S(1)}, bf16[3,656,128]{2,1,0:T(8,128)(2,1)S(1)}, u32[]{:S(2)}, u32[]{:S(2)}) collective-permute-start(bf16[3,656,128]{2,1,0:T(8,128)(2,1)S(1)} %copy-done.51), channel_id=1, source_target_pairs={{0,4},{4,0},{8,12},{12,8},{16,20},{20,16},{24,28},{28,24},{1,5},{5... | collective-permute-start | bytes 1511432 | tf_op jit(solution)/shard_map/gmlp0_d1/ppermute | solution.py:57
  161.2 24.9 %collective-permute-start.31 = (bf16[256,1024]{1,0:T(8,128)(2,1)S(1)}, bf16[256,1024]{1,0:T(8,128)(2,1)S(1)}, u32[]{:S(2)}, u32[]{:S(2)}) collective-permute-start(bf16[256,1024]{1,0:T(8,128)(2,1)S(1)} %copy-done.28), channel_id=1, source_target_pairs={{0,1},{1,0},{2,3},{3,2},{4,5},{5,4},{6,7},{7,6},{8,9},{9,8},{10,11... | collective-permute-start | bytes 1572872 | tf_op jit(solution)/shard_map/aog_t1/ppermute | solution.py:57
  171.8 15.6 %collective-permute-start.33 = (bf16[256,1024]{1,0:T(8,128)(2,1)S(1)}, bf16[256,1024]{1,0:T(8,128)(2,1)S(1)}, u32[]{:S(2)}, u32[]{:S(2)}) collective-permute-start(bf16[256,1024]{1,0:T(8,128)(2,1)S(1)} %collective-permute-done.32.refs_7_), channel_id=1, source_target_pairs={{0,1},{1,0},{2,3},{3,2},{4,5},{5,4},{6,7},{7,6},{8,9},{9,8},{10,11... | collective-permute-start | bytes 1572872 | tf_op jit(solution)/shard_map/aogfar_t1/ppermute | solution.py:57
  173.5 39.7 %collective-permute-start.37 = (bf16[3,656,128]{2,1,0:T(8,128)(2,1)S(1)}, bf16[3,656,128]{2,1,0:T(8,128)(2,1)S(1)}, u32[]{:S(2)}, u32[]{:S(2)}) collective-permute-start(bf16[3,656,128]{2,1,0:T(8,128)(2,1)S(1)} %add_convert_fusion.5), channel_id=1, source_target_pairs={{0,8},{4,12},{8,0},{12,4},{16,24},{20,28},{24,16},{28,20},{1,9},{5... | collective-permute-start | bytes 1511432 | tf_op jit(solution)/shard_map/gmlpz1_d2/ppermute | solution.py:57
  175.3 37.9 %collective-permute-start.35 = (bf16[3,656,128]{2,1,0:T(8,128)(2,1)}, bf16[3,656,128]{2,1,0:T(8,128)(2,1)S(1)}, u32[]{:S(2)}, u32[]{:S(2)}) collective-permute-start(bf16[3,656,128]{2,1,0:T(8,128)(2,1)} %get-tuple-element.180), channel_id=1, source_target_pairs={{0,4},{4,0},{8,12},{12,8},{16,20},{20,16},{24,28},{28,24},{1,5},{5... | collective-permute-start | bytes 1511432 | tf_op jit(solution)/shard_map/gmlp2_d1/ppermute | solution.py:57
  184.3 29.2 %collective-permute-start.38 = (bf16[3,656,128]{2,1,0:T(8,128)(2,1)S(1)}, bf16[3,656,128]{2,1,0:T(8,128)(2,1)S(1)}, u32[]{:S(2)}, u32[]{:S(2)}) collective-permute-start(bf16[3,656,128]{2,1,0:T(8,128)(2,1)S(1)} %add_convert_fusion.6), channel_id=1, source_target_pairs={{0,8},{4,12},{8,0},{12,4},{16,24},{20,28},{24,16},{28,20},{1,9},{5... | collective-permute-start | bytes 1511432 | tf_op jit(solution)/shard_map/gmlpz0_d2/ppermute | solution.py:57
  186.1 27.4 %collective-permute-start.39 = (bf16[3,656,128]{2,1,0:T(8,128)(2,1)S(1)}, bf16[3,656,128]{2,1,0:T(8,128)(2,1)S(1)}, u32[]{:S(2)}, u32[]{:S(2)}) collective-permute-start(bf16[3,656,128]{2,1,0:T(8,128)(2,1)S(1)} %copy-done.50), channel_id=1, source_target_pairs={{0,4},{4,0},{8,12},{12,8},{16,20},{20,16},{24,28},{28,24},{1,5},{5... | collective-permute-start | bytes 1511432 | tf_op jit(solution)/shard_map/gmlp3_d1/ppermute | solution.py:57
  216.3 26.5 %collective-permute-start.43 = (bf16[3,656,128]{2,1,0:T(8,128)(2,1)S(1)}, bf16[3,656,128]{2,1,0:T(8,128)(2,1)S(1)}, u32[]{:S(2)}, u32[]{:S(2)}) collective-permute-start(bf16[3,656,128]{2,1,0:T(8,128)(2,1)S(1)} %add_convert_fusion.4), channel_id=1, source_target_pairs={{0,16},{4,20},{8,24},{12,28},{16,0},{20,4},{24,8},{28,12},{1,17},{... | collective-permute-start | bytes 1511432 | tf_op jit(solution)/shard_map/gmlp_d4/ppermute | solution.py:57
  220.3 22.4 %collective-permute-start.51 = (bf16[4,128,256]{2,1,0:T(8,128)(2,1)S(1)}, bf16[4,128,256]{2,1,0:T(8,128)(2,1)S(1)}, u32[]{:S(2)}, u32[]{:S(2)}) collective-permute-start(bf16[4,128,256]{2,1,0:T(8,128)(2,1)S(1)} %copy-done.54), channel_id=1, source_target_pairs={{0,4},{4,0},{8,12},{12,8},{16,20},{20,16},{24,28},{28,24},{1,5},{5... | collective-permute-start | bytes 786440 | tf_op jit(solution)/shard_map/gqkv2_d1/ppermute | solution.py:57
  224.1 25.3 %collective-permute-start.41 = (bf16[272,1024]{1,0:T(8,128)(2,1)}, bf16[272,1024]{1,0:T(8,128)(2,1)S(1)}, u32[]{:S(2)}, u32[]{:S(2)}) collective-permute-start(bf16[272,1024]{1,0:T(8,128)(2,1)} %get-tuple-element.186), channel_id=1, source_target_pairs={{0,2},{1,3},{2,0},{3,1},{4,6},{5,7},{6,4},{7,5},{8,10},{9,11},{10,... | collective-permute-start | bytes 1671176 | tf_op jit(solution)/shard_map/nfar_t2/ppermute | solution.py:57
  224.7 24.7 %collective-permute-start.44 = (bf16[256,1024]{1,0:T(8,128)(2,1)S(1)}, bf16[256,1024]{1,0:T(8,128)(2,1)S(1)}, u32[]{:S(2)}, u32[]{:S(2)}) collective-permute-start(bf16[256,1024]{1,0:T(8,128)(2,1)S(1)} %copy-done.49), channel_id=1, source_target_pairs={{0,1},{1,0},{2,3},{3,2},{4,5},{5,4},{6,7},{7,6},{8,9},{9,8},{10,11... | collective-permute-start | bytes 1572872 | tf_op jit(solution)/shard_map/nnear_t1/ppermute | solution.py:57
  228.9 19.5 %collective-permute-start.53 = (bf16[4,128,256]{2,1,0:T(8,128)(2,1)S(1)}, bf16[4,128,256]{2,1,0:T(8,128)(2,1)S(1)}, u32[]{:S(2)}, u32[]{:S(2)}) collective-permute-start(bf16[4,128,256]{2,1,0:T(8,128)(2,1)S(1)} %add_convert_fusion.8), channel_id=1, source_target_pairs={{0,8},{4,12},{8,0},{12,4},{16,24},{20,28},{24,16},{28,20},{1,9},{5... | collective-permute-start | bytes 786440 | tf_op jit(solution)/shard_map/gqkvz1_d2/ppermute | solution.py:57
  242.8 24.6 %collective-permute-start.50 = (bf16[4,128,256]{2,1,0:T(8,128)(2,1)S(1)}, bf16[4,128,256]{2,1,0:T(8,128)(2,1)S(1)}, u32[]{:S(2)}, u32[]{:S(2)}) collective-permute-start(bf16[4,128,256]{2,1,0:T(8,128)(2,1)S(1)} %add_convert_fusion.9), channel_id=1, source_target_pairs={{0,8},{4,12},{8,0},{12,4},{16,24},{20,28},{24,16},{28,20},{1,9},{5... | collective-permute-start | bytes 786440 | tf_op jit(solution)/shard_map/gqkvz0_d2/ppermute | solution.py:57
  248.6 18.7 %collective-permute-start.54 = (bf16[4,128,256]{2,1,0:T(8,128)(2,1)S(1)}, bf16[4,128,256]{2,1,0:T(8,128)(2,1)S(1)}, u32[]{:S(2)}, u32[]{:S(2)}) collective-permute-start(bf16[4,128,256]{2,1,0:T(8,128)(2,1)S(1)} %add_convert_fusion.7), channel_id=1, source_target_pairs={{0,16},{4,20},{8,24},{12,28},{16,0},{20,4},{24,8},{28,12},{1,17},{... | collective-permute-start | bytes 786440 | tf_op jit(solution)/shard_map/gqkv_d4/ppermute | solution.py:57
  (79 other events, 737.0 us)
where the time goes:
time: 274 us; the launch traced here: 270 us
  waiting for transfers between devices  95.6 us (35%)
  Pallas kernels  87.8 us (32%)
  starting transfers between devices  67.6 us (25%)
  local copies, waits for them, and re-layouts  12.5 us (5%)
  other arithmetic  5.38 us (2%)
    ppermute x55, waiting for transfers between devices, swap(): return lax.ppermute(value, axis, [(i, i ^ distance) for i in range(size)])  95.6 us
    pallas_call x11, Pallas kernels, call(): pl.pallas_call(body, out_shape=[jax.ShapeDtypeStruct(o[0], o[1]) for o in...  87.8 us
    ppermute x55, starting transfers between devices, swap(): return lax.ppermute(value, axis, [(i, i ^ distance) for i in range(size)])  67.6 us
    unnamed x113, local copies, waits for them, and re-layouts  8.83 us
  transfers between devices with their start and end apart: 55, of which 25 were waited for; matrix products, arithmetic and copies ran while one was open for 3% of the time, Pallas kernels for 28%

commit v1 on v0

--- a/solution.py
+++ b/solution.py
@@ -75,6 +75,13 @@
     return copies
 
 
+def stop_rows(source, targets, sem, at):
+    rows = targets[0].shape[0]
+    return [
+        start(source.at[pl.ds(i * rows, rows)], x, sem.at[at + i]) for i, x in enumerate(targets)
+    ]
+
+
 def wait(copies):
     for c in copies:
         c.wait()
@@ -107,29 +114,34 @@
     pieces = refs[7 : 7 + n_pieces]
     refs = refs[7 + n_pieces :]
     parts, (mixed_out, q_out, k_out, v_out, lse_ref) = refs[0:4], refs[4:9]
-    n, tab, w, q, k, v, mixed, sem_w, sem = refs[9:]
+    n, tab, w, q, k, v, mixed, part, sem_w, sem = refs[9:]
     rows, width = n.shape[1], w.shape[2]
     loads = start_pieces(pieces, offs, piece_rows, w, sem_w, 1)
     norm_loads = [start(norms[i], n.at[i], sem.at[i]) for i in range(4)]
     table_load = start(table, tab, sem.at[4])
     wait(loads)
     table_load.wait()
-    for i in range(4):
-        at = pl.ds(i * rows, rows)
+    wait(norm_loads)
+
+    def project(i, carry):
+        at = pl.ds(pl.multiple_of(i * rows, rows), rows)
         cos, sin = angles_at(tab, mine[0] ^ i, rows)
-        norm_loads[i].wait()
         for j, ref in ((0, q), (1, k)):
             u = mm(n[i], w[j])
             for g in range(width // 128):
                 col = slice(g * 128, g * 128 + 128)
                 ref[at, col] = turn(u[:, col], cos, sin).astype(BF)
         v[at, :] = mm(n[i], w[2]).astype(BF)
+        return carry
+
+    lax.fori_loop(0, 4, project, 0)
     stores = [start(x, y, sem.at[5 + i]) for i, (x, y) in enumerate(((q, q_out), (k, k_out), (v, v_out)))]
     factor = scale * LOG2E
     heads = width // HD
     group = 2 * rows
-    for half in range(2):
-        at = pl.ds(half * group, group)
+
+    def attend(half, carry):
+        at = pl.ds(pl.multiple_of(half * group, group), group)
         masks = [head_mask((group, width), h) for h in range(heads)]
 
         def scores(h):
@@ -150,10 +162,12 @@
             s = ahead
         low = acc.astype(BF)
         mixed[at, :] = low
-        part = mm(low, w[3], NT).astype(BF)
-        parts[2 * half][...] = part[:rows]
-        parts[2 * half + 1][...] = part[rows:]
+        part[at, :] = mm(low, w[3], NT).astype(BF)
+        return carry
+
+    lax.fori_loop(0, 2, attend, 0)
     stores.append(start(mixed, mixed_out, sem.at[8]))
+    stores += stop_rows(part, parts, sem, 9)
     wait(stores)
 
 
@@ -188,22 +202,26 @@
 INV_SQRT2PI = 1.0 / math.sqrt(2.0 * math.pi)
 
 
-def feed_rows(n, c, w, grads, outs, hid, gug):
-    rows = n.shape[1]
-    products = [(mm(n[i], w[0], NT), mm(n[i], w[1], NT), mm(c[i], w[2], NT)) for i in range(2)]
-    for i, (gate, up, back) in enumerate(products):
-        at = pl.ds(i * rows, rows)
+def feed_rows(n, c, w, grad, out, hid, gug, count, rows):
+    def one_block(i, carry):
+        at = pl.ds(pl.multiple_of(i * rows, rows), rows)
+        gate = mm(n[at, :], w[0], NT)
+        up = mm(n[at, :], w[1], NT)
+        back = mm(c[at, :], w[2], NT)
         cdf = 0.5 * (1.0 + lax.erf(gate * INV_SQRT2))
         pdf = jnp.exp(-0.5 * gate * gate) * INV_SQRT2PI
         act = gate * cdf
         hidden = (act * up).astype(BF)
         g0 = (back * up * (cdf + gate * pdf)).astype(BF)
         g1 = (back * act).astype(BF)
-        grads[i][...] = (mm(g0, w[0]) + mm(g1, w[1])).astype(BF)
-        outs[i][...] = mm(hidden, w[2]).astype(BF)
+        grad[at, :] = (mm(g0, w[0]) + mm(g1, w[1])).astype(BF)
+        out[at, :] = mm(hidden, w[2]).astype(BF)
         hid[:, at] = hidden.T
         gug[0, :, at] = g0.T
         gug[1, :, at] = g1.T
+        return carry
+
+    lax.fori_loop(0, count, one_block, 0)
 
 
 def load_mlp(pieces, offs, size, w, sem):
@@ -214,18 +232,15 @@
 
 def feed_far(n_pieces, size, refs):
     offs, n_in, c_in, pieces = refs[0], refs[1:3], refs[3:5], refs[5 : 5 + n_pieces]
-    grads, outs, (hid, gug), (n, c, w, sem_w, sem) = (
-        refs[5 + n_pieces : 7 + n_pieces],
-        refs[7 + n_pieces : 9 + n_pieces],
-        refs[9 + n_pieces : 11 + n_pieces],
-        refs[11 + n_pieces :],
-    )
-    loads = [start(n_in[i], n.at[i], sem.at[i]) for i in range(2)]
-    loads += [start(c_in[i], c.at[i], sem.at[2 + i]) for i in range(2)]
+    refs = refs[5 + n_pieces :]
+    grads, outs, (hid, gug) = refs[0:2], refs[2:4], refs[4:6]
+    n, c, grad, out, w, sem_w, sem = refs[6:]
+    loads = start_rows(n_in, n, sem, 0) + start_rows(c_in, c, sem, 2)
     for group in load_mlp(pieces, offs, size, w, sem_w):
         wait(group)
     wait(loads)
-    feed_rows(n, c, w, grads, outs, hid, gug)
+    feed_rows(n, c, w, grad, out, hid, gug, 2, n_in[0].shape[0])
+    wait(stop_rows(grad, grads, sem, 0) + stop_rows(out, outs, sem, 2))
 
 
 def pick_columns(ref, first, second, size):
@@ -234,30 +249,30 @@
     return jnp.concatenate([a, b], axis=1)
 
 
-def mlp_grads(cols, blocks, n, c, hidden, grads, outs):
+def mlp_grads(cols, first_block, n, c, hidden, grads, block_sums):
     group = hidden[0].shape[1]
-    for k, block in enumerate(blocks):
-        first, second = cols[2 * block], cols[2 * block + 1]
-        rights = [pick_columns(x, first, second, 128) for x in (n, c)]
+
+    def one_block(k, carry):
+        at = 2 * (first_block + k)
+        rights = [pick_columns(x, cols[at], cols[at + 1], 128) for x in (n, c)]
         for j in range(3):
             left = hidden if j == 2 else [x.at[j] for x in grads]
             right = rights[1] if j == 2 else rights[0]
             total = mm(left[0][...], right[:group]) + mm(left[1][...], right[group:])
-            outs[2 * k][j] = total[:, :128].astype(BF)
-            outs[2 * k + 1][j] = total[:, 128:].astype(BF)
+            block_sums[k, 0, j] = total[:, :128].astype(BF)
+            block_sums[k, 1, j] = total[:, 128:].astype(BF)
+        return carry
+
+    lax.fori_loop(0, 2, one_block, 0)
+
+
+def stop_blocks(block_sums, blocks, sem, at):
+    return [start(block_sums.at[i // 2, i % 2], x, sem.at[at + i]) for i, x in enumerate(blocks)]
 
 
 def start_rows(sources, target, sem, at):
     rows = sources[0].shape[0]
     return [start(x, target.at[pl.ds(i * rows, rows)], sem.at[at + i]) for i, x in enumerate(sources)]
-
-
-class Halves:
-    def __init__(self, ref, rows):
-        self.ref, self.shape = ref, (2, rows, ref.shape[1])
-
-    def __getitem__(self, i):
-        return self.ref[pl.ds(i * self.shape[1], self.shape[1]), :]
 
 
 def feed_near(n_pieces, size, refs):
@@ -265,32 +280,31 @@
     pieces = refs[12 : 12 + n_pieces]
     refs = refs[12 + n_pieces :]
     grads, outs, (hid, gug), blocks = refs[0:2], refs[2:4], refs[4:6], refs[6:10]
-    n, c, hf, gf, w, sem_w, sem = refs[10:]
-    loads = start_rows(n_in, n, sem, 0)[:2]
+    n, c, hf, gf, grad, out, block_sums, w, sem_w, sem = refs[10:]
+    loads = start_rows(n_in, n, sem, 0)
     groups = load_mlp(pieces, offs, size, w, sem_w)
-    rows = n_in[0].shape[0]
-    more = start_rows(c_in, c, sem, 4)
+    loads += start_rows(c_in, c, sem, 4)
     late = [start(hid_far, hf, sem.at[8]), start(gug_far, gf, sem.at[9])]
     for group in groups:
         wait(group)
     wait(loads)
-    wait(more)
-    feed_rows(Halves(n, rows), Halves(c, rows), w, grads, outs, hid, gug)
-    for i in (2, 3):
-        pltpu.make_async_copy(n_in[i], n.at[pl.ds(i * rows, rows)], sem.at[i]).wait()
+    feed_rows(n, c, w, grad, out, hid, gug, 2, n_in[0].shape[0])
     wait(late)
-    mlp_grads(cols, (0, 1), n, c, (hid, hf), (gug, gf), blocks)
+    stores = stop_rows(grad, grads, sem, 0) + stop_rows(out, outs, sem, 2)
+    mlp_grads(cols, 0, n, c, (hid, hf), (gug, gf), block_sums)
+    wait(stores + stop_blocks(block_sums, blocks, sem, 4))
 
 
 def feed_late(refs):
     cols, n_in, c_in = refs[0], refs[1:5], refs[5:9]
     sources, blocks = refs[9:13], refs[13:17]
-    n, c, hn, hf, gn, gf, sem = refs[17:]
+    n, c, hn, hf, gn, gf, block_sums, sem = refs[17:]
     loads = start_rows(n_in, n, sem, 0)
     loads += [start(x, y, sem.at[8 + i]) for i, (x, y) in enumerate(zip(sources, (hn, hf, gn, gf)))]
     loads += start_rows(c_in, c, sem, 4)
     wait(loads)
-    mlp_grads(cols, (2, 3), n, c, (hn, hf), (gn, gf), blocks)
+    mlp_grads(cols, 2, n, c, (hn, hf), (gn, gf), block_sums)
+    wait(stop_blocks(block_sums, blocks, sem, 0))
 
 
 def norm_back(v, g):
@@ -320,7 +334,7 @@
     pieces = refs[14 : 14 + n_pieces]
     refs = refs[14 + n_pieces :]
     outs, parts, gain_ref = refs[0:8], refs[8:12], refs[12]
-    pg, do, o, q, k, v, lse, tab, n, a, dot_rows, dq, w, sem_w, sem = refs[13:]
+    pg, do, o, q, k, v, lse, tab, n, a, dot_rows, dq, w, block_sums, sent, sem_w, sem = refs[13:]
     rows = grads_in[0].shape[0]
     length, width = q.shape
     heads = width // HD
@@ -331,20 +345,23 @@
     late = [start(table, tab, sem.at[12])]
     late += start_rows(norms, n, sem, 13)
     wait(weights)
-    for i in range(4):
-        grads[i].wait()
-        at = pl.ds(i * rows, rows)
-        do[at, :] = mm(a[at, :], w[3]).astype(BF)
+    wait(grads)
     wait(near)
     lane = lax.broadcasted_iota(jnp.int32, (8, width), 1) >> 6
     head = lax.broadcasted_iota(jnp.int32, (8, width), 0)
     ones = jnp.where(lane == head, 1.0, 0.0).astype(BF)
-    for i in range(4):
-        at = pl.ds(i * rows, rows)
-        t = do[at, :].astype(F32) * o[at, :].astype(F32)
+
+    def output_grads(i, carry):
+        at = pl.ds(pl.multiple_of(i * rows, rows), rows)
+        d = mm(a[at, :], w[3]).astype(BF)
+        do[at, :] = d
+        t = d.astype(F32) * o[at, :].astype(F32)
         hi = t.astype(BF)
         lo = (t - hi.astype(F32)).astype(BF)
         dot_rows[:, at] = mm(ones, hi, NT) + mm(ones, lo, NT)
+        return carry
+
+    lax.fori_loop(0, 4, output_grads, 0)
     dq[...] = jnp.zeros_like(dq)
     factor = scale * LOG2E
     nil = jnp.zeros((), BF)
@@ -378,33 +395,46 @@
 
     wait(late[:1])
     lax.fori_loop(0, 4, one_block, 0)
-    for i in range(4):
-        at = pl.ds(i * rows, rows)
+
+    def query_grads(i, carry):
+        at = pl.ds(pl.multiple_of(i * rows, rows), rows)
         cos, sin = angles_at(tab, mine[0] ^ i, rows)
         for g in range(width // 128):
             col = slice(g * 128, g * 128 + 128)
             pg[at, col] = turn(dq[at, col] * scale, cos, -sin).astype(BF)
+        return carry
+
+    lax.fori_loop(0, 4, query_grads, 0)
     wait(late[1:])
-    for block in range(4):
+
+    def weight_grads(block, carry):
         first, second = cols[2 * block], cols[2 * block + 1]
         total = mm(pick_columns(n, first, second, 128), pg[...], TN)
-        for j in range(3):
-            part = total[:, j * width : (j + 1) * width].astype(BF)
-            outs[2 * block][j] = part[:128]
-            outs[2 * block + 1][j] = part[128:]
-        part = mm(pick_columns(a, first, second, 128), o[...], TN).astype(BF)
-        outs[2 * block][3] = part[:128]
-        outs[2 * block + 1][3] = part[128:]
-    sums = None
-    for i in range(4):
-        at = pl.ds(i * rows, rows)
+        last = mm(pick_columns(a, first, second, 128), o[...], TN)
+        for j in range(4):
+            part = last if j == 3 else total[:, j * width : (j + 1) * width]
+            part = part.astype(BF)
+            block_sums[block, 0, j] = part[:128]
+            block_sums[block, 1, j] = part[128:]
+        return carry
+
+    lax.fori_loop(0, 4, weight_grads, 0)
+    stores = stop_blocks(block_sums, outs, sem, 0)
+
+    def row_grads(i, sums):
+        at = pl.ds(pl.multiple_of(i * rows, rows), rows)
         total = sum(mm(pg[at, j * width : (j + 1) * width], w[j], NT) for j in range(3))
-        parts[i][pl.ds(0, rows), :] = total.astype(BF)
-        part = jnp.sum(total * n[at, :].astype(F32), axis=0, keepdims=True)
-        sums = part if sums is None else sums + part
+        sent[at, :] = total.astype(BF)
+        return sums + jnp.sum(total * n[at, :].astype(F32), axis=0, keepdims=True)
+
+    sums = lax.fori_loop(0, 4, row_grads, jnp.zeros((1, n.shape[1]), F32))
     sums = sums / gain[...]
     both = [sums[:, 128 * i : 128 * i + 128] for i in range(8)] + [gain_two[...]]
-    gain_ref[...] = write_gains(parts[3], rows, jnp.concatenate(both, axis=0))
+    gain_ref[...] = write_gains(sent, length, jnp.concatenate(both, axis=0))
+    ends = [rows] * 3 + [rows + 16]
+    for i in range(4):
+        stores.append(start(sent.at[pl.ds(i * rows, ends[i])], parts[i], sem.at[8 + i]))
+    wait(stores)
 
 
 def write_gains(ref, rows, gains):
@@ -543,10 +573,10 @@
         scalar(offs, mine_one)
         + away(normed_attn)
         + away([table] + qkvo),
-        [vm((rows, model))] * 4 + [hb((length, width))] * 4 + [vm((8, length), F32)],
+        [hb((rows, model))] * 4 + [hb((length, width))] * 4 + [vm((8, length), F32)],
         [buf(4, rows, model), buf(length, 128, dtype=F32), buf(4, model, width)]
         + [buf(length, width)] * 4
-        + [sems(n_pieces), sems(9)],
+        + [buf(length, model), sems(n_pieces), sems(13)],
         name="attend_forward",
     )
     if direct:
@@ -573,8 +603,8 @@
     far_back, far_send, far_out, far_out_send, far_hidden, far_grad = call(
         body(feed_far, n_pieces, piece),
         scalar(offs) + away(normed_mlp[2:] + cot[2:] + mlp),
-        [vm((rows, model))] * 4 + [vm((units, 2 * rows)), vm((2, units, 2 * rows))],
-        [buf(2, rows, model)] * 2 + [buf(3, units, model), sems(3, n_pieces), sems(4)],
+        [hb((rows, model))] * 4 + [vm((units, 2 * rows)), vm((2, units, 2 * rows))],
+        [buf(2 * rows, model)] * 4 + [buf(3, units, model), sems(3, n_pieces), sems(4)],
         name="feed_far",
     )
     far_sum = add(far_back, tensor(far_send, 1, "far"))
@@ -583,12 +613,13 @@
         body(feed_near, n_pieces, piece),
         scalar(offs, cols)
         + away(gate(normed_mlp, [far_sum]) + cot + [far_hidden, far_grad] + mlp),
-        [vm((rows, model))] * 4
+        [hb((rows, model))] * 4
         + [vm((units, 2 * rows)), vm((2, units, 2 * rows))]
-        + [vm((3, units, 128))] * 4,
+        + [hb((3, units, 128))] * 4,
         [buf(length, model)] * 2
         + [buf(units, 2 * rows), buf(2, units, 2 * rows)]
-        + [buf(3, units, model), sems(3, n_pieces), sems(10)],
+        + [buf(2 * rows, model)] * 2
+        + [buf(2, 2, 3, units, 128), buf(3, units, model), sems(3, n_pieces), sems(10)],
         name="feed_near",
     )
     near_got = tensor(near_send, 1, "near")
@@ -602,39 +633,47 @@
         name="middle_back",
     )
     attn_out_grad = spread(low_grad, "aog")
+    if direct:
+        (grads[0],) = gate(grads[:1], [from_far])
+        got = [depth(grads[0], 1, "gmlp0")]
+        sums = [add(grads[1], got[0])]
+        (grads[2],) = gate(grads[2:3], sums)
+        before = [low_grad, sums[0], out_sum, out_near]
+    else:
+        before = [low_grad]
     grads += call(
         body(feed_late),
         scalar(cols)
-        + away(gate(normed_mlp, [low_grad, out_sum, out_near]) + cot + [near_hidden, far_hidden, near_grad, far_grad]),
-        [vm((3, units, 128))] * 4,
+        + away(gate(normed_mlp, before) + cot + [near_hidden, far_hidden, near_grad, far_grad]),
+        [hb((3, units, 128))] * 4,
         [buf(length, model)] * 2
         + [buf(units, 2 * rows)] * 2
         + [buf(2, units, 2 * rows)] * 2
-        + [sems(12)],
+        + [buf(2, 2, 3, units, 128), sems(12)],
         name="feed_late",
     )
     early = [grads[7]]
     if direct:
-        grads[0], grads[2] = gate([grads[0], grads[2]], [from_far])
         grads[4], grads[6] = gate([grads[4], grads[6]], [attn_out_grad[2]])
-        got = [depth(grads[2 * i], 1, f"gmlp{i}") for i in range(4)]
-        sums = [add(grads[2 * i + 1], got[i]) for i in range(2)]
-        early.append(sums[0])
+        got += [depth(grads[2 * i], 1, f"gmlp{i}") for i in (1, 2, 3)]
+        sums.append(add(grads[3], got[1]))
         back = [depth(sums[i], 2, f"gmlpz{i}") for i in range(2)]
+        early.append(sums[1])
 
     *attn, b0, b1, b2, b3, gains = call(
         body(attend_backward, n_pieces, piece, scale),
         scalar(cols, mine_one, offs)
         + near(gain_one, gain_two_part)
         + away(gate(attn_out_grad, early) + [mixed, q, k, v, lse, table] + normed_attn + qkvo),
-        [vm((4, 128, width))] * 8
-        + [vm((rows, model))] * 3
-        + [vm((rows + 16, model)), vm((16, 128), F32)],
+        [hb((4, 128, width))] * 8
+        + [hb((rows, model))] * 3
+        + [hb((rows + 16, model)), vm((16, 128), F32)],
         [buf(length, 3 * width)]
         + [buf(length, width)] * 5
         + [buf(8, length, dtype=F32), buf(length, 128, dtype=F32), buf(length, model), buf(length, model)]
         + [buf(8, length, dtype=F32), buf(length, width, dtype=F32)]
-        + [buf(4, model, width), sems(n_pieces), sems(17)],
+        + [buf(4, model, width), buf(4, 2, 4, 128, width), buf(length + 16, model)]
+        + [sems(n_pieces), sems(17)],
         name="attend_backward",
     )
     if direct:

time: 274 us -> 265 us (0.967); the launches traced: 270 us -> 264 us
  starting transfers between devices: 67.6 us -> 59 us
  Pallas kernels: 87.8 us -> 96 us
  waiting for transfers between devices: 95.6 us -> 90.4 us
    ppermute x55, starting transfers between devices: 67.6 us -> 59 us  [swap(): return lax.ppermute(value, axis, [(i, i ^ distance) for i in range(size)])]
    pallas_call x11, Pallas kernels: 87.8 us -> 96 us  [call(): pl.pallas_call(body, out_shape=[jax.ShapeDtypeStruct(o[0], o[1]) for o in...]
    ppermute x55, waiting for transfers between devices: 95.6 us -> 90.4 us  [swap(): return lax.ppermute(value, axis, [(i, i ^ distance) for i in range(size)])]
  transfers between devices with their start and end apart: 55 -> 55, of which waited for: 25 -> 26; matrix products, arithmetic and copies ran while one was open for 3% -> 3% of each run, Pallas kernels for 28% -> 31%
where the time goes in v1:
time: 265 us; the launch traced here: 264 us
  Pallas kernels  96 us (36%)
  waiting for transfers between devices  90.4 us (34%)
  starting transfers between devices  59 us (22%)
  local copies, waits for them, and re-layouts  12.3 us (5%)
  other arithmetic  5.4 us (2%)
    pallas_call x11, Pallas kernels, call(): pl.pallas_call(body, out_shape=[jax.ShapeDtypeStruct(o[0], o[1]) for o in...  96 us
    ppermute x55, waiting for transfers between devices, swap(): return lax.ppermute(value, axis, [(i, i ^ distance) for i in range(size)])  90.4 us
    ppermute x55, starting transfers between devices, swap(): return lax.ppermute(value, axis, [(i, i ^ distance) for i in range(size)])  59 us
    unnamed x113, local copies, waits for them, and re-layouts  8.63 us
  transfers between devices with their start and end apart: 55, of which 26 were waited for; matrix products, arithmetic and copies ran while one was open for 3% of the time, Pallas kernels for 31%

profile of v1, /device:TPU:0, one launch (start us, length us, event | category | flops | bytes accessed | tf_op | source)
XLA Modules:
  0.0 264.4 jit_solution(9195623548110567561)
XLA Ops:
  0.6 2.1 pack.1
  2.7 4.0 %collective-permute-start.2 = (bf16[4,128,256]{2,1,0:T(8,128)(2,1)}, bf16[4,128,256]{2,1,0:T(8,128)(2,1)S(1)}, u32[]{:S(2)}, u32[]{:S(2)}) collective-permute-start(bf16[4,128,256]{2,1,0:T(8,128)(2,1)} %get-tuple-element.107.refs_7_.refs_19_), channel_id=1, source_target_pairs={{0,16},{4,20},{8,24},{12,28},{16,0},{20,4},{24,8},{28,12},{1,17},{... | collective-permute-start | bytes 786440 | tf_op jit(solution)/shard_map/qkvo_d4/ppermute | solution.py:57
  9.8 2.2 norm.1.refs_2_.refs_15_
  12.0 6.9 %collective-permute-done.2.refs_11_.refs_23_ = bf16[4,128,256]{2,1,0:T(8,128)(2,1)S(1)} collective-permute-done((bf16[4,128,256]{2,1,0:T(8,128)(2,1)}, bf16[4,128,256]{2,1,0:T(8,128)(2,1)S(1)}, u32[]{:S(2)}, u32[]{:S(2)}) %collective-permute-start.2) | collective-permute-done | bytes 262176 | tf_op jit(solution)/shard_map/qkvo_d4/ppermute | solution.py:57
  22.2 5.3 %collective-permute-done.8.refs_13_.refs_25_ = bf16[4,128,256]{2,1,0:T(8,128)(2,1)S(1)} collective-permute-done((bf16[4,128,256]{2,1,0:T(8,128)(2,1)S(1)}, bf16[4,128,256]{2,1,0:T(8,128)(2,1)S(1)}, u32[]{:S(2)}, u32[]{:S(2)}) %collective-permute-start.8) | collective-permute-done | bytes 262176 | tf_op jit(solution)/shard_map/qkvofar_d2/ppermute | solution.py:57
  32.3 4.4 %collective-permute-done.9.refs_14_.refs_26_ = bf16[4,128,256]{2,1,0:T(8,128)(2,1)S(1)} collective-permute-done((bf16[4,128,256]{2,1,0:T(8,128)(2,1)S(1)}, bf16[4,128,256]{2,1,0:T(8,128)(2,1)S(1)}, u32[]{:S(2)}, u32[]{:S(2)}) %collective-permute-start.9) | collective-permute-done | bytes 262176 | tf_op jit(solution)/shard_map/qkvo3_d1/ppermute | solution.py:57
  36.7 3.3 %collective-permute-start.11 = (bf16[3,656,128]{2,1,0:T(8,128)(2,1)}, bf16[3,656,128]{2,1,0:T(8,128)(2,1)S(1)}, u32[]{:S(2)}, u32[]{:S(2)}) collective-permute-start(bf16[3,656,128]{2,1,0:T(8,128)(2,1)} %get-tuple-element.116.refs_5_.refs_12_), channel_id=1, source_target_pairs={{0,16},{4,20},{8,24},{12,28},{16,0},{20,4},{24,8},{28,12},{1,17},{... | collective-permute-start | bytes 1511432 | tf_op jit(solution)/shard_map/mlp_d4/ppermute | solution.py:57
  41.7 2.1 collective-permute-start.10
  48.0 14.6 %attend_forward.1 = (bf16[256,1024]{1,0:T(8,128)(2,1)}, bf16[256,1024]{1,0:T(8,128)(2,1)}, bf16[256,1024]{1,0:T(8,128)(2,1)}, bf16[256,1024]{1,0:T(8,128)(2,1)},...) custom-call(s32[8]{0:T(128)} %iota_xor_fusion.refs_0_.refs_2_, ...), custom_call_target="tpu_custom_call" | custom-call | flops 1000 | bytes 1000 | tf_op jit(solution)/shard_map/attend_forward/pallas_call | solution.py:43
  70.7 9.3 %collective-permute-done.13.refs_8_.refs_15_ = bf16[3,656,128]{2,1,0:T(8,128)(2,1)S(1)} collective-permute-done((bf16[3,656,128]{2,1,0:T(8,128)(2,1)S(1)}, bf16[3,656,128]{2,1,0:T(8,128)(2,1)S(1)}, u32[]{:S(2)}, u32[]{:S(2)}) %collective-permute-start.13) | collective-permute-done | bytes 503840 | tf_op jit(solution)/shard_map/mlp1_d1/ppermute | solution.py:57
  81.8 3.0 %middle_rows.1 = (f32[256,1024]{1,0:T(8,128)}, bf16[256,1024]{1,0:T(8,128)(2,1)}) custom-call(bf16[256,1024]{1,0:T(8,128)(2,1)} %h.1, f32[1,1024]{1,0:T(1,128)} %bitcast.28, bf16[256,1024]{1,0:T(8,128)(2,1)} %get-tuple-element.121.a, bf16[256,1024]{1,0:T(8,128)(2,1)} %copy-done.35, bf16[256,1024]{1,0:T(8,128)(2,1)} %copy-done.36), custom_call_target="tpu_custom_call" | custom-call | flops 1000 | bytes 1000 | tf_op jit(solution)/shard_map/middle_rows/pallas_call | solution.py:43
  87.9 4.3 %collective-permute-done.23.refs_3_.refs_8_.refs_7_ = bf16[256,1024]{1,0:T(8,128)(2,1)S(1)} collective-permute-done((bf16[256,1024]{1,0:T(8,128)(2,1)S(1)}, bf16[256,1024]{1,0:T(8,128)(2,1)S(1)}, u32[]{:S(2)}, u32[]{:S(2)}) %collective-permute-start.23) | collective-permute-done | bytes 524320 | tf_op jit(solution)/shard_map/cot_t2/ppermute | solution.py:57
  92.2 8.1 %collective-permute-done.20.refs_10_.refs_17_ = bf16[3,656,128]{2,1,0:T(8,128)(2,1)S(1)} collective-permute-done((bf16[3,656,128]{2,1,0:T(8,128)(2,1)S(1)}, bf16[3,656,128]{2,1,0:T(8,128)(2,1)S(1)}, u32[]{:S(2)}, u32[]{:S(2)}) %collective-permute-start.20) | collective-permute-done | bytes 503840 | tf_op jit(solution)/shard_map/mlp2_d1/ppermute | solution.py:57
  100.3 8.2 %collective-permute-done.21.refs_12_.refs_19_ = bf16[3,656,128]{2,1,0:T(8,128)(2,1)S(1)} collective-permute-done((bf16[3,656,128]{2,1,0:T(8,128)(2,1)S(1)}, bf16[3,656,128]{2,1,0:T(8,128)(2,1)S(1)}, u32[]{:S(2)}, u32[]{:S(2)}) %collective-permute-start.21) | collective-permute-done | bytes 503840 | tf_op jit(solution)/shard_map/mlp3_d1/ppermute | solution.py:57
  108.6 1.9 collective-permute-done.22.refs_2_.refs_5_.refs_4_
  111.4 12.2 %feed_far.1 = (bf16[256,1024]{1,0:T(8,128)(2,1)}, bf16[256,1024]{1,0:T(8,128)(2,1)}, bf16[256,1024]{1,0:T(8,128)(2,1)}, bf16[256,1024]{1,0:T(8,128)(2,1)}, bf16[...) custom-call(s32[8]{0:T(128)} %iota_xor_fusion.refs_0_.refs_2_, bf16[256,1024]{1,0:T(8,128)(2,1)} %copy-done.1, ...), custom_call_target="tpu_custom_call" | custom-call | flops 1000 | bytes 1000 | tf_op jit(solution)/shard_map/feed_far/pallas_call | solution.py:43
  129.4 16.1 %feed_near.1 = (bf16[256,1024]{1,0:T(8,128)(2,1)}, bf16[256,1024]{1,0:T(8,128)(2,1)}, bf16[256,1024]{1,0:T(8,128)(2,1)}, bf16[256,1024]{1,0:T(8,128)(2,1)}, bf16...) custom-call(s32[8]{0:T(128)} %iota_xor_fusion.refs_0_.refs_2_, ...), custom_call_target="tpu_custom_call" | custom-call | flops 1000 | bytes 1000 | tf_op jit(solution)/shard_map/feed_near/pallas_call | solution.py:43
  148.5 3.9 %middle_back.1 = (f32[256,1024]{1,0:T(8,128)}, bf16[256,1024]{1,0:T(8,128)(2,1)}, f32[8,128]{1,0:T(8,128)}) custom-call(f32[256,1024]{1,0:T(8,128)} %get-tuple-element.125.mid, bf16[256,1024]{1,0:T(8,128)(2,1)} %refs_5_, f32[1,1024]{1,0:T(1,128)} %bitcast.29, bf16[256,1024]{1,0:T(8,128)(2,1)} %get-tuple-element.142.sa, bf16[256,1024]{1,0:T(8,128)(2,1)} %copy-done.37, ...), custom_call_target="tpu_custom_call" | custom-call | flops 1000 | bytes 1000 | tf_op jit(solution)/shard_map/middle_back/pallas_call | solution.py:43
  153.8 5.9 %collective-permute-done.34 = bf16[3,656,128]{2,1,0:T(8,128)(2,1)S(1)} collective-permute-done((bf16[3,656,128]{2,1,0:T(8,128)(2,1)}, bf16[3,656,128]{2,1,0:T(8,128)(2,1)S(1)}, u32[]{:S(2)}, u32[]{:S(2)}) %collective-permute-start.34) | collective-permute-done | bytes 503840 | tf_op jit(solution)/shard_map/gmlp0_d1/ppermute | solution.py:57
  161.4 8.0 %feed_late.1 = (bf16[3,656,128]{2,1,0:T(8,128)(2,1)}, bf16[3,656,128]{2,1,0:T(8,128)(2,1)}, bf16[3,656,128]{2,1,0:T(8,128)(2,1)}, bf16[3,656,128]{2,1,0:T(8,128)(2,1)}) custom-call(s32[8]{0:T(128)} %stack.35.refs_1_.refs_0_, bf16[256,1024]{1,0:T(8,128)(2,1)} %get-tuple-element.149.refs_2_.refs_1_, bf16[256,1024]{1,0:T(8,128)(2,1)} %copy-done.11, ...), custom_call_target="tpu_custom_call" | custom-call | flops 1000 | bytes 1000 | tf_op jit(solution)/shard_map/feed_late/pallas_call | solution.py:43
  170.6 2.5 collective-permute-done.35
  173.2 1.8 collective-permute-start.37
  177.6 28.0 %attend_backward.1 = (bf16[4,128,256]{2,1,0:T(8,128)(2,1)}, bf16[4,128,256]{2,1,0:T(8,128)(2,1)}, bf16[4,128,256]{2,1,0:T(8,128)(2,1)}, bf16[4,128,256]{2,1,0:T(...) custom-call(s32[8]{0:T(128)} %stack.35.refs_1_.refs_0_, ...), custom_call_target="tpu_custom_call" | custom-call | flops 1000 | bytes 1000 | tf_op jit(solution)/shard_map/attend_backward/pallas_call | solution.py:43
  208.7 4.4 %collective-permute-start.43 = (bf16[3,656,128]{2,1,0:T(8,128)(2,1)S(1)}, bf16[3,656,128]{2,1,0:T(8,128)(2,1)S(1)}, u32[]{:S(2)}, u32[]{:S(2)}) collective-permute-start(bf16[3,656,128]{2,1,0:T(8,128)(2,1)S(1)} %add_convert_fusion.4), channel_id=1, source_target_pairs={{0,16},{4,20},{8,24},{12,28},{16,0},{20,4},{24,8},{28,12},{1,17},{... | collective-permute-start | bytes 1511432 | tf_op jit(solution)/shard_map/gmlp_d4/ppermute | solution.py:57
  214.6 2.1 add_far.1
  218.0 3.4 %collective-permute-done.49 = bf16[4,128,256]{2,1,0:T(8,128)(2,1)S(1)} collective-permute-done((bf16[4,128,256]{2,1,0:T(8,128)(2,1)S(1)}, bf16[4,128,256]{2,1,0:T(8,128)(2,1)S(1)}, u32[]{:S(2)}, u32[]{:S(2)}) %collective-permute-start.49) | collective-permute-done | bytes 262176 | tf_op jit(solution)/shard_map/gqkv0_d1/ppermute | solution.py:57
  223.2 12.4 %collective-permute-done.43 = bf16[3,656,128]{2,1,0:T(8,128)(2,1)S(1)} collective-permute-done((bf16[3,656,128]{2,1,0:T(8,128)(2,1)S(1)}, bf16[3,656,128]{2,1,0:T(8,128)(2,1)S(1)}, u32[]{:S(2)}, u32[]{:S(2)}) %collective-permute-start.43) | collective-permute-done | bytes 503840 | tf_op jit(solution)/shard_map/gmlp_d4/ppermute | solution.py:57
  236.1 3.9 %collective-permute-done.53 = bf16[4,128,256]{2,1,0:T(8,128)(2,1)S(1)} collective-permute-done((bf16[4,128,256]{2,1,0:T(8,128)(2,1)S(1)}, bf16[4,128,256]{2,1,0:T(8,128)(2,1)S(1)}, u32[]{:S(2)}, u32[]{:S(2)}) %collective-permute-start.53) | collective-permute-done | bytes 262176 | tf_op jit(solution)/shard_map/gqkvz1_d2/ppermute | solution.py:57
  240.1 2.8 %collective-permute-start.54 = (bf16[4,128,256]{2,1,0:T(8,128)(2,1)S(1)}, bf16[4,128,256]{2,1,0:T(8,128)(2,1)S(1)}, u32[]{:S(2)}, u32[]{:S(2)}) collective-permute-start(bf16[4,128,256]{2,1,0:T(8,128)(2,1)S(1)} %add_convert_fusion.7), channel_id=1, source_target_pairs={{0,16},{4,20},{8,24},{12,28},{16,0},{20,4},{24,8},{28,12},{1,17},{... | collective-permute-start | bytes 786440 | tf_op jit(solution)/shard_map/gqkv_d4/ppermute | solution.py:57
  243.9 3.7 %input_back.1 = (f32[256,1024]{1,0:T(8,128)}, f32[16,128]{1,0:T(8,128)}) custom-call(bf16[256,1024]{1,0:T(8,128)(2,1)} %h.1, f32[256,1024]{1,0:T(8,128)} %get-tuple-element.188.mg, f32[1,1024]{1,0:T(1,128)} %bitcast.27, bf16[256,1024]{1,0:T(8,128)(2,1)} %get-tuple-element.189.sa, bf16[256,1024]{1,0:T(8,128)(2,1)} %copy-done.32, ...), custom_call_target="tpu_custom_call" | custom-call | flops 1000 | bytes 1000 | tf_op jit(solution)/shard_map/input_back/pallas_call | solution.py:43
  251.6 2.5 collective-permute-start.46
  256.6 3.8 %collective-permute-done.47 = f32[16,128]{1,0:T(8,128)S(1)} collective-permute-done((f32[16,128]{1,0:T(8,128)S(1)}, f32[16,128]{1,0:T(8,128)S(1)}, u32[]{:S(2)}, u32[]{:S(2)}) %collective-permute-start.47) | collective-permute-done | bytes 8224 | tf_op jit(solution)/shard_map/gain_d4/ppermute | solution.py:57
  (224 shorter events, 66.1 us)
Async XLA Ops:
  2.7 16.3 %collective-permute-start.2 = (bf16[4,128,256]{2,1,0:T(8,128)(2,1)}, bf16[4,128,256]{2,1,0:T(8,128)(2,1)S(1)}, u32[]{:S(2)}, u32[]{:S(2)}) collective-permute-start(bf16[4,128,256]{2,1,0:T(8,128)(2,1)} %get-tuple-element.107.refs_7_.refs_19_), channel_id=1, source_target_pairs={{0,16},{4,20},{8,24},{12,28},{16,0},{20,4},{24,8},{28,12},{1,17},{... | collective-permute-start | bytes 786440 | tf_op jit(solution)/shard_map/qkvo_d4/ppermute | solution.py:57
  29.5 15.5 %collective-permute-start.6 = (bf16[4,128,256]{2,1,0:T(8,128)(2,1)S(1)}, bf16[4,128,256]{2,1,0:T(8,128)(2,1)S(1)}, u32[]{:S(2)}, u32[]{:S(2)}) collective-permute-start(bf16[4,128,256]{2,1,0:T(8,128)(2,1)S(1)} %collective-permute-done.1.refs_9_.refs_21_), channel_id=1, source_target_pairs={{0,4},{4,0},{8,12},{12,8},{16,20},{20,16},{24,28},{28,24},{1,5},{5... | collective-permute-start | bytes 786440 | tf_op jit(solution)/shard_map/qkvo1_d1/ppermute | solution.py:57
  31.0 16.0 %collective-permute-start.3 = (bf16[256,1024]{1,0:T(8,128)(2,1)}, bf16[256,1024]{1,0:T(8,128)(2,1)S(1)}, u32[]{:S(2)}, u32[]{:S(2)}) collective-permute-start(bf16[256,1024]{1,0:T(8,128)(2,1)} %norm.1.refs_2_.refs_15_), channel_id=1, source_target_pairs={{0,1},{1,0},{2,3},{3,2},{4,5},{5,4},{6,7},{7,6},{8,9},{9,8},{10,11... | collective-permute-start | bytes 1572872 | tf_op jit(solution)/shard_map/norm_t1/ppermute | solution.py:57
  32.3 14.7 %collective-permute-start.5 = (bf16[256,1024]{1,0:T(8,128)(2,1)S(1)}, bf16[256,1024]{1,0:T(8,128)(2,1)S(1)}, u32[]{:S(2)}, u32[]{:S(2)}) collective-permute-start(bf16[256,1024]{1,0:T(8,128)(2,1)S(1)} %collective-permute-done.4.refs_4_.refs_17_), channel_id=1, source_target_pairs={{0,1},{1,0},{2,3},{3,2},{4,5},{5,4},{6,7},{7,6},{8,9},{9,8},{10,11... | collective-permute-start | bytes 1572872 | tf_op jit(solution)/shard_map/normfar_t1/ppermute | solution.py:57
  36.7 25.9 %collective-permute-start.11 = (bf16[3,656,128]{2,1,0:T(8,128)(2,1)}, bf16[3,656,128]{2,1,0:T(8,128)(2,1)S(1)}, u32[]{:S(2)}, u32[]{:S(2)}) collective-permute-start(bf16[3,656,128]{2,1,0:T(8,128)(2,1)} %get-tuple-element.116.refs_5_.refs_12_), channel_id=1, source_target_pairs={{0,16},{4,20},{8,24},{12,28},{16,0},{20,4},{24,8},{28,12},{1,17},{... | collective-permute-start | bytes 1511432 | tf_op jit(solution)/shard_map/mlp_d4/ppermute | solution.py:57
  41.7 20.9 %collective-permute-start.10 = (bf16[3,656,128]{2,1,0:T(8,128)(2,1)}, bf16[3,656,128]{2,1,0:T(8,128)(2,1)S(1)}, u32[]{:S(2)}, u32[]{:S(2)}) collective-permute-start(bf16[3,656,128]{2,1,0:T(8,128)(2,1)} %get-tuple-element.116.refs_5_.refs_12_), channel_id=1, source_target_pairs={{0,8},{4,12},{8,0},{12,4},{16,24},{20,28},{24,16},{28,20},{1,9},{5... | collective-permute-start | bytes 1511432 | tf_op jit(solution)/shard_map/mlp_d2/ppermute | solution.py:57
  45.0 17.7 %collective-permute-start.12 = (bf16[3,656,128]{2,1,0:T(8,128)(2,1)}, bf16[3,656,128]{2,1,0:T(8,128)(2,1)}, u32[]{:S(2)}, u32[]{:S(2)}) collective-permute-start(bf16[3,656,128]{2,1,0:T(8,128)(2,1)} %get-tuple-element.116.refs_5_.refs_12_), channel_id=1, source_target_pairs={{0,4},{4,0},{8,12},{12,8},{16,20},{20,16},{24,28},{28,24},{1,5},{5... | collective-permute-start | bytes 1511432 | tf_op jit(solution)/shard_map/mlp0_d1/ppermute | solution.py:57
  62.8 17.6 %collective-permute-start.15 = (bf16[256,1024]{1,0:T(8,128)(2,1)}, bf16[256,1024]{1,0:T(8,128)(2,1)S(1)}, u32[]{:S(2)}, u32[]{:S(2)}) collective-permute-start(bf16[256,1024]{1,0:T(8,128)(2,1)} %get-tuple-element.122), channel_id=1, source_target_pairs={{0,1},{1,0},{2,3},{3,2},{4,5},{5,4},{6,7},{7,6},{8,9},{9,8},{10,11... | collective-permute-start | bytes 1572872 | tf_op jit(solution)/shard_map/anear_t1/ppermute | solution.py:57
  66.1 14.8 %collective-permute-start.17 = (bf16[256,1024]{1,0:T(8,128)(2,1)S(1)}, bf16[256,1024]{1,0:T(8,128)(2,1)S(1)}, u32[]{:S(2)}, u32[]{:S(2)}) collective-permute-start(bf16[256,1024]{1,0:T(8,128)(2,1)S(1)} %add_convert_fusion.3), channel_id=1, source_target_pairs={{0,2},{1,3},{2,0},{3,1},{4,6},{5,7},{6,4},{7,5},{8,10},{9,11},{10,... | collective-permute-start | bytes 1572872 | tf_op jit(solution)/shard_map/afar_t2/ppermute | solution.py:57
  69.2 23.0 %collective-permute-start.23 = (bf16[256,1024]{1,0:T(8,128)(2,1)S(1)}, bf16[256,1024]{1,0:T(8,128)(2,1)S(1)}, u32[]{:S(2)}, u32[]{:S(2)}) collective-permute-start(bf16[256,1024]{1,0:T(8,128)(2,1)S(1)} %copy-done.4), channel_id=1, source_target_pairs={{0,2},{1,3},{2,0},{3,1},{4,6},{5,7},{6,4},{7,5},{8,10},{9,11},{10,... | collective-permute-start | bytes 1572872 | tf_op jit(solution)/shard_map/cot_t2/ppermute | solution.py:57
  84.7 23.8 %collective-permute-start.19 = (bf16[256,1024]{1,0:T(8,128)(2,1)}, bf16[256,1024]{1,0:T(8,128)(2,1)S(1)}, u32[]{:S(2)}, u32[]{:S(2)}) collective-permute-start(bf16[256,1024]{1,0:T(8,128)(2,1)} %get-tuple-element.149.refs_2_.refs_1_), channel_id=1, source_target_pairs={{0,2},{1,3},{2,0},{3,1},{4,6},{5,7},{6,4},{7,5},{8,10},{9,11},{10,... | collective-permute-start | bytes 1572872 | tf_op jit(solution)/shard_map/norm2_t2/ppermute | solution.py:57
  85.9 14.4 %collective-permute-start.20 = (bf16[3,656,128]{2,1,0:T(8,128)(2,1)S(1)}, bf16[3,656,128]{2,1,0:T(8,128)(2,1)S(1)}, u32[]{:S(2)}, u32[]{:S(2)}) collective-permute-start(bf16[3,656,128]{2,1,0:T(8,128)(2,1)S(1)} %collective-permute-done.11.refs_9_.refs_16_), channel_id=1, source_target_pairs={{0,4},{4,0},{8,12},{12,8},{16,20},{20,16},{24,28},{28,24},{1,5},{5... | collective-permute-start | bytes 1511432 | tf_op jit(solution)/shard_map/mlp2_d1/ppermute | solution.py:57
  87.2 21.3 %collective-permute-start.21 = (bf16[3,656,128]{2,1,0:T(8,128)(2,1)S(1)}, bf16[3,656,128]{2,1,0:T(8,128)(2,1)S(1)}, u32[]{:S(2)}, u32[]{:S(2)}) collective-permute-start(bf16[3,656,128]{2,1,0:T(8,128)(2,1)S(1)} %collective-permute-done.14.refs_11_.refs_18_), channel_id=1, source_target_pairs={{0,4},{4,0},{8,12},{12,8},{16,20},{20,16},{24,28},{28,24},{1,5},{5... | collective-permute-start | bytes 1511432 | tf_op jit(solution)/shard_map/mlp3_d1/ppermute | solution.py:57
  92.2 16.4 %collective-permute-start.24 = (bf16[256,1024]{1,0:T(8,128)(2,1)S(1)}, bf16[256,1024]{1,0:T(8,128)(2,1)S(1)}, u32[]{:S(2)}, u32[]{:S(2)}) collective-permute-start(bf16[256,1024]{1,0:T(8,128)(2,1)S(1)} %collective-permute-done.23.refs_3_.refs_8_.refs_7_), channel_id=1, source_target_pairs={{0,1},{1,0},{2,3},{3,2},{4,5},{5,4},{6,7},{7,6},{8,9},{9,8},{10,11... | collective-permute-start | bytes 1572872 | tf_op jit(solution)/shard_map/cotfar_t1/ppermute | solution.py:57
  127.0 18.6 %collective-permute-start.30 = (bf16[256,1024]{1,0:T(8,128)(2,1)S(1)}, bf16[256,1024]{1,0:T(8,128)(2,1)S(1)}, u32[]{:S(2)}, u32[]{:S(2)}) collective-permute-start(bf16[256,1024]{1,0:T(8,128)(2,1)S(1)} %add_convert_fusion.2), channel_id=1, source_target_pairs={{0,2},{1,3},{2,0},{3,1},{4,6},{5,7},{6,4},{7,5},{8,10},{9,11},{10,... | collective-permute-start | bytes 1572872 | tf_op jit(solution)/shard_map/far_t2/ppermute | solution.py:57
  145.6 14.1 %collective-permute-start.34 = (bf16[3,656,128]{2,1,0:T(8,128)(2,1)}, bf16[3,656,128]{2,1,0:T(8,128)(2,1)S(1)}, u32[]{:S(2)}, u32[]{:S(2)}) collective-permute-start(bf16[3,656,128]{2,1,0:T(8,128)(2,1)} %get-tuple-element.148), channel_id=1, source_target_pairs={{0,4},{4,0},{8,12},{12,8},{16,20},{20,16},{24,28},{28,24},{1,5},{5... | collective-permute-start | bytes 1511432 | tf_op jit(solution)/shard_map/gmlp0_d1/ppermute | solution.py:57
  146.8 14.2 %collective-permute-start.28 = (bf16[256,1024]{1,0:T(8,128)(2,1)S(1)}, bf16[256,1024]{1,0:T(8,128)(2,1)S(1)}, u32[]{:S(2)}, u32[]{:S(2)}) collective-permute-start(bf16[256,1024]{1,0:T(8,128)(2,1)S(1)} %copy-done.48), channel_id=1, source_target_pairs={{0,1},{1,0},{2,3},{3,2},{4,5},{5,4},{6,7},{7,6},{8,9},{9,8},{10,11... | collective-permute-start | bytes 1572872 | tf_op jit(solution)/shard_map/lofar_t1/ppermute | solution.py:57
  147.0 14.4 %collective-permute-start.27 = (bf16[256,1024]{1,0:T(8,128)(2,1)}, bf16[256,1024]{1,0:T(8,128)(2,1)S(1)}, u32[]{:S(2)}, u32[]{:S(2)}) collective-permute-start(bf16[256,1024]{1,0:T(8,128)(2,1)} %get-tuple-element.139), channel_id=1, source_target_pairs={{0,1},{1,0},{2,3},{3,2},{4,5},{5,4},{6,7},{7,6},{8,9},{9,8},{10,11... | collective-permute-start | bytes 1572872 | tf_op jit(solution)/shard_map/lonear_t1/ppermute | solution.py:57
  152.4 17.0 %collective-permute-start.32 = (bf16[256,1024]{1,0:T(8,128)(2,1)}, bf16[256,1024]{1,0:T(8,128)(2,1)S(1)}, u32[]{:S(2)}, u32[]{:S(2)}) collective-permute-start(bf16[256,1024]{1,0:T(8,128)(2,1)} %get-tuple-element.159.refs_5_), channel_id=1, source_target_pairs={{0,2},{1,3},{2,0},{3,1},{4,6},{5,7},{6,4},{7,5},{8,10},{9,11},{10,... | collective-permute-start | bytes 1572872 | tf_op jit(solution)/shard_map/aog_t2/ppermute | solution.py:57
  161.3 14.0 %collective-permute-start.31 = (bf16[256,1024]{1,0:T(8,128)(2,1)S(1)}, bf16[256,1024]{1,0:T(8,128)(2,1)S(1)}, u32[]{:S(2)}, u32[]{:S(2)}) collective-permute-start(bf16[256,1024]{1,0:T(8,128)(2,1)S(1)} %copy-done.28), channel_id=1, source_target_pairs={{0,1},{1,0},{2,3},{3,2},{4,5},{5,4},{6,7},{7,6},{8,9},{9,8},{10,11... | collective-permute-start | bytes 1572872 | tf_op jit(solution)/shard_map/aog_t1/ppermute | solution.py:57
  169.4 36.2 %collective-permute-start.36 = (bf16[3,656,128]{2,1,0:T(8,128)(2,1)}, bf16[3,656,128]{2,1,0:T(8,128)(2,1)S(1)}, u32[]{:S(2)}, u32[]{:S(2)}) collective-permute-start(bf16[3,656,128]{2,1,0:T(8,128)(2,1)} %get-tuple-element.182), channel_id=1, source_target_pairs={{0,4},{4,0},{8,12},{12,8},{16,20},{20,16},{24,28},{28,24},{1,5},{5... | collective-permute-start | bytes 1511432 | tf_op jit(solution)/shard_map/gmlp2_d1/ppermute | solution.py:57
  173.2 32.4 %collective-permute-start.37 = (bf16[3,656,128]{2,1,0:T(8,128)(2,1)S(1)}, bf16[3,656,128]{2,1,0:T(8,128)(2,1)S(1)}, u32[]{:S(2)}, u32[]{:S(2)}) collective-permute-start(bf16[3,656,128]{2,1,0:T(8,128)(2,1)S(1)} %add_convert_fusion.5), channel_id=1, source_target_pairs={{0,8},{4,12},{8,0},{12,4},{16,24},{20,28},{24,16},{28,20},{1,9},{5... | collective-permute-start | bytes 1511432 | tf_op jit(solution)/shard_map/gmlpz1_d2/ppermute | solution.py:57
  175.0 30.9 %collective-permute-start.38 = (bf16[3,656,128]{2,1,0:T(8,128)(2,1)S(1)}, bf16[3,656,128]{2,1,0:T(8,128)(2,1)S(1)}, u32[]{:S(2)}, u32[]{:S(2)}) collective-permute-start(bf16[3,656,128]{2,1,0:T(8,128)(2,1)S(1)} %add_convert_fusion.6), channel_id=1, source_target_pairs={{0,8},{4,12},{8,0},{12,4},{16,24},{20,28},{24,16},{28,20},{1,9},{5... | collective-permute-start | bytes 1511432 | tf_op jit(solution)/shard_map/gmlpz0_d2/ppermute | solution.py:57
  175.3 30.6 %collective-permute-start.39 = (bf16[3,656,128]{2,1,0:T(8,128)(2,1)S(1)}, bf16[3,656,128]{2,1,0:T(8,128)(2,1)S(1)}, u32[]{:S(2)}, u32[]{:S(2)}) collective-permute-start(bf16[3,656,128]{2,1,0:T(8,128)(2,1)S(1)} %copy-done.50), channel_id=1, source_target_pairs={{0,4},{4,0},{8,12},{12,8},{16,20},{20,16},{24,28},{28,24},{1,5},{5... | collective-permute-start | bytes 1511432 | tf_op jit(solution)/shard_map/gmlp3_d1/ppermute | solution.py:57
  207.3 14.1 %collective-permute-start.49 = (bf16[4,128,256]{2,1,0:T(8,128)(2,1)S(1)}, bf16[4,128,256]{2,1,0:T(8,128)(2,1)S(1)}, u32[]{:S(2)}, u32[]{:S(2)}) collective-permute-start(bf16[4,128,256]{2,1,0:T(8,128)(2,1)S(1)} %copy-done.54), channel_id=1, source_target_pairs={{0,4},{4,0},{8,12},{12,8},{16,20},{20,16},{24,28},{28,24},{1,5},{5... | collective-permute-start | bytes 786440 | tf_op jit(solution)/shard_map/gqkv0_d1/ppermute | solution.py:57
  208.7 26.9 %collective-permute-start.43 = (bf16[3,656,128]{2,1,0:T(8,128)(2,1)S(1)}, bf16[3,656,128]{2,1,0:T(8,128)(2,1)S(1)}, u32[]{:S(2)}, u32[]{:S(2)}) collective-permute-start(bf16[3,656,128]{2,1,0:T(8,128)(2,1)S(1)} %add_convert_fusion.4), channel_id=1, source_target_pairs={{0,16},{4,20},{8,24},{12,28},{16,0},{20,4},{24,8},{28,12},{1,17},{... | collective-permute-start | bytes 1511432 | tf_op jit(solution)/shard_map/gmlp_d4/ppermute | solution.py:57
  213.1 23.0 %collective-permute-start.51 = (bf16[4,128,256]{2,1,0:T(8,128)(2,1)S(1)}, bf16[4,128,256]{2,1,0:T(8,128)(2,1)S(1)}, u32[]{:S(2)}, u32[]{:S(2)}) collective-permute-start(bf16[4,128,256]{2,1,0:T(8,128)(2,1)S(1)} %copy-done.53), channel_id=1, source_target_pairs={{0,4},{4,0},{8,12},{12,8},{16,20},{20,16},{24,28},{28,24},{1,5},{5... | collective-permute-start | bytes 786440 | tf_op jit(solution)/shard_map/gqkv2_d1/ppermute | solution.py:57
  216.7 26.2 %collective-permute-start.41 = (bf16[272,1024]{1,0:T(8,128)(2,1)}, bf16[272,1024]{1,0:T(8,128)(2,1)S(1)}, u32[]{:S(2)}, u32[]{:S(2)}) collective-permute-start(bf16[272,1024]{1,0:T(8,128)(2,1)} %get-tuple-element.186), channel_id=1, source_target_pairs={{0,2},{1,3},{2,0},{3,1},{4,6},{5,7},{6,4},{7,5},{8,10},{9,11},{10,... | collective-permute-start | bytes 1671176 | tf_op jit(solution)/shard_map/nfar_t2/ppermute | solution.py:57
  217.9 25.0 %collective-permute-start.44 = (bf16[256,1024]{1,0:T(8,128)(2,1)S(1)}, bf16[256,1024]{1,0:T(8,128)(2,1)S(1)}, u32[]{:S(2)}, u32[]{:S(2)}) collective-permute-start(bf16[256,1024]{1,0:T(8,128)(2,1)S(1)} %copy-done.49), channel_id=1, source_target_pairs={{0,1},{1,0},{2,3},{3,2},{4,5},{5,4},{6,7},{7,6},{8,9},{9,8},{10,11... | collective-permute-start | bytes 1572872 | tf_op jit(solution)/shard_map/nnear_t1/ppermute | solution.py:57
  221.4 18.6 %collective-permute-start.53 = (bf16[4,128,256]{2,1,0:T(8,128)(2,1)S(1)}, bf16[4,128,256]{2,1,0:T(8,128)(2,1)S(1)}, u32[]{:S(2)}, u32[]{:S(2)}) collective-permute-start(bf16[4,128,256]{2,1,0:T(8,128)(2,1)S(1)} %add_convert_fusion.8), channel_id=1, source_target_pairs={{0,8},{4,12},{8,0},{12,4},{16,24},{20,28},{24,16},{28,20},{1,9},{5... | collective-permute-start | bytes 786440 | tf_op jit(solution)/shard_map/gqkvz1_d2/ppermute | solution.py:57
  235.5 26.0 %collective-permute-start.50 = (bf16[4,128,256]{2,1,0:T(8,128)(2,1)S(1)}, bf16[4,128,256]{2,1,0:T(8,128)(2,1)S(1)}, u32[]{:S(2)}, u32[]{:S(2)}) collective-permute-start(bf16[4,128,256]{2,1,0:T(8,128)(2,1)S(1)} %add_convert_fusion.9), channel_id=1, source_target_pairs={{0,8},{4,12},{8,0},{12,4},{16,24},{20,28},{24,16},{28,20},{1,9},{5... | collective-permute-start | bytes 786440 | tf_op jit(solution)/shard_map/gqkvz0_d2/ppermute | solution.py:57
  240.1 20.9 %collective-permute-start.54 = (bf16[4,128,256]{2,1,0:T(8,128)(2,1)S(1)}, bf16[4,128,256]{2,1,0:T(8,128)(2,1)S(1)}, u32[]{:S(2)}, u32[]{:S(2)}) collective-permute-start(bf16[4,128,256]{2,1,0:T(8,128)(2,1)S(1)} %add_convert_fusion.7), channel_id=1, source_target_pairs={{0,16},{4,20},{8,24},{12,28},{16,0},{20,4},{24,8},{28,12},{1,17},{... | collective-permute-start | bytes 786440 | tf_op jit(solution)/shard_map/gqkv_d4/ppermute | solution.py:57
  (79 other events, 720.1 us)

commit v2 on v1

--- a/solution.py
+++ b/solution.py
@@ -88,12 +88,14 @@
 
 
 def angles_at(table, block, rows):
-    both = table[pl.ds(pl.multiple_of(block * rows, rows), rows), :]
-    other = pltpu.roll(both, 64, 1)
+    both = table[pl.ds(pl.multiple_of((block & 1) * rows, rows), rows), :]
+    here = jnp.where(block < 2, both, pltpu.roll(both, 64, 1))
+    a, b, c = [pltpu.roll(here, shift, 1) for shift in (32, 64, 96)]
     lane = lax.broadcasted_iota(jnp.int32, both.shape, 1)
-    cos = jnp.where(lane < 64, both, other)
-    sin = jnp.where(lane < 64, other, both)
-    return cos, jnp.where((lane & 63) < 32, -sin, sin)
+    even = (lane & 63) < 32
+    cos = jnp.where(lane < 64, jnp.where(even, here, a), jnp.where(even, b, c))
+    sin = jnp.where(lane < 64, jnp.where(even, -c, here), jnp.where(even, -a, b))
+    return cos, sin
 
 
 def turn(u, cos, sin):
@@ -221,7 +223,7 @@
         gug[1, :, at] = g1.T
         return carry
 
-    lax.fori_loop(0, count, one_block, 0)
+    lax.fori_loop(0, count, one_block, 0, unroll=True)
 
 
 def load_mlp(pieces, offs, size, w, sem):
@@ -361,7 +363,7 @@
         dot_rows[:, at] = mm(ones, hi, NT) + mm(ones, lo, NT)
         return carry
 
-    lax.fori_loop(0, 4, output_grads, 0)
+    lax.fori_loop(0, 4, output_grads, 0, unroll=2)
     dq[...] = jnp.zeros_like(dq)
     factor = scale * LOG2E
     nil = jnp.zeros((), BF)
@@ -418,7 +420,7 @@
             block_sums[block, 1, j] = part[128:]
         return carry
 
-    lax.fori_loop(0, 4, weight_grads, 0)
+    lax.fori_loop(0, 4, weight_grads, 0, unroll=True)
     stores = stop_blocks(block_sums, outs, sem, 0)
 
     def row_grads(i, sums):
@@ -427,7 +429,7 @@
         sent[at, :] = total.astype(BF)
         return sums + jnp.sum(total * n[at, :].astype(F32), axis=0, keepdims=True)
 
-    sums = lax.fori_loop(0, 4, row_grads, jnp.zeros((1, n.shape[1]), F32))
+    sums = lax.fori_loop(0, 4, row_grads, jnp.zeros((1, n.shape[1]), F32), unroll=2)
     sums = sums / gain[...]
     both = [sums[:, 128 * i : 128 * i + 128] for i in range(8)] + [gain_two[...]]
     gain_ref[...] = write_gains(sent, length, jnp.concatenate(both, axis=0))
@@ -458,10 +460,8 @@
     gains_ref[...] = write_gains(o_ref, rows, gains[...] + read_gains(got, rows))
 
 
-def input_back(h, mg, gain, sa, sb, sc, gains, o_ref, gains_ref):
-    rows = sa.shape[0]
-    gains_ref[...] = gains[...] + read_gains(sc, rows)
-    got = sa[...].astype(F32) + sb[...].astype(F32) + sc[pl.ds(0, rows), :].astype(F32)
+def input_back(h, mg, gain, sa, sb, sc, o_ref):
+    got = sa[...].astype(F32) + sb[...].astype(F32) + sc[pl.ds(0, sa.shape[0]), :].astype(F32)
     back, _ = norm_back(h[...].astype(F32), gain[...] * got)
     o_ref[...] = mg[...] + back
 
@@ -475,7 +475,8 @@
     inverse = np.float32(ROPE_BASE) ** (-exponents)
     angles = np.arange(length).astype(np.float32)[:, None] * inverse[None, :]
     cos, sin = np.cos(angles), np.sin(angles)
-    return np.concatenate([cos, cos, sin, sin], axis=1).astype(np.float32)
+    half = length // 2
+    return np.concatenate([cos[:half], sin[:half], cos[half:], sin[half:]], axis=1).astype(np.float32)
 
 
 def shards(sizes, *args):
@@ -502,7 +503,8 @@
         if direct:
             far = depth(shard, 4, label)
             along = [shard, depth(shard, 2, label), far, depth(far, 2, label + "far")]
-            across = [depth(v, 1, f"{label}{i}") for i, v in enumerate(along)]
+            across = [depth(v, 1, f"{label}{i}") for i, v in enumerate(along[:3])]
+            across.append(depth(gate(along[3:], across[1:2])[0], 1, label + "3"))
             return [v for pair in zip(along, across) for v in pair]
         return [lax.all_gather(shard, "dp", axis=axis, tiled=True)]
 
@@ -558,7 +560,7 @@
     table = jnp.asarray(angle_table(length))
     if direct:
         (mlp_along,) = gate([mlp_shard], [qkvo[6]])
-        (mlp_across,) = gate([mlp_shard], [qkvo[7]])
+        (mlp_across,) = gate([mlp_shard], [qkvo[5], qkvo[7]])
         z2, z1 = [depth(mlp_along, 2 * k, "mlp") for k in (2, 1)]
         (cotangent_there,) = gate([cotangent], [normed_attn[2]])
     else:
@@ -571,24 +573,24 @@
     *parts, mixed, q, k, v, lse = call(
         body(attend_forward, n_pieces, piece, scale),
         scalar(offs, mine_one)
-        + away(normed_attn)
+        + away(gate(normed_attn, [z1]) if direct else normed_attn)
         + away([table] + qkvo),
         [hb((rows, model))] * 4 + [hb((length, width))] * 4 + [vm((8, length), F32)],
-        [buf(4, rows, model), buf(length, 128, dtype=F32), buf(4, model, width)]
+        [buf(4, rows, model), buf(length // 2, 128, dtype=F32), buf(4, model, width)]
         + [buf(length, width)] * 4
         + [buf(length, model), sems(n_pieces), sems(13)],
         name="attend_forward",
     )
     if direct:
-        y0 = depth(mlp_across, 1, "mlp0")
-        *parts, lse = gate(parts + [lse], [z1, z2, y0])
+        y0, y1 = depth(mlp_across, 1, "mlp0"), depth(gate([z1], [qkvo[5], qkvo[7]])[0], 1, "mlp1")
+        *parts, lse = gate(parts + [lse], [z2, y0, y1, cot[2]])
     attn_far = add(parts[2], tensor(parts[3], 1, "afar"))
     attn_near = tensor(parts[1], 1, "anear")
     attn_got = tensor(attn_far, 2, "afar")
     if direct:
         z3 = depth(gate([z2], [lse])[0], 2, "mlpfar")
-        y1, y2, y3 = [depth(gate([x], [lse])[0], 1, f"mlp{i}") for i, x in ((1, z1), (2, z2), (3, z3))]
-        before = [y1, z3]
+        y2, y3 = [depth(gate([x], [lse])[0], 1, f"mlp{i}") for i, x in ((2, z2), (3, z3))]
+        before = [y2, z3]
         mlp = [mlp_shard, y0, z1, y1, z2, y2, z3, y3]
     middle, normed_two = call(
         middle_rows,
@@ -670,7 +672,7 @@
         + [hb((rows + 16, model)), vm((16, 128), F32)],
         [buf(length, 3 * width)]
         + [buf(length, width)] * 5
-        + [buf(8, length, dtype=F32), buf(length, 128, dtype=F32), buf(length, model), buf(length, model)]
+        + [buf(8, length, dtype=F32), buf(length // 2, 128, dtype=F32), buf(length, model), buf(length, model)]
         + [buf(8, length, dtype=F32), buf(length, width, dtype=F32)]
         + [buf(4, model, width), buf(4, 2, 4, 128, width), buf(length + 16, model)]
         + [sems(n_pieces), sems(17)],
@@ -692,12 +694,14 @@
     got_far = tensor(sent_far, 2, "nfar")
     (b1,) = gate([b1], [sent_far])
     near_sum = tensor(b1, 1, "nnear")
-    if direct:
-        (b0,) = gate([b0], [last])
-    input_grad, gains = call(
+    gains = gains + (got_far[rows:, 0:128].astype(F32) + got_far[rows:, 128:256].astype(F32))
+    if direct:
+        gains = gains + depth(gains, 1, "gain")
+        (b0,) = gate([b0], [last, gains])
+    (input_grad,) = call(
         input_back,
-        near(hidden_in, middle_grad, gain_one, b0, near_sum, got_far, gains),
-        [vm((rows, model), F32), vm((16, 128), F32)],
+        near(hidden_in, middle_grad, gain_one, b0, near_sum, got_far),
+        [vm((rows, model), F32)],
         name="input_back",
     )
     out_far = tensor(gate([out_sum], [got_far])[0], 2, "lofar")
@@ -705,25 +709,28 @@
     layer_out = (middle + (out_near + out_far.astype(F32))).astype(BF)
 
     if direct:
-        (attn[6],) = gate(attn[6:7], [input_grad])
-        gains = gains + depth(gains, 1, "gain")
+        (attn[6],) = gate(attn[6:7], [got_far])
         gains = gains + depth(gains, 2, "gain")
         gains = gains + depth(gains, 4, "gain")
         gqkv.append(depth(attn[6], 1, "gqkv3"))
         qkv_late = sum_of(attn[5], gqkv[2], qkv_back[1]).astype(BF)
         qkv_last = depth(qkv_late, 4, "gqkv")
-        attn_total = sum_of(attn[7], gqkv[3], qkv_back[0], gate([qkv_last], [out_far, gains])[0])
+        ends = [attn[7], gqkv[3], qkv_back[0], gate([qkv_last], [out_far, gains])[0]]
+        qkv_shard = sum_of(*[x[0:3] for x in ends])
+        out_shard = sum_of(*[x[3] for x in ends]).T
     else:
         gains = lax.psum(gains, "dp")
         attn_total = reduce(attn, 1, "gqkv")
-    qkv_shard, out_shard = attn_total[0:3], attn_total[3].T
+        qkv_shard, out_shard = attn_total[0:3], attn_total[3].T
     gains = gains.reshape(2, model)
 
     if direct:
-        mlp_total = sum_of(grads[7], got[3], back[0], gate([last], [input_grad])[0])
+        ends = [grads[7], got[3], back[0], gate([last], [input_grad])[0]]
+        in_shard = sum_of(*[x[0:2] for x in ends]).transpose(0, 2, 1)
+        down_shard = sum_of(*[x[2] for x in ends])
     else:
         mlp_total = reduce(grads, 2, "gmlp")
-    in_shard, down_shard = mlp_total[0:2].transpose(0, 2, 1), mlp_total[2]
+        in_shard, down_shard = mlp_total[0:2].transpose(0, 2, 1), mlp_total[2]
 
     return (layer_out, input_grad, gains[0], qkv_shard, out_shard, gains[1], in_shard, down_shard)
 

time: 265 us -> 251 us (0.947)
  waiting for transfers between devices: 90.4 us -> 80.5 us
  other arithmetic: 5.4 us -> 11.6 us
  starting transfers between devices: 59 us -> 53.7 us
    ppermute x55, waiting for transfers between devices: 90.4 us -> 80.5 us  [swap(): return lax.ppermute(value, axis, [(i, i ^ distance) for i in range(size)])]
    ppermute x55, starting transfers between devices: 59 us -> 53.7 us  [swap(): return lax.ppermute(value, axis, [(i, i ^ distance) for i in range(size)])]
    add x2, other arithmetic: 0.4 us -> 3.68 us  [sum_of(): return sum((v.astype(F32) for v in values))]
    transpose x0 -> x2, other arithmetic: none -> 2.96 us  [the longest x1 2.02 us: shards(): in_shard = sum_of(*[x[0:2] for x in ends]).transpose(0, 2, 1)]
    unnamed x113 -> x105, local copies, waits for them, and re-layouts: 8.63 us -> 8.45 us
  transfers between devices with their start and end apart: 55 -> 55, of which waited for: 26 -> 22; matrix products, arithmetic and copies ran while one was open for 3% -> 4% of each run, Pallas kernels for 31% -> 31%
where the time goes in v2:
time: 251 us
  Pallas kernels  94.1 us (37%)
  waiting for transfers between devices  80.5 us (32%)
  starting transfers between devices  53.7 us (21%)
  other arithmetic  11.6 us (5%)
  local copies, waits for them, and re-layouts  9.71 us (4%)
    pallas_call x11, Pallas kernels, call(): pl.pallas_call(body, out_shape=[jax.ShapeDtypeStruct(o[0], o[1]) for o in...  94.1 us
    ppermute x55, waiting for transfers between devices, swap(): return lax.ppermute(value, axis, [(i, i ^ distance) for i in range(size)])  80.5 us
    ppermute x55, starting transfers between devices, swap(): return lax.ppermute(value, axis, [(i, i ^ distance) for i in range(size)])  53.7 us
    unnamed x105, local copies, waits for them, and re-layouts  8.45 us
  transfers between devices with their start and end apart: 55, of which 22 were waited for; matrix products, arithmetic and copies ran while one was open for 4% of the time, Pallas kernels for 31%

profile of v2, /device:TPU:0, one launch (start us, length us, event | category | flops | bytes accessed | tf_op | source)
XLA Modules:
  0.0 250.8 jit_solution(10248054347789727582)
XLA Ops:
  0.6 2.1 pack.1
  2.8 4.0 %collective-permute-start.2 = (bf16[4,128,256]{2,1,0:T(8,128)(2,1)}, bf16[4,128,256]{2,1,0:T(8,128)(2,1)S(1)}, u32[]{:S(2)}, u32[]{:S(2)}) collective-permute-start(bf16[4,128,256]{2,1,0:T(8,128)(2,1)} %get-tuple-element.110.refs_7_.refs_19_), channel_id=1, source_target_pairs={{0,16},{4,20},{8,24},{12,28},{16,0},{20,4},{24,8},{28,12},{1,17},{... | collective-permute-start | bytes 786440 | tf_op jit(solution)/shard_map/qkvo_d4/ppermute | solution.py:57
  9.9 9.1 %collective-permute-done.2.refs_11_.refs_23_ = bf16[4,128,256]{2,1,0:T(8,128)(2,1)S(1)} collective-permute-done((bf16[4,128,256]{2,1,0:T(8,128)(2,1)}, bf16[4,128,256]{2,1,0:T(8,128)(2,1)S(1)}, u32[]{:S(2)}, u32[]{:S(2)}) %collective-permute-start.2) | collective-permute-done | bytes 262176 | tf_op jit(solution)/shard_map/qkvo_d4/ppermute | solution.py:57
  19.8 2.2 norm.1.refs_2_.refs_15_
  29.5 3.3 %collective-permute-done.8.refs_10_.refs_22_ = bf16[4,128,256]{2,1,0:T(8,128)(2,1)S(1)} collective-permute-done((bf16[4,128,256]{2,1,0:T(8,128)(2,1)S(1)}, bf16[4,128,256]{2,1,0:T(8,128)(2,1)S(1)}, u32[]{:S(2)}, u32[]{:S(2)}) %collective-permute-start.8) | collective-permute-done | bytes 262176 | tf_op jit(solution)/shard_map/qkvo1_d1/ppermute | solution.py:57
  35.8 2.6 %collective-permute-done.9.refs_12_.refs_24_ = bf16[4,128,256]{2,1,0:T(8,128)(2,1)S(1)} collective-permute-done((bf16[4,128,256]{2,1,0:T(8,128)(2,1)S(1)}, bf16[4,128,256]{2,1,0:T(8,128)(2,1)S(1)}, u32[]{:S(2)}, u32[]{:S(2)}) %collective-permute-start.9) | collective-permute-done | bytes 262176 | tf_op jit(solution)/shard_map/qkvo2_d1/ppermute | solution.py:57
  38.7 3.7 %collective-permute-done.10.refs_14_.refs_26_ = bf16[4,128,256]{2,1,0:T(8,128)(2,1)S(1)} collective-permute-done((bf16[4,128,256]{2,1,0:T(8,128)(2,1)S(1)}, bf16[4,128,256]{2,1,0:T(8,128)(2,1)S(1)}, u32[]{:S(2)}, u32[]{:S(2)}) %collective-permute-start.10) | collective-permute-done | bytes 262176 | tf_op jit(solution)/shard_map/qkvo3_d1/ppermute | solution.py:57
  42.4 3.3 %collective-permute-start.11 = (bf16[3,656,128]{2,1,0:T(8,128)(2,1)}, bf16[3,656,128]{2,1,0:T(8,128)(2,1)}, u32[]{:S(2)}, u32[]{:S(2)}) collective-permute-start(bf16[3,656,128]{2,1,0:T(8,128)(2,1)} %get-tuple-element.124.refs_5_.refs_12_), channel_id=1, source_target_pairs={{0,16},{4,20},{8,24},{12,28},{16,0},{20,4},{24,8},{28,12},{1,17},{... | collective-permute-start | bytes 1511432 | tf_op jit(solution)/shard_map/mlp_d4/ppermute | solution.py:57
  49.1 14.7 %attend_forward.1 = (bf16[256,1024]{1,0:T(8,128)(2,1)}, bf16[256,1024]{1,0:T(8,128)(2,1)}, bf16[256,1024]{1,0:T(8,128)(2,1)}, bf16[256,1024]{1,0:T(8,128)(2,1)},...) custom-call(s32[8]{0:T(128)} %iota_xor_fusion.refs_0_.refs_2_, ...), custom_call_target="tpu_custom_call" | custom-call | flops 1000 | bytes 1000 | tf_op jit(solution)/shard_map/attend_forward/pallas_call | solution.py:43
  63.9 3.1 %collective-permute-done.11.refs_9_.refs_16_ = bf16[3,656,128]{2,1,0:T(8,128)(2,1)} collective-permute-done((bf16[3,656,128]{2,1,0:T(8,128)(2,1)}, bf16[3,656,128]{2,1,0:T(8,128)(2,1)}, u32[]{:S(2)}, u32[]{:S(2)}) %collective-permute-start.11) | collective-permute-done | bytes 503840 | tf_op jit(solution)/shard_map/mlp_d4/ppermute | solution.py:57
  74.6 11.5 %collective-permute-done.16.refs_11_.refs_18_ = bf16[3,656,128]{2,1,0:T(8,128)(2,1)S(1)} collective-permute-done((bf16[3,656,128]{2,1,0:T(8,128)(2,1)}, bf16[3,656,128]{2,1,0:T(8,128)(2,1)S(1)}, u32[]{:S(2)}, u32[]{:S(2)}) %collective-permute-start.16) | collective-permute-done | bytes 503840 | tf_op jit(solution)/shard_map/mlpfar_d2/ppermute | solution.py:57
  87.3 3.0 %middle_rows.1 = (f32[256,1024]{1,0:T(8,128)}, bf16[256,1024]{1,0:T(8,128)(2,1)}) custom-call(bf16[256,1024]{1,0:T(8,128)(2,1)} %h.1, f32[1,1024]{1,0:T(1,128)} %bitcast.28, bf16[256,1024]{1,0:T(8,128)(2,1)} %get-tuple-element.130.a, bf16[256,1024]{1,0:T(8,128)(2,1)} %copy-done.28, bf16[256,1024]{1,0:T(8,128)(2,1)} %copy-done.29), custom_call_target="tpu_custom_call" | custom-call | flops 1000 | bytes 1000 | tf_op jit(solution)/shard_map/middle_rows/pallas_call | solution.py:43
  93.3 10.3 %collective-permute-done.22.refs_12_.refs_19_ = bf16[3,656,128]{2,1,0:T(8,128)(2,1)S(1)} collective-permute-done((bf16[3,656,128]{2,1,0:T(8,128)(2,1)S(1)}, bf16[3,656,128]{2,1,0:T(8,128)(2,1)S(1)}, u32[]{:S(2)}, u32[]{:S(2)}) %collective-permute-start.22) | collective-permute-done | bytes 503840 | tf_op jit(solution)/shard_map/mlp3_d1/ppermute | solution.py:57
  103.7 1.9 collective-permute-done.23.refs_2_.refs_5_.refs_4_
  106.4 11.3 %feed_far.1 = (bf16[256,1024]{1,0:T(8,128)(2,1)}, bf16[256,1024]{1,0:T(8,128)(2,1)}, bf16[256,1024]{1,0:T(8,128)(2,1)}, bf16[256,1024]{1,0:T(8,128)(2,1)}, bf16[...) custom-call(s32[8]{0:T(128)} %iota_xor_fusion.refs_0_.refs_2_, bf16[256,1024]{1,0:T(8,128)(2,1)} %copy-done.1, ...), custom_call_target="tpu_custom_call" | custom-call | flops 1000 | bytes 1000 | tf_op jit(solution)/shard_map/feed_far/pallas_call | solution.py:43
  123.7 15.4 %feed_near.1 = (bf16[256,1024]{1,0:T(8,128)(2,1)}, bf16[256,1024]{1,0:T(8,128)(2,1)}, bf16[256,1024]{1,0:T(8,128)(2,1)}, bf16[256,1024]{1,0:T(8,128)(2,1)}, bf16...) custom-call(s32[8]{0:T(128)} %iota_xor_fusion.refs_0_.refs_2_, ...), custom_call_target="tpu_custom_call" | custom-call | flops 1000 | bytes 1000 | tf_op jit(solution)/shard_map/feed_near/pallas_call | solution.py:43
  142.2 4.0 %middle_back.1 = (f32[256,1024]{1,0:T(8,128)}, bf16[256,1024]{1,0:T(8,128)(2,1)}, f32[8,128]{1,0:T(8,128)}) custom-call(f32[256,1024]{1,0:T(8,128)} %get-tuple-element.134.mid, bf16[256,1024]{1,0:T(8,128)(2,1)} %refs_5_, f32[1,1024]{1,0:T(1,128)} %bitcast.29, bf16[256,1024]{1,0:T(8,128)(2,1)} %get-tuple-element.150.sa, bf16[256,1024]{1,0:T(8,128)(2,1)} %copy-done.30, ...), custom_call_target="tpu_custom_call" | custom-call | flops 1000 | bytes 1000 | tf_op jit(solution)/shard_map/middle_back/pallas_call | solution.py:43
  147.3 6.1 %collective-permute-done.34 = bf16[3,656,128]{2,1,0:T(8,128)(2,1)S(1)} collective-permute-done((bf16[3,656,128]{2,1,0:T(8,128)(2,1)}, bf16[3,656,128]{2,1,0:T(8,128)(2,1)S(1)}, u32[]{:S(2)}, u32[]{:S(2)}) %collective-permute-start.34) | collective-permute-done | bytes 503840 | tf_op jit(solution)/shard_map/gmlp0_d1/ppermute | solution.py:57
  155.4 8.0 %feed_late.1 = (bf16[3,656,128]{2,1,0:T(8,128)(2,1)}, bf16[3,656,128]{2,1,0:T(8,128)(2,1)}, bf16[3,656,128]{2,1,0:T(8,128)(2,1)}, bf16[3,656,128]{2,1,0:T(8,128)(2,1)}) custom-call(s32[8]{0:T(128)} %stack.35.refs_1_.refs_0_, bf16[256,1024]{1,0:T(8,128)(2,1)} %get-tuple-element.157.refs_2_.refs_1_, bf16[256,1024]{1,0:T(8,128)(2,1)} %copy-done.11, ...), custom_call_target="tpu_custom_call" | custom-call | flops 1000 | bytes 1000 | tf_op jit(solution)/shard_map/feed_late/pallas_call | solution.py:43
  164.3 2.3 collective-permute-done.35
  168.8 2.2 collective-permute-start.39
  171.9 27.5 %attend_backward.1 = (bf16[4,128,256]{2,1,0:T(8,128)(2,1)}, bf16[4,128,256]{2,1,0:T(8,128)(2,1)}, bf16[4,128,256]{2,1,0:T(8,128)(2,1)}, bf16[4,128,256]{2,1,0:T(...) custom-call(s32[8]{0:T(128)} %stack.35.refs_1_.refs_0_, ...), custom_call_target="tpu_custom_call" | custom-call | flops 1000 | bytes 1000 | tf_op jit(solution)/shard_map/attend_backward/pallas_call | solution.py:43
  203.2 2.2 add_far.1
  210.6 5.1 %collective-permute-done.49 = bf16[4,128,256]{2,1,0:T(8,128)(2,1)S(1)} collective-permute-done((bf16[4,128,256]{2,1,0:T(8,128)(2,1)S(1)}, bf16[4,128,256]{2,1,0:T(8,128)(2,1)S(1)}, u32[]{:S(2)}, u32[]{:S(2)}) %collective-permute-start.49) | collective-permute-done | bytes 262176 | tf_op jit(solution)/shard_map/gqkv0_d1/ppermute | solution.py:57
  215.8 4.5 %collective-permute-done.41.sc = bf16[272,1024]{1,0:T(8,128)(2,1)S(1)} collective-permute-done((bf16[272,1024]{1,0:T(8,128)(2,1)}, bf16[272,1024]{1,0:T(8,128)(2,1)S(1)}, u32[]{:S(2)}, u32[]{:S(2)}) %collective-permute-start.41) | collective-permute-done | bytes 557088 | tf_op jit(solution)/shard_map/nfar_t2/ppermute | solution.py:57
  221.8 3.7 %collective-permute-done.53 = bf16[4,128,256]{2,1,0:T(8,128)(2,1)S(1)} collective-permute-done((bf16[4,128,256]{2,1,0:T(8,128)(2,1)S(1)}, bf16[4,128,256]{2,1,0:T(8,128)(2,1)S(1)}, u32[]{:S(2)}, u32[]{:S(2)}) %collective-permute-start.53) | collective-permute-done | bytes 262176 | tf_op jit(solution)/shard_map/gqkvz1_d2/ppermute | solution.py:57
  225.6 3.5 %collective-permute-start.54 = (bf16[4,128,256]{2,1,0:T(8,128)(2,1)S(1)}, bf16[4,128,256]{2,1,0:T(8,128)(2,1)}, u32[]{:S(2)}, u32[]{:S(2)}) collective-permute-start(bf16[4,128,256]{2,1,0:T(8,128)(2,1)S(1)} %add_convert_fusion.7), channel_id=1, source_target_pairs={{0,16},{4,20},{8,24},{12,28},{16,0},{20,4},{24,8},{28,12},{1,17},{... | collective-permute-start | bytes 786440 | tf_op jit(solution)/shard_map/gqkv_d4/ppermute | solution.py:57
  229.1 1.9 collective-permute-start.48
  231.0 2.4 collective-permute-done.43
  235.0 3.7 %input_back.1 = f32[256,1024]{1,0:T(8,128)} custom-call(bf16[256,1024]{1,0:T(8,128)(2,1)} %h.1, f32[256,1024]{1,0:T(8,128)} %get-tuple-element.196.mg, f32[1,1024]{1,0:T(1,128)} %bitcast.27, bf16[256,1024]{1,0:T(8,128)(2,1)} %get-tuple-element.198.sa, bf16[256,1024]{1,0:T(8,128)(2,1)} %copy-done.25, bf16[272,1024]{1,0:T(8,128)(2,1)} %copy-done.22), custom_call_target="tpu_custom_call" | custom-call | flops 1000 | bytes 1000 | tf_op jit(solution)/shard_map/input_back/pallas_call | solution.py:43
  238.7 2.0 add_bitcast_fusion
  247.7 2.0 convert_add_fusion
  (215 shorter events, 67.3 us)
Async XLA Ops:
  2.8 16.3 %collective-permute-start.2 = (bf16[4,128,256]{2,1,0:T(8,128)(2,1)}, bf16[4,128,256]{2,1,0:T(8,128)(2,1)S(1)}, u32[]{:S(2)}, u32[]{:S(2)}) collective-permute-start(bf16[4,128,256]{2,1,0:T(8,128)(2,1)} %get-tuple-element.110.refs_7_.refs_19_), channel_id=1, source_target_pairs={{0,16},{4,20},{8,24},{12,28},{16,0},{20,4},{24,8},{28,12},{1,17},{... | collective-permute-start | bytes 786440 | tf_op jit(solution)/shard_map/qkvo_d4/ppermute | solution.py:57
  6.8 15.2 %collective-permute-start.1 = (bf16[4,128,256]{2,1,0:T(8,128)(2,1)}, bf16[4,128,256]{2,1,0:T(8,128)(2,1)S(1)}, u32[]{:S(2)}, u32[]{:S(2)}) collective-permute-start(bf16[4,128,256]{2,1,0:T(8,128)(2,1)} %get-tuple-element.110.refs_7_.refs_19_), channel_id=1, source_target_pairs={{0,8},{4,12},{8,0},{12,4},{16,24},{20,28},{24,16},{28,20},{1,9},{5... | collective-permute-start | bytes 786440 | tf_op jit(solution)/shard_map/qkvo_d2/ppermute | solution.py:57
  8.4 13.6 %collective-permute-start = (bf16[4,128,256]{2,1,0:T(8,128)(2,1)}, bf16[4,128,256]{2,1,0:T(8,128)(2,1)}, u32[]{:S(2)}, u32[]{:S(2)}) collective-permute-start(bf16[4,128,256]{2,1,0:T(8,128)(2,1)} %get-tuple-element.110.refs_7_.refs_19_), channel_id=1, source_target_pairs={{0,4},{4,0},{8,12},{12,8},{16,20},{20,16},{24,28},{28,24},{1,5},{5... | collective-permute-start | bytes 786440 | tf_op jit(solution)/shard_map/qkvo0_d1/ppermute | solution.py:57
  22.0 13.8 %collective-permute-start.4 = (bf16[256,1024]{1,0:T(8,128)(2,1)}, bf16[256,1024]{1,0:T(8,128)(2,1)S(1)}, u32[]{:S(2)}, u32[]{:S(2)}) collective-permute-start(bf16[256,1024]{1,0:T(8,128)(2,1)} %norm.1.refs_2_.refs_15_), channel_id=1, source_target_pairs={{0,2},{1,3},{2,0},{3,1},{4,6},{5,7},{6,4},{7,5},{8,10},{9,11},{10,... | collective-permute-start | bytes 1572872 | tf_op jit(solution)/shard_map/norm_t2/ppermute | solution.py:57
  25.0 22.2 %collective-permute-start.3 = (bf16[256,1024]{1,0:T(8,128)(2,1)}, bf16[256,1024]{1,0:T(8,128)(2,1)S(1)}, u32[]{:S(2)}, u32[]{:S(2)}) collective-permute-start(bf16[256,1024]{1,0:T(8,128)(2,1)} %norm.1.refs_2_.refs_15_), channel_id=1, source_target_pairs={{0,1},{1,0},{2,3},{3,2},{4,5},{5,4},{6,7},{7,6},{8,9},{9,8},{10,11... | collective-permute-start | bytes 1572872 | tf_op jit(solution)/shard_map/norm_t1/ppermute | solution.py:57
  26.5 19.2 %collective-permute-start.7 = (bf16[3,656,128]{2,1,0:T(8,128)(2,1)}, bf16[3,656,128]{2,1,0:T(8,128)(2,1)S(1)}, u32[]{:S(2)}, u32[]{:S(2)}) collective-permute-start(bf16[3,656,128]{2,1,0:T(8,128)(2,1)} %get-tuple-element.124.refs_5_.refs_12_), channel_id=1, source_target_pairs={{0,8},{4,12},{8,0},{12,4},{16,24},{20,28},{24,16},{28,20},{1,9},{5... | collective-permute-start | bytes 1511432 | tf_op jit(solution)/shard_map/mlp_d2/ppermute | solution.py:57
  38.4 28.6 %collective-permute-start.14 = (bf16[256,1024]{1,0:T(8,128)(2,1)S(1)}, bf16[256,1024]{1,0:T(8,128)(2,1)S(1)}, u32[]{:S(2)}, u32[]{:S(2)}) collective-permute-start(bf16[256,1024]{1,0:T(8,128)(2,1)S(1)} %copy-done.4), channel_id=1, source_target_pairs={{0,2},{1,3},{2,0},{3,1},{4,6},{5,7},{6,4},{7,5},{8,10},{9,11},{10,... | collective-permute-start | bytes 1572872 | tf_op jit(solution)/shard_map/cot_t2/ppermute | solution.py:57
  42.4 24.6 %collective-permute-start.11 = (bf16[3,656,128]{2,1,0:T(8,128)(2,1)}, bf16[3,656,128]{2,1,0:T(8,128)(2,1)}, u32[]{:S(2)}, u32[]{:S(2)}) collective-permute-start(bf16[3,656,128]{2,1,0:T(8,128)(2,1)} %get-tuple-element.124.refs_5_.refs_12_), channel_id=1, source_target_pairs={{0,16},{4,20},{8,24},{12,28},{16,0},{20,4},{24,8},{28,12},{1,17},{... | collective-permute-start | bytes 1511432 | tf_op jit(solution)/shard_map/mlp_d4/ppermute | solution.py:57
  45.7 21.3 %collective-permute-start.12 = (bf16[3,656,128]{2,1,0:T(8,128)(2,1)}, bf16[3,656,128]{2,1,0:T(8,128)(2,1)}, u32[]{:S(2)}, u32[]{:S(2)}) collective-permute-start(bf16[3,656,128]{2,1,0:T(8,128)(2,1)} %get-tuple-element.124.refs_5_.refs_12_), channel_id=1, source_target_pairs={{0,4},{4,0},{8,12},{12,8},{16,20},{20,16},{24,28},{28,24},{1,5},{5... | collective-permute-start | bytes 1511432 | tf_op jit(solution)/shard_map/mlp0_d1/ppermute | solution.py:57
  47.2 21.2 %collective-permute-start.13 = (bf16[3,656,128]{2,1,0:T(8,128)(2,1)S(1)}, bf16[3,656,128]{2,1,0:T(8,128)(2,1)}, u32[]{:S(2)}, u32[]{:S(2)}) collective-permute-start(bf16[3,656,128]{2,1,0:T(8,128)(2,1)S(1)} %collective-permute-done.7.refs_7_.refs_14_), channel_id=1, source_target_pairs={{0,4},{4,0},{8,12},{12,8},{16,20},{20,16},{24,28},{28,24},{1,5},{5... | collective-permute-start | bytes 1511432 | tf_op jit(solution)/shard_map/mlp1_d1/ppermute | solution.py:57
  68.5 17.8 %collective-permute-start.17 = (bf16[256,1024]{1,0:T(8,128)(2,1)}, bf16[256,1024]{1,0:T(8,128)(2,1)S(1)}, u32[]{:S(2)}, u32[]{:S(2)}) collective-permute-start(bf16[256,1024]{1,0:T(8,128)(2,1)} %get-tuple-element.131), channel_id=1, source_target_pairs={{0,1},{1,0},{2,3},{3,2},{4,5},{5,4},{6,7},{7,6},{8,9},{9,8},{10,11... | collective-permute-start | bytes 1572872 | tf_op jit(solution)/shard_map/anear_t1/ppermute | solution.py:57
  71.8 14.5 %collective-permute-start.19 = (bf16[256,1024]{1,0:T(8,128)(2,1)S(1)}, bf16[256,1024]{1,0:T(8,128)(2,1)S(1)}, u32[]{:S(2)}, u32[]{:S(2)}) collective-permute-start(bf16[256,1024]{1,0:T(8,128)(2,1)S(1)} %add_convert_fusion.3), channel_id=1, source_target_pairs={{0,2},{1,3},{2,0},{3,1},{4,6},{5,7},{6,4},{7,5},{8,10},{9,11},{10,... | collective-permute-start | bytes 1572872 | tf_op jit(solution)/shard_map/afar_t2/ppermute | solution.py:57
  72.6 13.5 %collective-permute-start.16 = (bf16[3,656,128]{2,1,0:T(8,128)(2,1)}, bf16[3,656,128]{2,1,0:T(8,128)(2,1)S(1)}, u32[]{:S(2)}, u32[]{:S(2)}) collective-permute-start(bf16[3,656,128]{2,1,0:T(8,128)(2,1)} %collective-permute-done.11.refs_9_.refs_16_), channel_id=1, source_target_pairs={{0,8},{4,12},{8,0},{12,4},{16,24},{20,28},{24,16},{28,20},{1,9},{5... | collective-permute-start | bytes 1511432 | tf_op jit(solution)/shard_map/mlpfar_d2/ppermute | solution.py:57
  90.2 13.4 %collective-permute-start.21 = (bf16[256,1024]{1,0:T(8,128)(2,1)}, bf16[256,1024]{1,0:T(8,128)(2,1)S(1)}, u32[]{:S(2)}, u32[]{:S(2)}) collective-permute-start(bf16[256,1024]{1,0:T(8,128)(2,1)} %get-tuple-element.157.refs_2_.refs_1_), channel_id=1, source_target_pairs={{0,2},{1,3},{2,0},{3,1},{4,6},{5,7},{6,4},{7,5},{8,10},{9,11},{10,... | collective-permute-start | bytes 1572872 | tf_op jit(solution)/shard_map/norm2_t2/ppermute | solution.py:57
  121.1 18.1 %collective-permute-start.30 = (bf16[256,1024]{1,0:T(8,128)(2,1)S(1)}, bf16[256,1024]{1,0:T(8,128)(2,1)S(1)}, u32[]{:S(2)}, u32[]{:S(2)}) collective-permute-start(bf16[256,1024]{1,0:T(8,128)(2,1)S(1)} %add_convert_fusion.2), channel_id=1, source_target_pairs={{0,2},{1,3},{2,0},{3,1},{4,6},{5,7},{6,4},{7,5},{8,10},{9,11},{10,... | collective-permute-start | bytes 1572872 | tf_op jit(solution)/shard_map/far_t2/ppermute | solution.py:57
  139.3 14.1 %collective-permute-start.34 = (bf16[3,656,128]{2,1,0:T(8,128)(2,1)}, bf16[3,656,128]{2,1,0:T(8,128)(2,1)S(1)}, u32[]{:S(2)}, u32[]{:S(2)}) collective-permute-start(bf16[3,656,128]{2,1,0:T(8,128)(2,1)} %get-tuple-element.156), channel_id=1, source_target_pairs={{0,4},{4,0},{8,12},{12,8},{16,20},{20,16},{24,28},{28,24},{1,5},{5... | collective-permute-start | bytes 1511432 | tf_op jit(solution)/shard_map/gmlp0_d1/ppermute | solution.py:57
  140.9 14.2 %collective-permute-start.28 = (bf16[256,1024]{1,0:T(8,128)(2,1)S(1)}, bf16[256,1024]{1,0:T(8,128)(2,1)S(1)}, u32[]{:S(2)}, u32[]{:S(2)}) collective-permute-start(bf16[256,1024]{1,0:T(8,128)(2,1)S(1)} %copy-done.45), channel_id=1, source_target_pairs={{0,1},{1,0},{2,3},{3,2},{4,5},{5,4},{6,7},{7,6},{8,9},{9,8},{10,11... | collective-permute-start | bytes 1572872 | tf_op jit(solution)/shard_map/lofar_t1/ppermute | solution.py:57
  141.0 14.4 %collective-permute-start.27 = (bf16[256,1024]{1,0:T(8,128)(2,1)}, bf16[256,1024]{1,0:T(8,128)(2,1)S(1)}, u32[]{:S(2)}, u32[]{:S(2)}) collective-permute-start(bf16[256,1024]{1,0:T(8,128)(2,1)} %get-tuple-element.147), channel_id=1, source_target_pairs={{0,1},{1,0},{2,3},{3,2},{4,5},{5,4},{6,7},{7,6},{8,9},{9,8},{10,11... | collective-permute-start | bytes 1572872 | tf_op jit(solution)/shard_map/lonear_t1/ppermute | solution.py:57
  146.2 17.3 %collective-permute-start.32 = (bf16[256,1024]{1,0:T(8,128)(2,1)}, bf16[256,1024]{1,0:T(8,128)(2,1)S(1)}, u32[]{:S(2)}, u32[]{:S(2)}) collective-permute-start(bf16[256,1024]{1,0:T(8,128)(2,1)} %get-tuple-element.167.refs_5_), channel_id=1, source_target_pairs={{0,2},{1,3},{2,0},{3,1},{4,6},{5,7},{6,4},{7,5},{8,10},{9,11},{10,... | collective-permute-start | bytes 1572872 | tf_op jit(solution)/shard_map/aog_t2/ppermute | solution.py:57
  155.3 13.5 %collective-permute-start.31 = (bf16[256,1024]{1,0:T(8,128)(2,1)S(1)}, bf16[256,1024]{1,0:T(8,128)(2,1)S(1)}, u32[]{:S(2)}, u32[]{:S(2)}) collective-permute-start(bf16[256,1024]{1,0:T(8,128)(2,1)S(1)} %copy-done.31), channel_id=1, source_target_pairs={{0,1},{1,0},{2,3},{3,2},{4,5},{5,4},{6,7},{7,6},{8,9},{9,8},{10,11... | collective-permute-start | bytes 1572872 | tf_op jit(solution)/shard_map/aog_t1/ppermute | solution.py:57
  163.5 36.0 %collective-permute-start.36 = (bf16[3,656,128]{2,1,0:T(8,128)(2,1)}, bf16[3,656,128]{2,1,0:T(8,128)(2,1)S(1)}, u32[]{:S(2)}, u32[]{:S(2)}) collective-permute-start(bf16[3,656,128]{2,1,0:T(8,128)(2,1)} %get-tuple-element.190), channel_id=1, source_target_pairs={{0,4},{4,0},{8,12},{12,8},{16,20},{20,16},{24,28},{28,24},{1,5},{5... | collective-permute-start | bytes 1511432 | tf_op jit(solution)/shard_map/gmlp2_d1/ppermute | solution.py:57
  166.7 32.7 %collective-permute-start.37 = (bf16[3,656,128]{2,1,0:T(8,128)(2,1)S(1)}, bf16[3,656,128]{2,1,0:T(8,128)(2,1)S(1)}, u32[]{:S(2)}, u32[]{:S(2)}) collective-permute-start(bf16[3,656,128]{2,1,0:T(8,128)(2,1)S(1)} %add_convert_fusion.5), channel_id=1, source_target_pairs={{0,8},{4,12},{8,0},{12,4},{16,24},{20,28},{24,16},{28,20},{1,9},{5... | collective-permute-start | bytes 1511432 | tf_op jit(solution)/shard_map/gmlpz1_d2/ppermute | solution.py:57
  168.0 31.7 %collective-permute-start.38 = (bf16[3,656,128]{2,1,0:T(8,128)(2,1)S(1)}, bf16[3,656,128]{2,1,0:T(8,128)(2,1)S(1)}, u32[]{:S(2)}, u32[]{:S(2)}) collective-permute-start(bf16[3,656,128]{2,1,0:T(8,128)(2,1)S(1)} %add_convert_fusion.6), channel_id=1, source_target_pairs={{0,8},{4,12},{8,0},{12,4},{16,24},{20,28},{24,16},{28,20},{1,9},{5... | collective-permute-start | bytes 1511432 | tf_op jit(solution)/shard_map/gmlpz0_d2/ppermute | solution.py:57
  168.8 30.9 %collective-permute-start.39 = (bf16[3,656,128]{2,1,0:T(8,128)(2,1)}, bf16[3,656,128]{2,1,0:T(8,128)(2,1)}, u32[]{:S(2)}, u32[]{:S(2)}) collective-permute-start(bf16[3,656,128]{2,1,0:T(8,128)(2,1)} %get-tuple-element.191), channel_id=1, source_target_pairs={{0,4},{4,0},{8,12},{12,8},{16,20},{20,16},{24,28},{28,24},{1,5},{5... | collective-permute-start | bytes 1511432 | tf_op jit(solution)/shard_map/gmlp3_d1/ppermute | solution.py:57
  205.4 14.9 %collective-permute-start.41 = (bf16[272,1024]{1,0:T(8,128)(2,1)}, bf16[272,1024]{1,0:T(8,128)(2,1)S(1)}, u32[]{:S(2)}, u32[]{:S(2)}) collective-permute-start(bf16[272,1024]{1,0:T(8,128)(2,1)} %get-tuple-element.194), channel_id=1, source_target_pairs={{0,2},{1,3},{2,0},{3,1},{4,6},{5,7},{6,4},{7,5},{8,10},{9,11},{10,... | collective-permute-start | bytes 1671176 | tf_op jit(solution)/shard_map/nfar_t2/ppermute | solution.py:57
  206.7 26.6 %collective-permute-start.43 = (bf16[3,656,128]{2,1,0:T(8,128)(2,1)S(1)}, bf16[3,656,128]{2,1,0:T(8,128)(2,1)S(1)}, u32[]{:S(2)}, u32[]{:S(2)}) collective-permute-start(bf16[3,656,128]{2,1,0:T(8,128)(2,1)S(1)} %add_convert_fusion.4), channel_id=1, source_target_pairs={{0,16},{4,20},{8,24},{12,28},{16,0},{20,4},{24,8},{28,12},{1,17},{... | collective-permute-start | bytes 1511432 | tf_op jit(solution)/shard_map/gmlp_d4/ppermute | solution.py:57
  207.9 13.6 %collective-permute-start.51 = (bf16[4,128,256]{2,1,0:T(8,128)(2,1)S(1)}, bf16[4,128,256]{2,1,0:T(8,128)(2,1)S(1)}, u32[]{:S(2)}, u32[]{:S(2)}) collective-permute-start(bf16[4,128,256]{2,1,0:T(8,128)(2,1)S(1)} %copy-done.49), channel_id=1, source_target_pairs={{0,4},{4,0},{8,12},{12,8},{16,20},{20,16},{24,28},{28,24},{1,5},{5... | collective-permute-start | bytes 786440 | tf_op jit(solution)/shard_map/gqkv2_d1/ppermute | solution.py:57
  209.9 15.6 %collective-permute-start.53 = (bf16[4,128,256]{2,1,0:T(8,128)(2,1)S(1)}, bf16[4,128,256]{2,1,0:T(8,128)(2,1)S(1)}, u32[]{:S(2)}, u32[]{:S(2)}) collective-permute-start(bf16[4,128,256]{2,1,0:T(8,128)(2,1)S(1)} %add_convert_fusion.8), channel_id=1, source_target_pairs={{0,8},{4,12},{8,0},{12,4},{16,24},{20,28},{24,16},{28,20},{1,9},{5... | collective-permute-start | bytes 786440 | tf_op jit(solution)/shard_map/gqkvz1_d2/ppermute | solution.py:57
  215.7 18.5 %collective-permute-start.45 = (bf16[256,1024]{1,0:T(8,128)(2,1)S(1)}, bf16[256,1024]{1,0:T(8,128)(2,1)S(1)}, u32[]{:S(2)}, u32[]{:S(2)}) collective-permute-start(bf16[256,1024]{1,0:T(8,128)(2,1)S(1)} %copy-done.46), channel_id=1, source_target_pairs={{0,1},{1,0},{2,3},{3,2},{4,5},{5,4},{6,7},{7,6},{8,9},{9,8},{10,11... | collective-permute-start | bytes 1572872 | tf_op jit(solution)/shard_map/nnear_t1/ppermute | solution.py:57
  220.3 25.7 %collective-permute-start.50 = (bf16[4,128,256]{2,1,0:T(8,128)(2,1)S(1)}, bf16[4,128,256]{2,1,0:T(8,128)(2,1)}, u32[]{:S(2)}, u32[]{:S(2)}) collective-permute-start(bf16[4,128,256]{2,1,0:T(8,128)(2,1)S(1)} %add_convert_fusion.9), channel_id=1, source_target_pairs={{0,8},{4,12},{8,0},{12,4},{16,24},{20,28},{24,16},{28,20},{1,9},{5... | collective-permute-start | bytes 786440 | tf_op jit(solution)/shard_map/gqkvz0_d2/ppermute | solution.py:57
  225.6 20.4 %collective-permute-start.54 = (bf16[4,128,256]{2,1,0:T(8,128)(2,1)S(1)}, bf16[4,128,256]{2,1,0:T(8,128)(2,1)}, u32[]{:S(2)}, u32[]{:S(2)}) collective-permute-start(bf16[4,128,256]{2,1,0:T(8,128)(2,1)S(1)} %add_convert_fusion.7), channel_id=1, source_target_pairs={{0,16},{4,20},{8,24},{12,28},{16,0},{20,4},{24,8},{28,12},{1,17},{... | collective-permute-start | bytes 786440 | tf_op jit(solution)/shard_map/gqkv_d4/ppermute | solution.py:57
  229.1 16.9 %collective-permute-start.48 = (bf16[4,128,256]{2,1,0:T(8,128)(2,1)S(1)}, bf16[4,128,256]{2,1,0:T(8,128)(2,1)}, u32[]{:S(2)}, u32[]{:S(2)}) collective-permute-start(bf16[4,128,256]{2,1,0:T(8,128)(2,1)S(1)} %copy-done.48), channel_id=1, source_target_pairs={{0,4},{4,0},{8,12},{12,8},{16,20},{20,16},{24,28},{28,24},{1,5},{5... | collective-permute-start | bytes 786440 | tf_op jit(solution)/shard_map/gqkv3_d1/ppermute | solution.py:57
  (75 other events, 718.3 us)

commit v3 on v2

--- a/solution.py
+++ b/solution.py
@@ -16,7 +16,7 @@
 F32 = jnp.float32
 LOG2E = math.log2(math.e)
 COST = 1000
-VMEM_MIB = 56
+VMEM_MIB = 32
 
 NN = (((1,), (0,)), ((), ()))
 NT = (((1,), (1,)), ((), ()))
@@ -223,7 +223,7 @@
         gug[1, :, at] = g1.T
         return carry
 
-    lax.fori_loop(0, count, one_block, 0, unroll=True)
+    lax.fori_loop(0, count, one_block, 0)
 
 
 def load_mlp(pieces, offs, size, w, sem):

time: 251 us -> 242 us (0.964)
  Pallas kernels: 94.1 us -> 69.1 us
  local copies, waits for them, and re-layouts: 9.71 us -> 30.4 us
  other arithmetic: 11.6 us -> 7.8 us
  waiting for transfers between devices: 80.5 us -> 77 us
    pallas_call x11, Pallas kernels: 94.1 us -> 69.1 us  [call(): pl.pallas_call(body, out_shape=[jax.ShapeDtypeStruct(o[0], o[1]) for o in...]
    unnamed x105 -> x155, local copies, waits for them, and re-layouts: 8.45 us -> 29.7 us
    ppermute x55, waiting for transfers between devices: 80.5 us -> 77 us  [swap(): return lax.ppermute(value, axis, [(i, i ^ distance) for i in range(size)])]
  transfers between devices with their start and end apart: 55 -> 55, of which waited for: 22 -> 25; matrix products, arithmetic and copies ran while one was open for 4% -> 2% of each run, Pallas kernels for 31% -> 24%
where the time goes in v3:
time: 242 us; the launch traced here: 241 us
  waiting for transfers between devices  77 us (32%)
  Pallas kernels  69.1 us (29%)
  starting transfers between devices  55.1 us (23%)
  local copies, waits for them, and re-layouts  30.4 us (13%)
  other arithmetic  7.8 us (3%)
    ppermute x55, waiting for transfers between devices, swap(): return lax.ppermute(value, axis, [(i, i ^ distance) for i in range(size)])  77 us
    pallas_call x11, Pallas kernels, call(): pl.pallas_call(body, out_shape=[jax.ShapeDtypeStruct(o[0], o[1]) for o in...  69.1 us
    ppermute x55, starting transfers between devices, swap(): return lax.ppermute(value, axis, [(i, i ^ distance) for i in range(size)])  55.1 us
    unnamed x155, local copies, waits for them, and re-layouts  29.7 us
  transfers between devices with their start and end apart: 55, of which 25 were waited for; matrix products, arithmetic and copies ran while one was open for 2% of the time, Pallas kernels for 24%

profile of v3, /device:TPU:0, one launch (start us, length us, event | category | flops | bytes accessed | tf_op | source)
XLA Modules:
  0.0 240.8 jit_solution(80004497022846489)
XLA Ops:
  4.4 4.1 %collective-permute-start.2 = (bf16[4,128,256]{2,1,0:T(8,128)(2,1)S(1)}, bf16[4,128,256]{2,1,0:T(8,128)(2,1)S(1)}, u32[]{:S(2)}, u32[]{:S(2)}) collective-permute-start(bf16[4,128,256]{2,1,0:T(8,128)(2,1)S(1)} %get-tuple-element.110.refs_7_.refs_19_), channel_id=1, source_target_pairs={{0,16},{4,20},{8,24},{12,28},{16,0},{20,4},{24,8},{28,12},{1,17},{... | collective-permute-start | bytes 786440 | tf_op jit(solution)/shard_map/qkvo_d4/ppermute | solution.py:57
  8.5 1.6 collective-permute-start.1
  11.6 8.9 %collective-permute-done.2.refs_11_.refs_23_ = bf16[4,128,256]{2,1,0:T(8,128)(2,1)S(1)} collective-permute-done((bf16[4,128,256]{2,1,0:T(8,128)(2,1)S(1)}, bf16[4,128,256]{2,1,0:T(8,128)(2,1)S(1)}, u32[]{:S(2)}, u32[]{:S(2)}) %collective-permute-start.2) | collective-permute-done | bytes 262176 | tf_op jit(solution)/shard_map/qkvo_d4/ppermute | solution.py:57
  30.9 3.4 %collective-permute-done.8.refs_10_.refs_22_ = bf16[4,128,256]{2,1,0:T(8,128)(2,1)S(1)} collective-permute-done((bf16[4,128,256]{2,1,0:T(8,128)(2,1)S(1)}, bf16[4,128,256]{2,1,0:T(8,128)(2,1)S(1)}, u32[]{:S(2)}, u32[]{:S(2)}) %collective-permute-start.8) | collective-permute-done | bytes 262176 | tf_op jit(solution)/shard_map/qkvo1_d1/ppermute | solution.py:57
  35.1 2.0 collective-permute-start.10
  37.8 2.2 collective-permute-done.9.refs_12_.refs_24_
  41.2 3.3 %collective-permute-done.10.refs_14_.refs_26_ = bf16[4,128,256]{2,1,0:T(8,128)(2,1)S(1)} collective-permute-done((bf16[4,128,256]{2,1,0:T(8,128)(2,1)S(1)}, bf16[4,128,256]{2,1,0:T(8,128)(2,1)S(1)}, u32[]{:S(2)}, u32[]{:S(2)}) %collective-permute-start.10) | collective-permute-done | bytes 262176 | tf_op jit(solution)/shard_map/qkvo3_d1/ppermute | solution.py:57
  45.2 3.4 %collective-permute-start.11 = (bf16[3,656,128]{2,1,0:T(8,128)(2,1)S(1)}, bf16[3,656,128]{2,1,0:T(8,128)(2,1)}, u32[]{:S(2)}, u32[]{:S(2)}) collective-permute-start(bf16[3,656,128]{2,1,0:T(8,128)(2,1)S(1)} %get-tuple-element.124.refs_5_.refs_12_), channel_id=1, source_target_pairs={{0,16},{4,20},{8,24},{12,28},{16,0},{20,4},{24,8},{28,12},{1,17},{... | collective-permute-start | bytes 1511432 | tf_op jit(solution)/shard_map/mlp_d4/ppermute | solution.py:57
  48.6 1.5 collective-permute-start.12
  58.4 10.9 %attend_forward.1 = (bf16[256,1024]{1,0:T(8,128)(2,1)S(1)}, bf16[256,1024]{1,0:T(8,128)(2,1)S(1)}, bf16[256,1024]{1,0:T(8,128)(2,1)S(1)}, bf16[256,1024]{1,0:T(8...) custom-call(s32[8]{0:T(128)S(1)} %iota_xor_fusion.refs_0_.refs_2_, ...), custom_call_target="tpu_custom_call" | custom-call | flops 1000 | bytes 1000 | tf_op jit(solution)/shard_map/attend_forward/pallas_call | solution.py:43
  76.2 11.3 %collective-permute-done.16.refs_11_.refs_18_ = bf16[3,656,128]{2,1,0:T(8,128)(2,1)S(1)} collective-permute-done((bf16[3,656,128]{2,1,0:T(8,128)(2,1)}, bf16[3,656,128]{2,1,0:T(8,128)(2,1)S(1)}, u32[]{:S(2)}, u32[]{:S(2)}) %collective-permute-start.16) | collective-permute-done | bytes 503840 | tf_op jit(solution)/shard_map/mlpfar_d2/ppermute | solution.py:57
  93.1 10.6 %collective-permute-done.22.refs_12_.refs_19_ = bf16[3,656,128]{2,1,0:T(8,128)(2,1)S(1)} collective-permute-done((bf16[3,656,128]{2,1,0:T(8,128)(2,1)S(1)}, bf16[3,656,128]{2,1,0:T(8,128)(2,1)S(1)}, u32[]{:S(2)}, u32[]{:S(2)}) %collective-permute-start.22) | collective-permute-done | bytes 503840 | tf_op jit(solution)/shard_map/mlp3_d1/ppermute | solution.py:57
  103.7 1.9 collective-permute-done.23.refs_2_.refs_5_.refs_4_
  105.6 8.8 %feed_far.1 = (bf16[256,1024]{1,0:T(8,128)(2,1)S(1)}, bf16[256,1024]{1,0:T(8,128)(2,1)S(1)}, bf16[256,1024]{1,0:T(8,128)(2,1)S(1)}, bf16[256,1024]{1,0:T(8,128)(...) custom-call(s32[8]{0:T(128)S(1)} %iota_xor_fusion.refs_0_.refs_2_, ...), custom_call_target="tpu_custom_call" | custom-call | flops 1000 | bytes 1000 | tf_op jit(solution)/shard_map/feed_far/pallas_call | solution.py:43
  126.4 13.4 %feed_near.1 = (bf16[256,1024]{1,0:T(8,128)(2,1)S(1)}, bf16[256,1024]{1,0:T(8,128)(2,1)S(1)}, bf16[256,1024]{1,0:T(8,128)(2,1)S(1)}, bf16[256,1024]{1,0:T(8,128)...) custom-call(s32[8]{0:T(128)S(1)} %iota_xor_fusion.refs_0_.refs_2_, ...), custom_call_target="tpu_custom_call" | custom-call | flops 1000 | bytes 1000 | tf_op jit(solution)/shard_map/feed_near/pallas_call | solution.py:43
  141.8 2.1 middle_back.1
  145.1 8.7 %collective-permute-done.34 = bf16[3,656,128]{2,1,0:T(8,128)(2,1)S(1)} collective-permute-done((bf16[3,656,128]{2,1,0:T(8,128)(2,1)S(1)}, bf16[3,656,128]{2,1,0:T(8,128)(2,1)S(1)}, u32[]{:S(2)}, u32[]{:S(2)}) %collective-permute-start.34) | collective-permute-done | bytes 503840 | tf_op jit(solution)/shard_map/gmlp0_d1/ppermute | solution.py:57
  156.4 7.0 %feed_late.1 = (bf16[3,656,128]{2,1,0:T(8,128)(2,1)S(1)}, bf16[3,656,128]{2,1,0:T(8,128)(2,1)S(1)}, bf16[3,656,128]{2,1,0:T(8,128)(2,1)S(1)}, bf16[3,656,128]{2,1,0:T(8,128)(2,1)S(1)}) custom-call(s32[8]{0:T(128)S(1)} %stack.35.refs_1_.refs_0_, bf16[256,1024]{1,0:T(8,128)(2,1)} %get-tuple-element.157.refs_2_.refs_1_, ...), custom_call_target="tpu_custom_call" | custom-call | flops 1000 | bytes 1000 | tf_op jit(solution)/shard_map/feed_late/pallas_call | solution.py:43
  164.6 2.8 %collective-permute-done.35 = bf16[3,656,128]{2,1,0:T(8,128)(2,1)S(1)} collective-permute-done((bf16[3,656,128]{2,1,0:T(8,128)(2,1)S(1)}, bf16[3,656,128]{2,1,0:T(8,128)(2,1)S(1)}, u32[]{:S(2)}, u32[]{:S(2)}) %collective-permute-start.35) | collective-permute-done | bytes 503840 | tf_op jit(solution)/shard_map/gmlp1_d1/ppermute | solution.py:57
  171.2 23.1 %attend_backward.1 = (bf16[4,128,256]{2,1,0:T(8,128)(2,1)S(1)}, bf16[4,128,256]{2,1,0:T(8,128)(2,1)S(1)}, bf16[4,128,256]{2,1,0:T(8,128)(2,1)S(1)}, bf16[4,128,2...) custom-call(s32[8]{0:T(128)S(1)} %stack.35.refs_1_.refs_0_, ...), custom_call_target="tpu_custom_call" | custom-call | flops 1000 | bytes 1000 | tf_op jit(solution)/shard_map/attend_backward/pallas_call | solution.py:43
  201.2 2.6 %collective-permute-done.52 = bf16[4,128,256]{2,1,0:T(8,128)(2,1)S(1)} collective-permute-done((bf16[4,128,256]{2,1,0:T(8,128)(2,1)S(1)}, bf16[4,128,256]{2,1,0:T(8,128)(2,1)S(1)}, u32[]{:S(2)}, u32[]{:S(2)}) %collective-permute-start.52) | collective-permute-done | bytes 262176 | tf_op jit(solution)/shard_map/gqkv1_d1/ppermute | solution.py:57
  203.9 1.8 collective-permute-start.53
  205.6 3.8 %collective-permute-done.49 = bf16[4,128,256]{2,1,0:T(8,128)(2,1)S(1)} collective-permute-done((bf16[4,128,256]{2,1,0:T(8,128)(2,1)S(1)}, bf16[4,128,256]{2,1,0:T(8,128)(2,1)S(1)}, u32[]{:S(2)}, u32[]{:S(2)}) %collective-permute-start.49) | collective-permute-done | bytes 262176 | tf_op jit(solution)/shard_map/gqkv0_d1/ppermute | solution.py:57
  209.5 1.9 collective-permute-done.41.sc
  211.4 1.7 collective-permute-start.50
  215.2 2.1 collective-permute-done.53
  217.4 3.4 %collective-permute-start.54 = (bf16[4,128,256]{2,1,0:T(8,128)(2,1)S(1)}, bf16[4,128,256]{2,1,0:T(8,128)(2,1)}, u32[]{:S(2)}, u32[]{:S(2)}) collective-permute-start(bf16[4,128,256]{2,1,0:T(8,128)(2,1)S(1)} %add_convert_fusion.7), channel_id=1, source_target_pairs={{0,16},{4,20},{8,24},{12,28},{16,0},{20,4},{24,8},{28,12},{1,17},{... | collective-permute-start | bytes 786440 | tf_op jit(solution)/shard_map/gqkv_d4/ppermute | solution.py:57
  220.8 1.9 collective-permute-start.48
  222.7 2.4 collective-permute-done.43
  226.0 1.9 input_back.1
  231.8 2.9 %collective-permute-done.47 = f32[16,128]{1,0:T(8,128)S(1)} collective-permute-done((f32[16,128]{1,0:T(8,128)S(1)}, f32[16,128]{1,0:T(8,128)S(1)}, u32[]{:S(2)}, u32[]{:S(2)}) %collective-permute-start.47) | collective-permute-done | bytes 8224 | tf_op jit(solution)/shard_map/gain_d4/ppermute | solution.py:57
  237.8 1.9 convert_add_fusion
  (265 shorter events, 80.1 us)
Async XLA Ops:
  4.4 16.1 %collective-permute-start.2 = (bf16[4,128,256]{2,1,0:T(8,128)(2,1)S(1)}, bf16[4,128,256]{2,1,0:T(8,128)(2,1)S(1)}, u32[]{:S(2)}, u32[]{:S(2)}) collective-permute-start(bf16[4,128,256]{2,1,0:T(8,128)(2,1)S(1)} %get-tuple-element.110.refs_7_.refs_19_), channel_id=1, source_target_pairs={{0,16},{4,20},{8,24},{12,28},{16,0},{20,4},{24,8},{28,12},{1,17},{... | collective-permute-start | bytes 786440 | tf_op jit(solution)/shard_map/qkvo_d4/ppermute | solution.py:57
  8.5 14.8 %collective-permute-start.1 = (bf16[4,128,256]{2,1,0:T(8,128)(2,1)S(1)}, bf16[4,128,256]{2,1,0:T(8,128)(2,1)S(1)}, u32[]{:S(2)}, u32[]{:S(2)}) collective-permute-start(bf16[4,128,256]{2,1,0:T(8,128)(2,1)S(1)} %get-tuple-element.110.refs_7_.refs_19_), channel_id=1, source_target_pairs={{0,8},{4,12},{8,0},{12,4},{16,24},{20,28},{24,16},{28,20},{1,9},{5... | collective-permute-start | bytes 786440 | tf_op jit(solution)/shard_map/qkvo_d2/ppermute | solution.py:57
  24.1 13.7 %collective-permute-start.4 = (bf16[256,1024]{1,0:T(8,128)(2,1)S(1)}, bf16[256,1024]{1,0:T(8,128)(2,1)S(1)}, u32[]{:S(2)}, u32[]{:S(2)}) collective-permute-start(bf16[256,1024]{1,0:T(8,128)(2,1)S(1)} %norm.1.refs_2_.refs_15_), channel_id=1, source_target_pairs={{0,2},{1,3},{2,0},{3,1},{4,6},{5,7},{6,4},{7,5},{8,10},{9,11},{10,... | collective-permute-start | bytes 1572872 | tf_op jit(solution)/shard_map/norm_t2/ppermute | solution.py:57
  27.8 22.3 %collective-permute-start.3 = (bf16[256,1024]{1,0:T(8,128)(2,1)S(1)}, bf16[256,1024]{1,0:T(8,128)(2,1)S(1)}, u32[]{:S(2)}, u32[]{:S(2)}) collective-permute-start(bf16[256,1024]{1,0:T(8,128)(2,1)S(1)} %norm.1.refs_2_.refs_15_), channel_id=1, source_target_pairs={{0,1},{1,0},{2,3},{3,2},{4,5},{5,4},{6,7},{7,6},{8,9},{9,8},{10,11... | collective-permute-start | bytes 1572872 | tf_op jit(solution)/shard_map/norm_t1/ppermute | solution.py:57
  28.0 20.6 %collective-permute-start.7 = (bf16[3,656,128]{2,1,0:T(8,128)(2,1)S(1)}, bf16[3,656,128]{2,1,0:T(8,128)(2,1)}, u32[]{:S(2)}, u32[]{:S(2)}) collective-permute-start(bf16[3,656,128]{2,1,0:T(8,128)(2,1)S(1)} %get-tuple-element.124.refs_5_.refs_12_), channel_id=1, source_target_pairs={{0,8},{4,12},{8,0},{12,4},{16,24},{20,28},{24,16},{28,20},{1,9},{5... | collective-permute-start | bytes 1511432 | tf_op jit(solution)/shard_map/mlp_d2/ppermute | solution.py:57
  40.7 30.3 %collective-permute-start.14 = (bf16[256,1024]{1,0:T(8,128)(2,1)}, bf16[256,1024]{1,0:T(8,128)(2,1)S(1)}, u32[]{:S(2)}, u32[]{:S(2)}) collective-permute-start(bf16[256,1024]{1,0:T(8,128)(2,1)} %refs_5_), channel_id=1, source_target_pairs={{0,2},{1,3},{2,0},{3,1},{4,6},{5,7},{6,4},{7,5},{8,10},{9,11},{10,... | collective-permute-start | bytes 1572872 | tf_op jit(solution)/shard_map/cot_t2/ppermute | solution.py:57
  45.2 25.8 %collective-permute-start.11 = (bf16[3,656,128]{2,1,0:T(8,128)(2,1)S(1)}, bf16[3,656,128]{2,1,0:T(8,128)(2,1)}, u32[]{:S(2)}, u32[]{:S(2)}) collective-permute-start(bf16[3,656,128]{2,1,0:T(8,128)(2,1)S(1)} %get-tuple-element.124.refs_5_.refs_12_), channel_id=1, source_target_pairs={{0,16},{4,20},{8,24},{12,28},{16,0},{20,4},{24,8},{28,12},{1,17},{... | collective-permute-start | bytes 1511432 | tf_op jit(solution)/shard_map/mlp_d4/ppermute | solution.py:57
  48.6 22.4 %collective-permute-start.12 = (bf16[3,656,128]{2,1,0:T(8,128)(2,1)S(1)}, bf16[3,656,128]{2,1,0:T(8,128)(2,1)}, u32[]{:S(2)}, u32[]{:S(2)}) collective-permute-start(bf16[3,656,128]{2,1,0:T(8,128)(2,1)S(1)} %get-tuple-element.124.refs_5_.refs_12_), channel_id=1, source_target_pairs={{0,4},{4,0},{8,12},{12,8},{16,20},{20,16},{24,28},{28,24},{1,5},{5... | collective-permute-start | bytes 1511432 | tf_op jit(solution)/shard_map/mlp0_d1/ppermute | solution.py:57
  50.1 21.0 %collective-permute-start.13 = (bf16[3,656,128]{2,1,0:T(8,128)(2,1)}, bf16[3,656,128]{2,1,0:T(8,128)(2,1)}, u32[]{:S(2)}, u32[]{:S(2)}) collective-permute-start(bf16[3,656,128]{2,1,0:T(8,128)(2,1)} %collective-permute-done.7.refs_7_.refs_14_), channel_id=1, source_target_pairs={{0,4},{4,0},{8,12},{12,8},{16,20},{20,16},{24,28},{28,24},{1,5},{5... | collective-permute-start | bytes 1511432 | tf_op jit(solution)/shard_map/mlp1_d1/ppermute | solution.py:57
  71.1 16.9 %collective-permute-start.17 = (bf16[256,1024]{1,0:T(8,128)(2,1)S(1)}, bf16[256,1024]{1,0:T(8,128)(2,1)S(1)}, u32[]{:S(2)}, u32[]{:S(2)}) collective-permute-start(bf16[256,1024]{1,0:T(8,128)(2,1)S(1)} %get-tuple-element.131), channel_id=1, source_target_pairs={{0,1},{1,0},{2,3},{3,2},{4,5},{5,4},{6,7},{7,6},{8,9},{9,8},{10,11... | collective-permute-start | bytes 1572872 | tf_op jit(solution)/shard_map/anear_t1/ppermute | solution.py:57
  73.2 14.8 %collective-permute-start.19 = (bf16[256,1024]{1,0:T(8,128)(2,1)S(1)}, bf16[256,1024]{1,0:T(8,128)(2,1)S(1)}, u32[]{:S(2)}, u32[]{:S(2)}) collective-permute-start(bf16[256,1024]{1,0:T(8,128)(2,1)S(1)} %add_convert_fusion.3), channel_id=1, source_target_pairs={{0,2},{1,3},{2,0},{3,1},{4,6},{5,7},{6,4},{7,5},{8,10},{9,11},{10,... | collective-permute-start | bytes 1572872 | tf_op jit(solution)/shard_map/afar_t2/ppermute | solution.py:57
  74.1 13.5 %collective-permute-start.16 = (bf16[3,656,128]{2,1,0:T(8,128)(2,1)}, bf16[3,656,128]{2,1,0:T(8,128)(2,1)S(1)}, u32[]{:S(2)}, u32[]{:S(2)}) collective-permute-start(bf16[3,656,128]{2,1,0:T(8,128)(2,1)} %collective-permute-done.11.refs_9_.refs_16_), channel_id=1, source_target_pairs={{0,8},{4,12},{8,0},{12,4},{16,24},{20,28},{24,16},{28,20},{1,9},{5... | collective-permute-start | bytes 1511432 | tf_op jit(solution)/shard_map/mlpfar_d2/ppermute | solution.py:57
  90.4 13.3 %collective-permute-start.21 = (bf16[256,1024]{1,0:T(8,128)(2,1)}, bf16[256,1024]{1,0:T(8,128)(2,1)S(1)}, u32[]{:S(2)}, u32[]{:S(2)}) collective-permute-start(bf16[256,1024]{1,0:T(8,128)(2,1)} %get-tuple-element.157.refs_2_.refs_1_), channel_id=1, source_target_pairs={{0,2},{1,3},{2,0},{3,1},{4,6},{5,7},{6,4},{7,5},{8,10},{9,11},{10,... | collective-permute-start | bytes 1572872 | tf_op jit(solution)/shard_map/norm2_t2/ppermute | solution.py:57
  119.1 20.8 %collective-permute-start.30 = (bf16[256,1024]{1,0:T(8,128)(2,1)}, bf16[256,1024]{1,0:T(8,128)(2,1)}, u32[]{:S(2)}, u32[]{:S(2)}) collective-permute-start(bf16[256,1024]{1,0:T(8,128)(2,1)} %add_convert_fusion.2), channel_id=1, source_target_pairs={{0,2},{1,3},{2,0},{3,1},{4,6},{5,7},{6,4},{7,5},{8,10},{9,11},{10,... | collective-permute-start | bytes 1572872 | tf_op jit(solution)/shard_map/far_t2/ppermute | solution.py:57
  139.9 13.9 %collective-permute-start.34 = (bf16[3,656,128]{2,1,0:T(8,128)(2,1)S(1)}, bf16[3,656,128]{2,1,0:T(8,128)(2,1)S(1)}, u32[]{:S(2)}, u32[]{:S(2)}) collective-permute-start(bf16[3,656,128]{2,1,0:T(8,128)(2,1)S(1)} %get-tuple-element.156), channel_id=1, source_target_pairs={{0,4},{4,0},{8,12},{12,8},{16,20},{20,16},{24,28},{28,24},{1,5},{5... | collective-permute-start | bytes 1511432 | tf_op jit(solution)/shard_map/gmlp0_d1/ppermute | solution.py:57
  141.1 14.0 %collective-permute-start.28 = (bf16[256,1024]{1,0:T(8,128)(2,1)S(1)}, bf16[256,1024]{1,0:T(8,128)(2,1)S(1)}, u32[]{:S(2)}, u32[]{:S(2)}) collective-permute-start(bf16[256,1024]{1,0:T(8,128)(2,1)S(1)} %copy-done.74), channel_id=1, source_target_pairs={{0,1},{1,0},{2,3},{3,2},{4,5},{5,4},{6,7},{7,6},{8,9},{9,8},{10,11... | collective-permute-start | bytes 1572872 | tf_op jit(solution)/shard_map/lofar_t1/ppermute | solution.py:57
  141.3 14.2 %collective-permute-start.27 = (bf16[256,1024]{1,0:T(8,128)(2,1)S(1)}, bf16[256,1024]{1,0:T(8,128)(2,1)S(1)}, u32[]{:S(2)}, u32[]{:S(2)}) collective-permute-start(bf16[256,1024]{1,0:T(8,128)(2,1)S(1)} %get-tuple-element.147), channel_id=1, source_target_pairs={{0,1},{1,0},{2,3},{3,2},{4,5},{5,4},{6,7},{7,6},{8,9},{9,8},{10,11... | collective-permute-start | bytes 1572872 | tf_op jit(solution)/shard_map/lonear_t1/ppermute | solution.py:57
  143.9 19.5 %collective-permute-start.32 = (bf16[256,1024]{1,0:T(8,128)(2,1)S(1)}, bf16[256,1024]{1,0:T(8,128)(2,1)S(1)}, u32[]{:S(2)}, u32[]{:S(2)}) collective-permute-start(bf16[256,1024]{1,0:T(8,128)(2,1)S(1)} %get-tuple-element.167.refs_5_), channel_id=1, source_target_pairs={{0,2},{1,3},{2,0},{3,1},{4,6},{5,7},{6,4},{7,5},{8,10},{9,11},{10,... | collective-permute-start | bytes 1572872 | tf_op jit(solution)/shard_map/aog_t2/ppermute | solution.py:57
  153.9 13.5 %collective-permute-start.35 = (bf16[3,656,128]{2,1,0:T(8,128)(2,1)S(1)}, bf16[3,656,128]{2,1,0:T(8,128)(2,1)S(1)}, u32[]{:S(2)}, u32[]{:S(2)}) collective-permute-start(bf16[3,656,128]{2,1,0:T(8,128)(2,1)S(1)} %get-tuple-element.166), channel_id=1, source_target_pairs={{0,4},{4,0},{8,12},{12,8},{16,20},{20,16},{24,28},{28,24},{1,5},{5... | collective-permute-start | bytes 1511432 | tf_op jit(solution)/shard_map/gmlp1_d1/ppermute | solution.py:57
  155.3 14.3 %collective-permute-start.31 = (bf16[256,1024]{1,0:T(8,128)(2,1)S(1)}, bf16[256,1024]{1,0:T(8,128)(2,1)S(1)}, u32[]{:S(2)}, u32[]{:S(2)}) collective-permute-start(bf16[256,1024]{1,0:T(8,128)(2,1)S(1)} %get-tuple-element.167.refs_5_), channel_id=1, source_target_pairs={{0,1},{1,0},{2,3},{3,2},{4,5},{5,4},{6,7},{7,6},{8,9},{9,8},{10,11... | collective-permute-start | bytes 1572872 | tf_op jit(solution)/shard_map/aog_t1/ppermute | solution.py:57
  163.4 30.8 %collective-permute-start.36 = (bf16[3,656,128]{2,1,0:T(8,128)(2,1)S(1)}, bf16[3,656,128]{2,1,0:T(8,128)(2,1)S(1)}, u32[]{:S(2)}, u32[]{:S(2)}) collective-permute-start(bf16[3,656,128]{2,1,0:T(8,128)(2,1)S(1)} %get-tuple-element.190), channel_id=1, source_target_pairs={{0,4},{4,0},{8,12},{12,8},{16,20},{20,16},{24,28},{28,24},{1,5},{5... | collective-permute-start | bytes 1511432 | tf_op jit(solution)/shard_map/gmlp2_d1/ppermute | solution.py:57
  167.5 26.8 %collective-permute-start.37 = (bf16[3,656,128]{2,1,0:T(8,128)(2,1)S(1)}, bf16[3,656,128]{2,1,0:T(8,128)(2,1)S(1)}, u32[]{:S(2)}, u32[]{:S(2)}) collective-permute-start(bf16[3,656,128]{2,1,0:T(8,128)(2,1)S(1)} %add_convert_fusion.5), channel_id=1, source_target_pairs={{0,8},{4,12},{8,0},{12,4},{16,24},{20,28},{24,16},{28,20},{1,9},{5... | collective-permute-start | bytes 1511432 | tf_op jit(solution)/shard_map/gmlpz1_d2/ppermute | solution.py:57
  168.2 26.3 %collective-permute-start.38 = (bf16[3,656,128]{2,1,0:T(8,128)(2,1)S(1)}, bf16[3,656,128]{2,1,0:T(8,128)(2,1)S(1)}, u32[]{:S(2)}, u32[]{:S(2)}) collective-permute-start(bf16[3,656,128]{2,1,0:T(8,128)(2,1)S(1)} %add_convert_fusion.6), channel_id=1, source_target_pairs={{0,8},{4,12},{8,0},{12,4},{16,24},{20,28},{24,16},{28,20},{1,9},{5... | collective-permute-start | bytes 1511432 | tf_op jit(solution)/shard_map/gmlpz0_d2/ppermute | solution.py:57
  169.6 24.9 %collective-permute-start.39 = (bf16[3,656,128]{2,1,0:T(8,128)(2,1)S(1)}, bf16[3,656,128]{2,1,0:T(8,128)(2,1)S(1)}, u32[]{:S(2)}, u32[]{:S(2)}) collective-permute-start(bf16[3,656,128]{2,1,0:T(8,128)(2,1)S(1)} %get-tuple-element.191), channel_id=1, source_target_pairs={{0,4},{4,0},{8,12},{12,8},{16,20},{20,16},{24,28},{28,24},{1,5},{5... | collective-permute-start | bytes 1511432 | tf_op jit(solution)/shard_map/gmlp3_d1/ppermute | solution.py:57
  196.7 14.7 %collective-permute-start.41 = (bf16[272,1024]{1,0:T(8,128)(2,1)S(1)}, bf16[272,1024]{1,0:T(8,128)(2,1)S(1)}, u32[]{:S(2)}, u32[]{:S(2)}) collective-permute-start(bf16[272,1024]{1,0:T(8,128)(2,1)S(1)} %get-tuple-element.194), channel_id=1, source_target_pairs={{0,2},{1,3},{2,0},{3,1},{4,6},{5,7},{6,4},{7,5},{8,10},{9,11},{10,... | collective-permute-start | bytes 1671176 | tf_op jit(solution)/shard_map/nfar_t2/ppermute | solution.py:57
  198.5 26.6 %collective-permute-start.43 = (bf16[3,656,128]{2,1,0:T(8,128)(2,1)S(1)}, bf16[3,656,128]{2,1,0:T(8,128)(2,1)S(1)}, u32[]{:S(2)}, u32[]{:S(2)}) collective-permute-start(bf16[3,656,128]{2,1,0:T(8,128)(2,1)S(1)} %add_convert_fusion.4), channel_id=1, source_target_pairs={{0,16},{4,20},{8,24},{12,28},{16,0},{20,4},{24,8},{28,12},{1,17},{... | collective-permute-start | bytes 1511432 | tf_op jit(solution)/shard_map/gmlp_d4/ppermute | solution.py:57
  199.7 14.8 %collective-permute-start.51 = (bf16[4,128,256]{2,1,0:T(8,128)(2,1)S(1)}, bf16[4,128,256]{2,1,0:T(8,128)(2,1)S(1)}, u32[]{:S(2)}, u32[]{:S(2)}) collective-permute-start(bf16[4,128,256]{2,1,0:T(8,128)(2,1)S(1)} %get-tuple-element.207), channel_id=1, source_target_pairs={{0,4},{4,0},{8,12},{12,8},{16,20},{20,16},{24,28},{28,24},{1,5},{5... | collective-permute-start | bytes 786440 | tf_op jit(solution)/shard_map/gqkv2_d1/ppermute | solution.py:57
  203.9 13.4 %collective-permute-start.53 = (bf16[4,128,256]{2,1,0:T(8,128)(2,1)S(1)}, bf16[4,128,256]{2,1,0:T(8,128)(2,1)S(1)}, u32[]{:S(2)}, u32[]{:S(2)}) collective-permute-start(bf16[4,128,256]{2,1,0:T(8,128)(2,1)S(1)} %add_convert_fusion.8), channel_id=1, source_target_pairs={{0,8},{4,12},{8,0},{12,4},{16,24},{20,28},{24,16},{28,20},{1,9},{5... | collective-permute-start | bytes 786440 | tf_op jit(solution)/shard_map/gqkvz1_d2/ppermute | solution.py:57
  209.4 16.6 %collective-permute-start.45 = (bf16[256,1024]{1,0:T(8,128)(2,1)S(1)}, bf16[256,1024]{1,0:T(8,128)(2,1)S(1)}, u32[]{:S(2)}, u32[]{:S(2)}) collective-permute-start(bf16[256,1024]{1,0:T(8,128)(2,1)S(1)} %get-tuple-element.200), channel_id=1, source_target_pairs={{0,1},{1,0},{2,3},{3,2},{4,5},{5,4},{6,7},{7,6},{8,9},{9,8},{10,11... | collective-permute-start | bytes 1572872 | tf_op jit(solution)/shard_map/nnear_t1/ppermute | solution.py:57
  211.4 24.7 %collective-permute-start.50 = (bf16[4,128,256]{2,1,0:T(8,128)(2,1)S(1)}, bf16[4,128,256]{2,1,0:T(8,128)(2,1)S(1)}, u32[]{:S(2)}, u32[]{:S(2)}) collective-permute-start(bf16[4,128,256]{2,1,0:T(8,128)(2,1)S(1)} %add_convert_fusion.9), channel_id=1, source_target_pairs={{0,8},{4,12},{8,0},{12,4},{16,24},{20,28},{24,16},{28,20},{1,9},{5... | collective-permute-start | bytes 786440 | tf_op jit(solution)/shard_map/gqkvz0_d2/ppermute | solution.py:57
  217.4 17.9 %collective-permute-start.54 = (bf16[4,128,256]{2,1,0:T(8,128)(2,1)S(1)}, bf16[4,128,256]{2,1,0:T(8,128)(2,1)}, u32[]{:S(2)}, u32[]{:S(2)}) collective-permute-start(bf16[4,128,256]{2,1,0:T(8,128)(2,1)S(1)} %add_convert_fusion.7), channel_id=1, source_target_pairs={{0,16},{4,20},{8,24},{12,28},{16,0},{20,4},{24,8},{28,12},{1,17},{... | collective-permute-start | bytes 786440 | tf_op jit(solution)/shard_map/gqkv_d4/ppermute | solution.py:57
  220.8 15.4 %collective-permute-start.48 = (bf16[4,128,256]{2,1,0:T(8,128)(2,1)S(1)}, bf16[4,128,256]{2,1,0:T(8,128)(2,1)}, u32[]{:S(2)}, u32[]{:S(2)}) collective-permute-start(bf16[4,128,256]{2,1,0:T(8,128)(2,1)S(1)} %get-tuple-element.203), channel_id=1, source_target_pairs={{0,4},{4,0},{8,12},{12,8},{16,20},{20,16},{24,28},{28,24},{1,5},{5... | collective-permute-start | bytes 786440 | tf_op jit(solution)/shard_map/gqkv3_d1/ppermute | solution.py:57
  (100 other events, 960.3 us)

commit v4 on v3

--- a/solution.py
+++ b/solution.py
@@ -36,7 +36,7 @@
 
 
 def hbm():
-    return pl.BlockSpec(memory_space=pltpu.HBM)
+    return pl.BlockSpec(memory_space=pl.ANY)
 
 
 def call(body, ins, outs, scratch=(), name=None):

time: 242 us -> 242 us (level)
  no operation moved by 1% of the time
where the time goes in v4:
time: 242 us; the launch traced here: 241 us
  waiting for transfers between devices  77 us (32%)
  Pallas kernels  69.1 us (29%)
  starting transfers between devices  55.1 us (23%)
  local copies, waits for them, and re-layouts  30.4 us (13%)
  other arithmetic  7.8 us (3%)
    ppermute x55, waiting for transfers between devices, swap(): return lax.ppermute(value, axis, [(i, i ^ distance) for i in range(size)])  77 us
    pallas_call x11, Pallas kernels, call(): pl.pallas_call(body, out_shape=[jax.ShapeDtypeStruct(o[0], o[1]) for o in...  69.1 us
    ppermute x55, starting transfers between devices, swap(): return lax.ppermute(value, axis, [(i, i ^ distance) for i in range(size)])  55.1 us
    unnamed x155, local copies, waits for them, and re-layouts  29.7 us
  transfers between devices with their start and end apart: 55, of which 25 were waited for; matrix products, arithmetic and copies ran while one was open for 2% of the time, Pallas kernels for 24%

profile of v4, /device:TPU:0, one launch (start us, length us, event | category | flops | bytes accessed | tf_op | source)
XLA Modules:
  0.0 240.8 jit_solution(80004497022846489)
XLA Ops:
  4.4 4.1 %collective-permute-start.2 = (bf16[4,128,256]{2,1,0:T(8,128)(2,1)S(1)}, bf16[4,128,256]{2,1,0:T(8,128)(2,1)S(1)}, u32[]{:S(2)}, u32[]{:S(2)}) collective-permute-start(bf16[4,128,256]{2,1,0:T(8,128)(2,1)S(1)} %get-tuple-element.110.refs_7_.refs_19_), channel_id=1, source_target_pairs={{0,16},{4,20},{8,24},{12,28},{16,0},{20,4},{24,8},{28,12},{1,17},{... | collective-permute-start | bytes 786440 | tf_op jit(solution)/shard_map/qkvo_d4/ppermute | solution.py:57
  8.5 1.6 collective-permute-start.1
  11.6 8.9 %collective-permute-done.2.refs_11_.refs_23_ = bf16[4,128,256]{2,1,0:T(8,128)(2,1)S(1)} collective-permute-done((bf16[4,128,256]{2,1,0:T(8,128)(2,1)S(1)}, bf16[4,128,256]{2,1,0:T(8,128)(2,1)S(1)}, u32[]{:S(2)}, u32[]{:S(2)}) %collective-permute-start.2) | collective-permute-done | bytes 262176 | tf_op jit(solution)/shard_map/qkvo_d4/ppermute | solution.py:57
  30.9 3.4 %collective-permute-done.8.refs_10_.refs_22_ = bf16[4,128,256]{2,1,0:T(8,128)(2,1)S(1)} collective-permute-done((bf16[4,128,256]{2,1,0:T(8,128)(2,1)S(1)}, bf16[4,128,256]{2,1,0:T(8,128)(2,1)S(1)}, u32[]{:S(2)}, u32[]{:S(2)}) %collective-permute-start.8) | collective-permute-done | bytes 262176 | tf_op jit(solution)/shard_map/qkvo1_d1/ppermute | solution.py:57
  35.1 2.0 collective-permute-start.10
  37.8 2.2 collective-permute-done.9.refs_12_.refs_24_
  41.2 3.3 %collective-permute-done.10.refs_14_.refs_26_ = bf16[4,128,256]{2,1,0:T(8,128)(2,1)S(1)} collective-permute-done((bf16[4,128,256]{2,1,0:T(8,128)(2,1)S(1)}, bf16[4,128,256]{2,1,0:T(8,128)(2,1)S(1)}, u32[]{:S(2)}, u32[]{:S(2)}) %collective-permute-start.10) | collective-permute-done | bytes 262176 | tf_op jit(solution)/shard_map/qkvo3_d1/ppermute | solution.py:57
  45.2 3.4 %collective-permute-start.11 = (bf16[3,656,128]{2,1,0:T(8,128)(2,1)S(1)}, bf16[3,656,128]{2,1,0:T(8,128)(2,1)}, u32[]{:S(2)}, u32[]{:S(2)}) collective-permute-start(bf16[3,656,128]{2,1,0:T(8,128)(2,1)S(1)} %get-tuple-element.124.refs_5_.refs_12_), channel_id=1, source_target_pairs={{0,16},{4,20},{8,24},{12,28},{16,0},{20,4},{24,8},{28,12},{1,17},{... | collective-permute-start | bytes 1511432 | tf_op jit(solution)/shard_map/mlp_d4/ppermute | solution.py:57
  48.6 1.5 collective-permute-start.12
  58.4 10.9 %attend_forward.1 = (bf16[256,1024]{1,0:T(8,128)(2,1)S(1)}, bf16[256,1024]{1,0:T(8,128)(2,1)S(1)}, bf16[256,1024]{1,0:T(8,128)(2,1)S(1)}, bf16[256,1024]{1,0:T(8...) custom-call(s32[8]{0:T(128)S(1)} %iota_xor_fusion.refs_0_.refs_2_, ...), custom_call_target="tpu_custom_call" | custom-call | flops 1000 | bytes 1000 | tf_op jit(solution)/shard_map/attend_forward/pallas_call | solution.py:43
  76.2 11.3 %collective-permute-done.16.refs_11_.refs_18_ = bf16[3,656,128]{2,1,0:T(8,128)(2,1)S(1)} collective-permute-done((bf16[3,656,128]{2,1,0:T(8,128)(2,1)}, bf16[3,656,128]{2,1,0:T(8,128)(2,1)S(1)}, u32[]{:S(2)}, u32[]{:S(2)}) %collective-permute-start.16) | collective-permute-done | bytes 503840 | tf_op jit(solution)/shard_map/mlpfar_d2/ppermute | solution.py:57
  93.1 10.6 %collective-permute-done.22.refs_12_.refs_19_ = bf16[3,656,128]{2,1,0:T(8,128)(2,1)S(1)} collective-permute-done((bf16[3,656,128]{2,1,0:T(8,128)(2,1)S(1)}, bf16[3,656,128]{2,1,0:T(8,128)(2,1)S(1)}, u32[]{:S(2)}, u32[]{:S(2)}) %collective-permute-start.22) | collective-permute-done | bytes 503840 | tf_op jit(solution)/shard_map/mlp3_d1/ppermute | solution.py:57
  103.7 1.9 collective-permute-done.23.refs_2_.refs_5_.refs_4_
  105.6 8.8 %feed_far.1 = (bf16[256,1024]{1,0:T(8,128)(2,1)S(1)}, bf16[256,1024]{1,0:T(8,128)(2,1)S(1)}, bf16[256,1024]{1,0:T(8,128)(2,1)S(1)}, bf16[256,1024]{1,0:T(8,128)(...) custom-call(s32[8]{0:T(128)S(1)} %iota_xor_fusion.refs_0_.refs_2_, ...), custom_call_target="tpu_custom_call" | custom-call | flops 1000 | bytes 1000 | tf_op jit(solution)/shard_map/feed_far/pallas_call | solution.py:43
  126.4 13.4 %feed_near.1 = (bf16[256,1024]{1,0:T(8,128)(2,1)S(1)}, bf16[256,1024]{1,0:T(8,128)(2,1)S(1)}, bf16[256,1024]{1,0:T(8,128)(2,1)S(1)}, bf16[256,1024]{1,0:T(8,128)...) custom-call(s32[8]{0:T(128)S(1)} %iota_xor_fusion.refs_0_.refs_2_, ...), custom_call_target="tpu_custom_call" | custom-call | flops 1000 | bytes 1000 | tf_op jit(solution)/shard_map/feed_near/pallas_call | solution.py:43
  141.8 2.1 middle_back.1
  145.1 8.7 %collective-permute-done.34 = bf16[3,656,128]{2,1,0:T(8,128)(2,1)S(1)} collective-permute-done((bf16[3,656,128]{2,1,0:T(8,128)(2,1)S(1)}, bf16[3,656,128]{2,1,0:T(8,128)(2,1)S(1)}, u32[]{:S(2)}, u32[]{:S(2)}) %collective-permute-start.34) | collective-permute-done | bytes 503840 | tf_op jit(solution)/shard_map/gmlp0_d1/ppermute | solution.py:57
  156.4 7.0 %feed_late.1 = (bf16[3,656,128]{2,1,0:T(8,128)(2,1)S(1)}, bf16[3,656,128]{2,1,0:T(8,128)(2,1)S(1)}, bf16[3,656,128]{2,1,0:T(8,128)(2,1)S(1)}, bf16[3,656,128]{2,1,0:T(8,128)(2,1)S(1)}) custom-call(s32[8]{0:T(128)S(1)} %stack.35.refs_1_.refs_0_, bf16[256,1024]{1,0:T(8,128)(2,1)} %get-tuple-element.157.refs_2_.refs_1_, ...), custom_call_target="tpu_custom_call" | custom-call | flops 1000 | bytes 1000 | tf_op jit(solution)/shard_map/feed_late/pallas_call | solution.py:43
  164.6 2.8 %collective-permute-done.35 = bf16[3,656,128]{2,1,0:T(8,128)(2,1)S(1)} collective-permute-done((bf16[3,656,128]{2,1,0:T(8,128)(2,1)S(1)}, bf16[3,656,128]{2,1,0:T(8,128)(2,1)S(1)}, u32[]{:S(2)}, u32[]{:S(2)}) %collective-permute-start.35) | collective-permute-done | bytes 503840 | tf_op jit(solution)/shard_map/gmlp1_d1/ppermute | solution.py:57
  171.2 23.1 %attend_backward.1 = (bf16[4,128,256]{2,1,0:T(8,128)(2,1)S(1)}, bf16[4,128,256]{2,1,0:T(8,128)(2,1)S(1)}, bf16[4,128,256]{2,1,0:T(8,128)(2,1)S(1)}, bf16[4,128,2...) custom-call(s32[8]{0:T(128)S(1)} %stack.35.refs_1_.refs_0_, ...), custom_call_target="tpu_custom_call" | custom-call | flops 1000 | bytes 1000 | tf_op jit(solution)/shard_map/attend_backward/pallas_call | solution.py:43
  201.2 2.6 %collective-permute-done.52 = bf16[4,128,256]{2,1,0:T(8,128)(2,1)S(1)} collective-permute-done((bf16[4,128,256]{2,1,0:T(8,128)(2,1)S(1)}, bf16[4,128,256]{2,1,0:T(8,128)(2,1)S(1)}, u32[]{:S(2)}, u32[]{:S(2)}) %collective-permute-start.52) | collective-permute-done | bytes 262176 | tf_op jit(solution)/shard_map/gqkv1_d1/ppermute | solution.py:57
  203.9 1.8 collective-permute-start.53
  205.6 3.8 %collective-permute-done.49 = bf16[4,128,256]{2,1,0:T(8,128)(2,1)S(1)} collective-permute-done((bf16[4,128,256]{2,1,0:T(8,128)(2,1)S(1)}, bf16[4,128,256]{2,1,0:T(8,128)(2,1)S(1)}, u32[]{:S(2)}, u32[]{:S(2)}) %collective-permute-start.49) | collective-permute-done | bytes 262176 | tf_op jit(solution)/shard_map/gqkv0_d1/ppermute | solution.py:57
  209.5 1.9 collective-permute-done.41.sc
  211.4 1.7 collective-permute-start.50
  215.2 2.1 collective-permute-done.53
  217.4 3.4 %collective-permute-start.54 = (bf16[4,128,256]{2,1,0:T(8,128)(2,1)S(1)}, bf16[4,128,256]{2,1,0:T(8,128)(2,1)}, u32[]{:S(2)}, u32[]{:S(2)}) collective-permute-start(bf16[4,128,256]{2,1,0:T(8,128)(2,1)S(1)} %add_convert_fusion.7), channel_id=1, source_target_pairs={{0,16},{4,20},{8,24},{12,28},{16,0},{20,4},{24,8},{28,12},{1,17},{... | collective-permute-start | bytes 786440 | tf_op jit(solution)/shard_map/gqkv_d4/ppermute | solution.py:57
  220.8 1.9 collective-permute-start.48
  222.7 2.4 collective-permute-done.43
  226.0 1.9 input_back.1
  231.8 2.9 %collective-permute-done.47 = f32[16,128]{1,0:T(8,128)S(1)} collective-permute-done((f32[16,128]{1,0:T(8,128)S(1)}, f32[16,128]{1,0:T(8,128)S(1)}, u32[]{:S(2)}, u32[]{:S(2)}) %collective-permute-start.47) | collective-permute-done | bytes 8224 | tf_op jit(solution)/shard_map/gain_d4/ppermute | solution.py:57
  237.8 1.9 convert_add_fusion
  (265 shorter events, 80.1 us)
Async XLA Ops:
  4.4 16.1 %collective-permute-start.2 = (bf16[4,128,256]{2,1,0:T(8,128)(2,1)S(1)}, bf16[4,128,256]{2,1,0:T(8,128)(2,1)S(1)}, u32[]{:S(2)}, u32[]{:S(2)}) collective-permute-start(bf16[4,128,256]{2,1,0:T(8,128)(2,1)S(1)} %get-tuple-element.110.refs_7_.refs_19_), channel_id=1, source_target_pairs={{0,16},{4,20},{8,24},{12,28},{16,0},{20,4},{24,8},{28,12},{1,17},{... | collective-permute-start | bytes 786440 | tf_op jit(solution)/shard_map/qkvo_d4/ppermute | solution.py:57
  8.5 14.8 %collective-permute-start.1 = (bf16[4,128,256]{2,1,0:T(8,128)(2,1)S(1)}, bf16[4,128,256]{2,1,0:T(8,128)(2,1)S(1)}, u32[]{:S(2)}, u32[]{:S(2)}) collective-permute-start(bf16[4,128,256]{2,1,0:T(8,128)(2,1)S(1)} %get-tuple-element.110.refs_7_.refs_19_), channel_id=1, source_target_pairs={{0,8},{4,12},{8,0},{12,4},{16,24},{20,28},{24,16},{28,20},{1,9},{5... | collective-permute-start | bytes 786440 | tf_op jit(solution)/shard_map/qkvo_d2/ppermute | solution.py:57
  24.1 13.7 %collective-permute-start.4 = (bf16[256,1024]{1,0:T(8,128)(2,1)S(1)}, bf16[256,1024]{1,0:T(8,128)(2,1)S(1)}, u32[]{:S(2)}, u32[]{:S(2)}) collective-permute-start(bf16[256,1024]{1,0:T(8,128)(2,1)S(1)} %norm.1.refs_2_.refs_15_), channel_id=1, source_target_pairs={{0,2},{1,3},{2,0},{3,1},{4,6},{5,7},{6,4},{7,5},{8,10},{9,11},{10,... | collective-permute-start | bytes 1572872 | tf_op jit(solution)/shard_map/norm_t2/ppermute | solution.py:57
  27.8 22.3 %collective-permute-start.3 = (bf16[256,1024]{1,0:T(8,128)(2,1)S(1)}, bf16[256,1024]{1,0:T(8,128)(2,1)S(1)}, u32[]{:S(2)}, u32[]{:S(2)}) collective-permute-start(bf16[256,1024]{1,0:T(8,128)(2,1)S(1)} %norm.1.refs_2_.refs_15_), channel_id=1, source_target_pairs={{0,1},{1,0},{2,3},{3,2},{4,5},{5,4},{6,7},{7,6},{8,9},{9,8},{10,11... | collective-permute-start | bytes 1572872 | tf_op jit(solution)/shard_map/norm_t1/ppermute | solution.py:57
  28.0 20.6 %collective-permute-start.7 = (bf16[3,656,128]{2,1,0:T(8,128)(2,1)S(1)}, bf16[3,656,128]{2,1,0:T(8,128)(2,1)}, u32[]{:S(2)}, u32[]{:S(2)}) collective-permute-start(bf16[3,656,128]{2,1,0:T(8,128)(2,1)S(1)} %get-tuple-element.124.refs_5_.refs_12_), channel_id=1, source_target_pairs={{0,8},{4,12},{8,0},{12,4},{16,24},{20,28},{24,16},{28,20},{1,9},{5... | collective-permute-start | bytes 1511432 | tf_op jit(solution)/shard_map/mlp_d2/ppermute | solution.py:57
  40.7 30.3 %collective-permute-start.14 = (bf16[256,1024]{1,0:T(8,128)(2,1)}, bf16[256,1024]{1,0:T(8,128)(2,1)S(1)}, u32[]{:S(2)}, u32[]{:S(2)}) collective-permute-start(bf16[256,1024]{1,0:T(8,128)(2,1)} %refs_5_), channel_id=1, source_target_pairs={{0,2},{1,3},{2,0},{3,1},{4,6},{5,7},{6,4},{7,5},{8,10},{9,11},{10,... | collective-permute-start | bytes 1572872 | tf_op jit(solution)/shard_map/cot_t2/ppermute | solution.py:57
  45.2 25.8 %collective-permute-start.11 = (bf16[3,656,128]{2,1,0:T(8,128)(2,1)S(1)}, bf16[3,656,128]{2,1,0:T(8,128)(2,1)}, u32[]{:S(2)}, u32[]{:S(2)}) collective-permute-start(bf16[3,656,128]{2,1,0:T(8,128)(2,1)S(1)} %get-tuple-element.124.refs_5_.refs_12_), channel_id=1, source_target_pairs={{0,16},{4,20},{8,24},{12,28},{16,0},{20,4},{24,8},{28,12},{1,17},{... | collective-permute-start | bytes 1511432 | tf_op jit(solution)/shard_map/mlp_d4/ppermute | solution.py:57
  48.6 22.4 %collective-permute-start.12 = (bf16[3,656,128]{2,1,0:T(8,128)(2,1)S(1)}, bf16[3,656,128]{2,1,0:T(8,128)(2,1)}, u32[]{:S(2)}, u32[]{:S(2)}) collective-permute-start(bf16[3,656,128]{2,1,0:T(8,128)(2,1)S(1)} %get-tuple-element.124.refs_5_.refs_12_), channel_id=1, source_target_pairs={{0,4},{4,0},{8,12},{12,8},{16,20},{20,16},{24,28},{28,24},{1,5},{5... | collective-permute-start | bytes 1511432 | tf_op jit(solution)/shard_map/mlp0_d1/ppermute | solution.py:57
  50.1 21.0 %collective-permute-start.13 = (bf16[3,656,128]{2,1,0:T(8,128)(2,1)}, bf16[3,656,128]{2,1,0:T(8,128)(2,1)}, u32[]{:S(2)}, u32[]{:S(2)}) collective-permute-start(bf16[3,656,128]{2,1,0:T(8,128)(2,1)} %collective-permute-done.7.refs_7_.refs_14_), channel_id=1, source_target_pairs={{0,4},{4,0},{8,12},{12,8},{16,20},{20,16},{24,28},{28,24},{1,5},{5... | collective-permute-start | bytes 1511432 | tf_op jit(solution)/shard_map/mlp1_d1/ppermute | solution.py:57
  71.1 16.9 %collective-permute-start.17 = (bf16[256,1024]{1,0:T(8,128)(2,1)S(1)}, bf16[256,1024]{1,0:T(8,128)(2,1)S(1)}, u32[]{:S(2)}, u32[]{:S(2)}) collective-permute-start(bf16[256,1024]{1,0:T(8,128)(2,1)S(1)} %get-tuple-element.131), channel_id=1, source_target_pairs={{0,1},{1,0},{2,3},{3,2},{4,5},{5,4},{6,7},{7,6},{8,9},{9,8},{10,11... | collective-permute-start | bytes 1572872 | tf_op jit(solution)/shard_map/anear_t1/ppermute | solution.py:57
  73.2 14.8 %collective-permute-start.19 = (bf16[256,1024]{1,0:T(8,128)(2,1)S(1)}, bf16[256,1024]{1,0:T(8,128)(2,1)S(1)}, u32[]{:S(2)}, u32[]{:S(2)}) collective-permute-start(bf16[256,1024]{1,0:T(8,128)(2,1)S(1)} %add_convert_fusion.3), channel_id=1, source_target_pairs={{0,2},{1,3},{2,0},{3,1},{4,6},{5,7},{6,4},{7,5},{8,10},{9,11},{10,... | collective-permute-start | bytes 1572872 | tf_op jit(solution)/shard_map/afar_t2/ppermute | solution.py:57
  74.1 13.5 %collective-permute-start.16 = (bf16[3,656,128]{2,1,0:T(8,128)(2,1)}, bf16[3,656,128]{2,1,0:T(8,128)(2,1)S(1)}, u32[]{:S(2)}, u32[]{:S(2)}) collective-permute-start(bf16[3,656,128]{2,1,0:T(8,128)(2,1)} %collective-permute-done.11.refs_9_.refs_16_), channel_id=1, source_target_pairs={{0,8},{4,12},{8,0},{12,4},{16,24},{20,28},{24,16},{28,20},{1,9},{5... | collective-permute-start | bytes 1511432 | tf_op jit(solution)/shard_map/mlpfar_d2/ppermute | solution.py:57
  90.4 13.3 %collective-permute-start.21 = (bf16[256,1024]{1,0:T(8,128)(2,1)}, bf16[256,1024]{1,0:T(8,128)(2,1)S(1)}, u32[]{:S(2)}, u32[]{:S(2)}) collective-permute-start(bf16[256,1024]{1,0:T(8,128)(2,1)} %get-tuple-element.157.refs_2_.refs_1_), channel_id=1, source_target_pairs={{0,2},{1,3},{2,0},{3,1},{4,6},{5,7},{6,4},{7,5},{8,10},{9,11},{10,... | collective-permute-start | bytes 1572872 | tf_op jit(solution)/shard_map/norm2_t2/ppermute | solution.py:57
  119.1 20.8 %collective-permute-start.30 = (bf16[256,1024]{1,0:T(8,128)(2,1)}, bf16[256,1024]{1,0:T(8,128)(2,1)}, u32[]{:S(2)}, u32[]{:S(2)}) collective-permute-start(bf16[256,1024]{1,0:T(8,128)(2,1)} %add_convert_fusion.2), channel_id=1, source_target_pairs={{0,2},{1,3},{2,0},{3,1},{4,6},{5,7},{6,4},{7,5},{8,10},{9,11},{10,... | collective-permute-start | bytes 1572872 | tf_op jit(solution)/shard_map/far_t2/ppermute | solution.py:57
  139.9 13.9 %collective-permute-start.34 = (bf16[3,656,128]{2,1,0:T(8,128)(2,1)S(1)}, bf16[3,656,128]{2,1,0:T(8,128)(2,1)S(1)}, u32[]{:S(2)}, u32[]{:S(2)}) collective-permute-start(bf16[3,656,128]{2,1,0:T(8,128)(2,1)S(1)} %get-tuple-element.156), channel_id=1, source_target_pairs={{0,4},{4,0},{8,12},{12,8},{16,20},{20,16},{24,28},{28,24},{1,5},{5... | collective-permute-start | bytes 1511432 | tf_op jit(solution)/shard_map/gmlp0_d1/ppermute | solution.py:57
  141.1 14.0 %collective-permute-start.28 = (bf16[256,1024]{1,0:T(8,128)(2,1)S(1)}, bf16[256,1024]{1,0:T(8,128)(2,1)S(1)}, u32[]{:S(2)}, u32[]{:S(2)}) collective-permute-start(bf16[256,1024]{1,0:T(8,128)(2,1)S(1)} %copy-done.74), channel_id=1, source_target_pairs={{0,1},{1,0},{2,3},{3,2},{4,5},{5,4},{6,7},{7,6},{8,9},{9,8},{10,11... | collective-permute-start | bytes 1572872 | tf_op jit(solution)/shard_map/lofar_t1/ppermute | solution.py:57
  141.3 14.2 %collective-permute-start.27 = (bf16[256,1024]{1,0:T(8,128)(2,1)S(1)}, bf16[256,1024]{1,0:T(8,128)(2,1)S(1)}, u32[]{:S(2)}, u32[]{:S(2)}) collective-permute-start(bf16[256,1024]{1,0:T(8,128)(2,1)S(1)} %get-tuple-element.147), channel_id=1, source_target_pairs={{0,1},{1,0},{2,3},{3,2},{4,5},{5,4},{6,7},{7,6},{8,9},{9,8},{10,11... | collective-permute-start | bytes 1572872 | tf_op jit(solution)/shard_map/lonear_t1/ppermute | solution.py:57
  143.9 19.5 %collective-permute-start.32 = (bf16[256,1024]{1,0:T(8,128)(2,1)S(1)}, bf16[256,1024]{1,0:T(8,128)(2,1)S(1)}, u32[]{:S(2)}, u32[]{:S(2)}) collective-permute-start(bf16[256,1024]{1,0:T(8,128)(2,1)S(1)} %get-tuple-element.167.refs_5_), channel_id=1, source_target_pairs={{0,2},{1,3},{2,0},{3,1},{4,6},{5,7},{6,4},{7,5},{8,10},{9,11},{10,... | collective-permute-start | bytes 1572872 | tf_op jit(solution)/shard_map/aog_t2/ppermute | solution.py:57
  153.9 13.5 %collective-permute-start.35 = (bf16[3,656,128]{2,1,0:T(8,128)(2,1)S(1)}, bf16[3,656,128]{2,1,0:T(8,128)(2,1)S(1)}, u32[]{:S(2)}, u32[]{:S(2)}) collective-permute-start(bf16[3,656,128]{2,1,0:T(8,128)(2,1)S(1)} %get-tuple-element.166), channel_id=1, source_target_pairs={{0,4},{4,0},{8,12},{12,8},{16,20},{20,16},{24,28},{28,24},{1,5},{5... | collective-permute-start | bytes 1511432 | tf_op jit(solution)/shard_map/gmlp1_d1/ppermute | solution.py:57
  155.3 14.3 %collective-permute-start.31 = (bf16[256,1024]{1,0:T(8,128)(2,1)S(1)}, bf16[256,1024]{1,0:T(8,128)(2,1)S(1)}, u32[]{:S(2)}, u32[]{:S(2)}) collective-permute-start(bf16[256,1024]{1,0:T(8,128)(2,1)S(1)} %get-tuple-element.167.refs_5_), channel_id=1, source_target_pairs={{0,1},{1,0},{2,3},{3,2},{4,5},{5,4},{6,7},{7,6},{8,9},{9,8},{10,11... | collective-permute-start | bytes 1572872 | tf_op jit(solution)/shard_map/aog_t1/ppermute | solution.py:57
  163.4 30.8 %collective-permute-start.36 = (bf16[3,656,128]{2,1,0:T(8,128)(2,1)S(1)}, bf16[3,656,128]{2,1,0:T(8,128)(2,1)S(1)}, u32[]{:S(2)}, u32[]{:S(2)}) collective-permute-start(bf16[3,656,128]{2,1,0:T(8,128)(2,1)S(1)} %get-tuple-element.190), channel_id=1, source_target_pairs={{0,4},{4,0},{8,12},{12,8},{16,20},{20,16},{24,28},{28,24},{1,5},{5... | collective-permute-start | bytes 1511432 | tf_op jit(solution)/shard_map/gmlp2_d1/ppermute | solution.py:57
  167.5 26.8 %collective-permute-start.37 = (bf16[3,656,128]{2,1,0:T(8,128)(2,1)S(1)}, bf16[3,656,128]{2,1,0:T(8,128)(2,1)S(1)}, u32[]{:S(2)}, u32[]{:S(2)}) collective-permute-start(bf16[3,656,128]{2,1,0:T(8,128)(2,1)S(1)} %add_convert_fusion.5), channel_id=1, source_target_pairs={{0,8},{4,12},{8,0},{12,4},{16,24},{20,28},{24,16},{28,20},{1,9},{5... | collective-permute-start | bytes 1511432 | tf_op jit(solution)/shard_map/gmlpz1_d2/ppermute | solution.py:57
  168.2 26.3 %collective-permute-start.38 = (bf16[3,656,128]{2,1,0:T(8,128)(2,1)S(1)}, bf16[3,656,128]{2,1,0:T(8,128)(2,1)S(1)}, u32[]{:S(2)}, u32[]{:S(2)}) collective-permute-start(bf16[3,656,128]{2,1,0:T(8,128)(2,1)S(1)} %add_convert_fusion.6), channel_id=1, source_target_pairs={{0,8},{4,12},{8,0},{12,4},{16,24},{20,28},{24,16},{28,20},{1,9},{5... | collective-permute-start | bytes 1511432 | tf_op jit(solution)/shard_map/gmlpz0_d2/ppermute | solution.py:57
  169.6 24.9 %collective-permute-start.39 = (bf16[3,656,128]{2,1,0:T(8,128)(2,1)S(1)}, bf16[3,656,128]{2,1,0:T(8,128)(2,1)S(1)}, u32[]{:S(2)}, u32[]{:S(2)}) collective-permute-start(bf16[3,656,128]{2,1,0:T(8,128)(2,1)S(1)} %get-tuple-element.191), channel_id=1, source_target_pairs={{0,4},{4,0},{8,12},{12,8},{16,20},{20,16},{24,28},{28,24},{1,5},{5... | collective-permute-start | bytes 1511432 | tf_op jit(solution)/shard_map/gmlp3_d1/ppermute | solution.py:57
  196.7 14.7 %collective-permute-start.41 = (bf16[272,1024]{1,0:T(8,128)(2,1)S(1)}, bf16[272,1024]{1,0:T(8,128)(2,1)S(1)}, u32[]{:S(2)}, u32[]{:S(2)}) collective-permute-start(bf16[272,1024]{1,0:T(8,128)(2,1)S(1)} %get-tuple-element.194), channel_id=1, source_target_pairs={{0,2},{1,3},{2,0},{3,1},{4,6},{5,7},{6,4},{7,5},{8,10},{9,11},{10,... | collective-permute-start | bytes 1671176 | tf_op jit(solution)/shard_map/nfar_t2/ppermute | solution.py:57
  198.5 26.6 %collective-permute-start.43 = (bf16[3,656,128]{2,1,0:T(8,128)(2,1)S(1)}, bf16[3,656,128]{2,1,0:T(8,128)(2,1)S(1)}, u32[]{:S(2)}, u32[]{:S(2)}) collective-permute-start(bf16[3,656,128]{2,1,0:T(8,128)(2,1)S(1)} %add_convert_fusion.4), channel_id=1, source_target_pairs={{0,16},{4,20},{8,24},{12,28},{16,0},{20,4},{24,8},{28,12},{1,17},{... | collective-permute-start | bytes 1511432 | tf_op jit(solution)/shard_map/gmlp_d4/ppermute | solution.py:57
  199.7 14.8 %collective-permute-start.51 = (bf16[4,128,256]{2,1,0:T(8,128)(2,1)S(1)}, bf16[4,128,256]{2,1,0:T(8,128)(2,1)S(1)}, u32[]{:S(2)}, u32[]{:S(2)}) collective-permute-start(bf16[4,128,256]{2,1,0:T(8,128)(2,1)S(1)} %get-tuple-element.207), channel_id=1, source_target_pairs={{0,4},{4,0},{8,12},{12,8},{16,20},{20,16},{24,28},{28,24},{1,5},{5... | collective-permute-start | bytes 786440 | tf_op jit(solution)/shard_map/gqkv2_d1/ppermute | solution.py:57
  203.9 13.4 %collective-permute-start.53 = (bf16[4,128,256]{2,1,0:T(8,128)(2,1)S(1)}, bf16[4,128,256]{2,1,0:T(8,128)(2,1)S(1)}, u32[]{:S(2)}, u32[]{:S(2)}) collective-permute-start(bf16[4,128,256]{2,1,0:T(8,128)(2,1)S(1)} %add_convert_fusion.8), channel_id=1, source_target_pairs={{0,8},{4,12},{8,0},{12,4},{16,24},{20,28},{24,16},{28,20},{1,9},{5... | collective-permute-start | bytes 786440 | tf_op jit(solution)/shard_map/gqkvz1_d2/ppermute | solution.py:57
  209.4 16.6 %collective-permute-start.45 = (bf16[256,1024]{1,0:T(8,128)(2,1)S(1)}, bf16[256,1024]{1,0:T(8,128)(2,1)S(1)}, u32[]{:S(2)}, u32[]{:S(2)}) collective-permute-start(bf16[256,1024]{1,0:T(8,128)(2,1)S(1)} %get-tuple-element.200), channel_id=1, source_target_pairs={{0,1},{1,0},{2,3},{3,2},{4,5},{5,4},{6,7},{7,6},{8,9},{9,8},{10,11... | collective-permute-start | bytes 1572872 | tf_op jit(solution)/shard_map/nnear_t1/ppermute | solution.py:57
  211.4 24.7 %collective-permute-start.50 = (bf16[4,128,256]{2,1,0:T(8,128)(2,1)S(1)}, bf16[4,128,256]{2,1,0:T(8,128)(2,1)S(1)}, u32[]{:S(2)}, u32[]{:S(2)}) collective-permute-start(bf16[4,128,256]{2,1,0:T(8,128)(2,1)S(1)} %add_convert_fusion.9), channel_id=1, source_target_pairs={{0,8},{4,12},{8,0},{12,4},{16,24},{20,28},{24,16},{28,20},{1,9},{5... | collective-permute-start | bytes 786440 | tf_op jit(solution)/shard_map/gqkvz0_d2/ppermute | solution.py:57
  217.4 17.9 %collective-permute-start.54 = (bf16[4,128,256]{2,1,0:T(8,128)(2,1)S(1)}, bf16[4,128,256]{2,1,0:T(8,128)(2,1)}, u32[]{:S(2)}, u32[]{:S(2)}) collective-permute-start(bf16[4,128,256]{2,1,0:T(8,128)(2,1)S(1)} %add_convert_fusion.7), channel_id=1, source_target_pairs={{0,16},{4,20},{8,24},{12,28},{16,0},{20,4},{24,8},{28,12},{1,17},{... | collective-permute-start | bytes 786440 | tf_op jit(solution)/shard_map/gqkv_d4/ppermute | solution.py:57
  220.8 15.4 %collective-permute-start.48 = (bf16[4,128,256]{2,1,0:T(8,128)(2,1)S(1)}, bf16[4,128,256]{2,1,0:T(8,128)(2,1)}, u32[]{:S(2)}, u32[]{:S(2)}) collective-permute-start(bf16[4,128,256]{2,1,0:T(8,128)(2,1)S(1)} %get-tuple-element.203), channel_id=1, source_target_pairs={{0,4},{4,0},{8,12},{12,8},{16,20},{20,16},{24,28},{28,24},{1,5},{5... | collective-permute-start | bytes 786440 | tf_op jit(solution)/shard_map/gqkv3_d1/ppermute | solution.py:57
  (100 other events, 960.3 us)
